TPU v7x, 512 devices: a whole 4x8x8 slice. The times are simulated.
512 devices in a mesh: seq: 32 (over z_lo, y), blk: 8 (over x, core), grp: 2 (over z_hi).
Axes of the slice: x: 4, y: 8, z: 8 (z_hi: 2, z_lo: 4; z = z_hi * 4 + z_lo), core: 2. Of those that a mesh axis runs over, the one named last changes fastest.
Arguments:
- activations: bfloat16 [32768, 8192], P('seq', 'blk'), may hold values from -23 to 23
- cotangent: bfloat16 [32768, 1024], P('seq'), may hold values from -0.0625 to 0.0625
- factor: float32 [8192, 1024], P('blk', ('seq', 'grp')), may hold values from -0.3 to 1.7
Outputs:
- new_factor: float32 [8192, 1024], P('blk', ('seq', 'grp'))
- direction: float32 [8192, 1024], P('blk', ('seq', 'grp'))
All inputs are finite; a program needn't handle non-finite values.
Results may differ from a plain program's by a relative error of at most 0.007.
Values may be sent and summed in bfloat16 or wider, within the bound.
No kernel may reach another device: no remote copies, remote signals or barrier semaphores. Data moves between devices by JAX's collectives and lax.ppermute only.
A program may use at most 64 MiB of HBM per device.

v0:
```python
import jax
import jax.numpy as jnp
from jax import lax
from jax.sharding import Mesh
from jax.sharding import PartitionSpec as P

SEQ = ("seq_0", "seq_1")
SEQ_GRP = ("seq_0", "seq_1", "grp")


damping = 0.25
step_size = 0.4


def laid_out(blocks, dim):
    blocks = jnp.moveaxis(blocks, 0, dim)
    lengths = blocks.shape
    return blocks.reshape(*lengths[:dim], lengths[dim] * lengths[dim + 1], *lengths[dim + 2 :])


def stacked_from(array, axes, sequence):
    blocks = array
    for k in sequence:
        blocks = lax.all_gather(blocks, axes[k])
    done = sequence[::-1]
    back = [done.index(k) for k in range(len(axes))]
    blocks = blocks.transpose(*back, *range(len(axes), blocks.ndim))
    return blocks.reshape(-1, *array.shape)


def gather_axes(array, axes, sequence, dim):
    return laid_out(stacked_from(array, axes, sequence), dim)


def in_blocks(array, dim, count):
    lengths = array.shape
    blocks = array.reshape(*lengths[:dim], count, lengths[dim] // count, *lengths[dim + 1 :])
    return jnp.moveaxis(blocks, dim, 0)


def sent_and_summed(array, axis, dim):
    blocks = in_blocks(array, dim, lax.axis_size(axis))
    arrived = lax.all_to_all(blocks, axis, split_axis=0, concat_axis=0, tiled=True)
    return arrived.sum(axis=0)


def strided_columns(matrix, seq_count, grp_count, grp_index):
    height = matrix.shape[0]
    narrow = matrix.shape[1] // (seq_count * grp_count)
    shaped = matrix.reshape(height, seq_count, grp_count, narrow)
    picked = lax.dynamic_slice_in_dim(shaped, grp_index, 1, 2)
    return picked.reshape(height, seq_count * narrow)


def on_device(activations, cotangent, factor):
    seq_count = lax.axis_size(SEQ)
    grp_count = lax.axis_size("grp")
    seq_index = lax.axis_index(SEQ)
    grp_index = lax.axis_index("grp")
    width = factor.shape[0]
    owned = factor.shape[1]
    total_tokens = activations.shape[0] * seq_count
    tokens_first = (((0,), (0,)), ((), ()))
    factor_low = factor.astype(jnp.bfloat16)
    whole_factor = gather_axes(factor_low, SEQ_GRP, (2, 0, 1), 1)
    whitened = jnp.dot(activations, whole_factor, preferred_element_type=jnp.float32).astype(
        jnp.bfloat16
    )
    chosen = strided_columns(whitened, seq_count, grp_count, grp_index)
    out_columns = strided_columns(cotangent, seq_count, grp_count, grp_index)
    piece = out_columns
    gradient_rows = sent_and_summed(
        lax.dot_general(piece, activations, tokens_first, preferred_element_type=jnp.float32),
        SEQ,
        0,
    ).astype(jnp.bfloat16)
    piece = chosen
    gram_rows = sent_and_summed(
        lax.dot_general(piece, whitened, tokens_first, preferred_element_type=jnp.float32), SEQ, 0
    )
    cross_rows = lax.dot_general(
        factor_low, whole_factor, tokens_first, preferred_element_type=jnp.float32
    )
    position = seq_index * grp_count + grp_index
    column_ids = position * owned + jnp.arange(owned, dtype=jnp.int32)
    identity_rows = (jnp.arange(width, dtype=jnp.int32)[None, :] == column_ids[:, None]).astype(
        jnp.float32
    )
    curvature = (gram_rows / total_tokens + damping * cross_rows - identity_rows).astype(
        jnp.bfloat16
    )
    update = lax.dot_general(
        whole_factor, curvature, (((1,), (1,)), ((), ())), preferred_element_type=jnp.float32
    )
    new_factor = factor - 0.5 * step_size * update
    half = lax.dot_general(
        whole_factor, gradient_rows, (((0,), (1,)), ((), ())), preferred_element_type=jnp.float32
    ).astype(jnp.bfloat16)
    direction = jnp.dot(whole_factor, half, preferred_element_type=jnp.float32)
    return (new_factor, direction)


def solution(mesh):
    torus = Mesh(
        mesh.devices.reshape(4, 8, mesh.shape["blk"], mesh.shape["grp"]),
        ("seq_0", "seq_1", "blk", "grp"),
    )
    return jax.shard_map(
        on_device,
        mesh=torus,
        in_specs=(P(SEQ, "blk"), P(SEQ, None), P("blk", SEQ_GRP)),
        out_specs=(P("blk", SEQ_GRP), P("blk", SEQ_GRP)),
        check_vma=False,
    )
```

profile of v0, /device:TPU:6, one launch (start us, length us, event | category | flops | bytes accessed | tf_op | source)
XLA Modules:
  0.0 195.8 jit_solution(5180129152464739098)
XLA Ops:
  7.2 0.0 copy-start
  7.2 0.0 all-gather.5.cloned.1.call-start
  7.2 1.0 convert_element_type.19
  8.2 11.6 %all-gather = bf16[2048,16]{0,1:T(8,128)(2,1)S(1)} all-gather(bf16[1024,16]{0,1:T(8,128)(2,1)S(1)} %convert_element_type.19), channel_id=2, replica_groups=mesh['seq_0'=4,'seq_1'=8,'blk'=8,'grp'=2] {'grp'}, dimensions={0}, use_global_device_ids=true | all-gather | bytes 98304 | tf_op jit(solution)/shard_map/all_gather | solution.py:24
  19.8 15.0 %all-gather.1 = bf16[8,1024,16]{1,2,0:T(8,128)(2,1)} all-gather(bf16[2,1024,16]{1,2,0:T(8,128)(2,1)S(1)} %bitcast.54), channel_id=3, replica_groups=mesh['seq_0'=4,'seq_1'=8,'blk'=8,'grp'=2] {'seq_0'}, dimensions={0}, use_global_device_ids=true | all-gather | bytes 327680 | tf_op jit(solution)/shard_map/all_gather | solution.py:24
  34.8 0.0 all-gather.5.cloned.1.call-update
  34.9 3.9 %copy.16 = bf16[1024,1024]{0,1:T(8,128)(2,1)} copy(bf16[1024,1024]{1,0:T(8,128)(2,1)} %param.4) | data formatting | bytes 4194304 | tf_op args[1]
  38.8 0.0 copy-done
  38.8 3.8 %fusion = f32[32,16,1024]{2,1,0:T(8,128)} fusion(bf16[1024,1024]{1,0:T(8,128)(2,1)S(1)} %copy-done, bf16[1024,32,2,16]{0,3,2,1:T(8,128)(2,1)} %bitcast.52, s32[]{:T(128)S(6)} %select_n.4), kind=kOutput, calls=%fused_computation | convolution fusion | flops 1073741824 | bytes 5242884 | tf_op jit(solution)/shard_map/dot_general | solution.py:73
  42.6 10.5 %all-to-all-start.1 = ((f32[32,16,1024]{2,1,0:T(8,128)}), f32[32,16,1024]{2,1,0:T(8,128)}, u32[]{:S(2)}, u32[]{:S(2)}) async-start(f32[32,16,1024]{2,1,0:T(8,128)} %fusion), calls=%async_computation.1 | async-start | bytes 4194304 | tf_op jit(solution)/shard_map/all_to_all | solution.py:43
  53.1 63.5 %all-gather.5.cloned.1.call-done = bf16[32,2,1024,16]{2,3,1,0:T(8,128)(2,1)} async-done(((bf16[4,2,1024,16]{2,3,1,0:T(8,128)(2,1)}), bf16[32,2,1024,16]{2,3,1,0:T(8,128)(2,1)}) %all-gather.5.cloned.1.call-update) | async-done | bytes 2097168 | tf_op jit(solution)/shard_map/all_gather | solution.py:24
  116.7 1.8 copy.14
  118.4 0.0 copy-start.1
  118.4 2.4 %convolution_convert_fusion = bf16[1024,1024]{0,1:T(8,128)(2,1)S(1)} fusion(bf16[1024,1024]{1,0:T(8,128)(2,1)S(1)} %copy-done, bf16[1024,1024]{0,1:T(8,128)(2,1)S(1)} %bitcast.48), kind=kOutput, calls=%fused_computation.4 | convolution fusion | flops 2148532224 | bytes 6291456 | tf_op jit(solution)/shard_map/dot_general | solution.py:66
  120.8 0.0 copy-done.1
  120.8 2.6 %fusion.2 = f32[32,16,1024]{2,1,0:T(8,128)} fusion(bf16[1024,1024]{0,1:T(8,128)(2,1)S(1)} %convolution_convert_fusion, bf16[1024,32,2,16]{0,3,2,1:T(8,128)(2,1)S(1)} %bitcast.56, s32[]{:T(128)S(6)} %select_n.4), kind=kOutput, calls=%fused_computation.2 | convolution fusion | flops 1073741824 | bytes 5242884 | tf_op jit(solution)/shard_map/dot_general | solution.py:79
  123.5 0.0 all-to-all-done.1
  123.5 8.3 %all-to-all-start = ((f32[32,16,1024]{2,1,0:T(8,128)}), f32[32,16,1024]{2,1,0:T(8,128)}, u32[]{:S(2)}, u32[]{:S(2)}) async-start(f32[32,16,1024]{2,1,0:T(8,128)} %fusion.2), calls=%async_computation | async-start | bytes 4194304 | tf_op jit(solution)/shard_map/all_to_all | solution.py:43
  131.8 1.7 reduce_sum.19
  133.5 3.8 %convolution_bitcast_fusion = f32[1024,16]{0,1:T(8,128)} fusion(bf16[1024,1024]{0,1:T(8,128)(2,1)} %bitcast.49, bf16[16,1024]{1,0:T(8,128)(2,1)S(1)} %reduce_sum.19), kind=kOutput, calls=%fused_computation.5 | convolution fusion | flops 67125248 | bytes 2195456 | tf_op jit(solution)/shard_map/dot_general | solution.py:99
  137.3 0.0 copy-start.2
  137.3 46.2 %all-to-all-done = f32[32,16,1024]{2,1,0:T(8,128)} async-done(((f32[32,16,1024]{2,1,0:T(8,128)}), f32[32,16,1024]{2,1,0:T(8,128)}, u32[]{:S(2)}, u32[]{:S(2)}) %all-to-all-start) | async-done | bytes 2097184 | tf_op jit(solution)/shard_map/all_to_all | solution.py:43
  183.4 1.7 reduce_sum.18
  185.1 0.0 copy-done.2
  185.2 3.8 %fusion.5 = f32[1024,16]{0,1:T(8,128)} fusion(f32[1024,16]{0,1:T(8,128)S(1)} %copy-done.2, bf16[1024,1024]{0,1:T(8,128)(2,1)} %bitcast.50, f32[16,1024]{1,0:T(8,128)S(1)} %reduce_sum.18, s32[16]{0:T(128)S(1)} %iota_add_fusion), kind=kOutput, calls=%fused_computation.8 | convolution fusion | flops 67272704 | bytes 2293824 | tf_op jit(solution)/shard_map/dot_general | solution.py:92
  (2 shorter events, 0.0 us)
Async XLA Ops:
  7.2 31.6 %copy-start = (bf16[1024,1024]{1,0:T(8,128)(2,1)S(1)}, bf16[1024,1024]{1,0:T(8,128)(2,1)}, u32[]{:S(2)}) copy-start(bf16[1024,1024]{1,0:T(8,128)(2,1)} %param.3) | copy-start | bytes 6291460
  7.2 109.5 %all-gather.5.cloned.1.call-start = ((), (), s32[]{:S(2)}) async-start(), calls=%async_computation.2 | async-start | bytes 2359296 | tf_op jit(solution)/shard_map/all_gather | solution.py:24
  42.6 80.9 %all-to-all-start.1 = ((f32[32,16,1024]{2,1,0:T(8,128)}), f32[32,16,1024]{2,1,0:T(8,128)}, u32[]{:S(2)}, u32[]{:S(2)}) async-start(f32[32,16,1024]{2,1,0:T(8,128)} %fusion), calls=%async_computation.1 | async-start | bytes 4194304 | tf_op jit(solution)/shard_map/all_to_all | solution.py:43
  118.4 2.4 %copy-start.1 = (bf16[4,8,2,1024,16]{3,4,2,1,0:T(8,128)(2,1)}, bf16[4,8,2,1024,16]{3,4,2,1,0:T(8,128)(2,1)S(1)}, u32[]{:S(2)}) copy-start(bf16[4,8,2,1024,16]{3,4,2,1,0:T(8,128)(2,1)S(1)} %copy.14) | copy-start | bytes 6291460
  123.5 60.0 %all-to-all-start = ((f32[32,16,1024]{2,1,0:T(8,128)}), f32[32,16,1024]{2,1,0:T(8,128)}, u32[]{:S(2)}, u32[]{:S(2)}) async-start(f32[32,16,1024]{2,1,0:T(8,128)} %fusion.2), calls=%async_computation | async-start | bytes 4194304 | tf_op jit(solution)/shard_map/all_to_all | solution.py:43
  137.3 47.9 %copy-start.2 = (f32[1024,16]{0,1:T(8,128)S(1)}, f32[1024,16]{0,1:T(8,128)}, u32[]{:S(2)}) copy-start(f32[1024,16]{0,1:T(8,128)} %param.5) | copy-start | bytes 196612
Sparse Core Ops, SparseCore 0:
  35.0 81.6 all-gather.4
where the time goes:
time: 196 us
  waiting for transfers between devices  110 us (56%)
  blocking collectives  26.6 us (14%)
  starting transfers between devices  18.8 us (10%)
  matrix products  16.4 us (8%)
  between operations  14.1 us (7%)
  local copies, waits for them, and re-layouts  5.72 us (3%)
  other arithmetic  4.4 us (2%)
    all_gather x1, waiting for transfers between devices, stacked_from(): blocks = lax.all_gather(blocks, axes[k])  63.5 us
    all_to_all x2, waiting for transfers between devices, sent_and_summed(): lax.all_to_all(blocks, axis, split_axis=0, concat_axis=0, tiled=True)  46.2 us
    all_gather x2, blocking collectives, stacked_from(): blocks = lax.all_gather(blocks, axes[k])  26.6 us
    all_to_all x2, starting transfers between devices, sent_and_summed(): lax.all_to_all(blocks, axis, split_axis=0, concat_axis=0, tiled=True)  18.8 us
    unnamed x7, local copies, waits for them, and re-layouts  3.95 us
  transfers between devices with their start and end apart: 3, of which 2 were waited for; matrix products, arithmetic and copies ran while one was open for 10% of the time, Pallas kernels for 0%

commit v1 on v0

v1 whole, which is shorter than its diff:
```python
import jax
import jax.numpy as jnp
from jax import lax
from jax.sharding import Mesh
from jax.sharding import PartitionSpec as P

SEQ = ("seq_0", "seq_1")
SEQ_GRP = ("seq_0", "seq_1", "grp")


damping = 0.25
step_size = 0.4


def class_groups(seq_count):
    return [[q * 2 + (h ^ (q & 1)) for q in range(seq_count)] for h in range(2)]


def exchange(blocks, groups):
    return lax.all_to_all(
        blocks, SEQ_GRP, split_axis=0, concat_axis=0, tiled=True, axis_index_groups=groups
    )


def class_rows(matrix, seq_count, owned, chosen):
    shaped = matrix.reshape(seq_count // 2, 2, 2, owned, matrix.shape[1])
    even = lax.dynamic_index_in_dim(shaped[:, 0], chosen, 1)
    odd = lax.dynamic_index_in_dim(shaped[:, 1], 1 - chosen, 1)
    return jnp.concatenate([even, odd], axis=1).reshape(seq_count, owned, matrix.shape[1])


def on_device(activations, cotangent, factor):
    f32, bf16 = jnp.float32, jnp.bfloat16
    seq_count = lax.axis_size(SEQ)
    y_count = lax.axis_size("seq_1")
    seq_index = lax.axis_index(SEQ)
    chosen = lax.axis_index("grp") ^ (seq_index & 1)
    owned = factor.shape[1]
    width = factor.shape[0]
    half_width = width // 2
    total_tokens = activations.shape[0] * seq_count
    groups = class_groups(seq_count)
    tokens_first = (((0,), (0,)), ((), ()))
    rows_rows = (((1,), (1,)), ((), ()))

    own = factor.T
    own_low = own.astype(bf16)
    near = exchange(jnp.broadcast_to(own_low[None], (seq_count, owned, width)), groups)
    near = near.reshape(half_width, width)

    gradient_part = lax.dot_general(
        cotangent, activations, tokens_first, preferred_element_type=f32
    ).astype(bf16)
    gradient_blocks = exchange(class_rows(gradient_part, seq_count, owned, chosen), groups)

    far = lax.ppermute(near, "seq_1", [(y, y ^ 1) for y in range(y_count)])

    whitened = lax.dot_general(near, activations, rows_rows, preferred_element_type=f32).astype(bf16)
    moment = jnp.dot(whitened, activations, preferred_element_type=f32).astype(bf16)
    moment_blocks = exchange(moment.reshape(seq_count, owned, width), groups)

    gradient = gradient_blocks.astype(f32).sum(axis=0).astype(bf16)
    half_near = lax.dot_general(gradient, near, rows_rows, preferred_element_type=f32).astype(bf16)
    half_far = lax.dot_general(gradient, far, rows_rows, preferred_element_type=f32).astype(bf16)
    direction = jnp.dot(half_near, near, preferred_element_type=f32) + jnp.dot(
        half_far, far, preferred_element_type=f32
    )

    inner = (
        moment_blocks.astype(f32).sum(axis=0) / total_tokens + damping * own_low.astype(f32)
    ).astype(bf16)
    identity = (
        jnp.arange(half_width, dtype=jnp.int32)[None, :]
        == (seq_index * owned + jnp.arange(owned, dtype=jnp.int32))[:, None]
    ).astype(f32)
    curve_near = (
        lax.dot_general(inner, near, rows_rows, preferred_element_type=f32) - identity
    ).astype(bf16)
    curve_far = lax.dot_general(inner, far, rows_rows, preferred_element_type=f32).astype(bf16)
    update = jnp.dot(curve_near, near, preferred_element_type=f32) + jnp.dot(
        curve_far, far, preferred_element_type=f32
    )
    new_factor = own - 0.5 * step_size * update
    return (new_factor.T, direction.T)


def solution(mesh):
    torus = Mesh(
        mesh.devices.reshape(4, 8, mesh.shape["blk"], mesh.shape["grp"]),
        ("seq_0", "seq_1", "blk", "grp"),
    )
    return jax.shard_map(
        on_device,
        mesh=torus,
        in_specs=(P(SEQ, "blk"), P(SEQ, None), P("blk", SEQ_GRP)),
        out_specs=(P("blk", SEQ_GRP), P("blk", SEQ_GRP)),
        check_vma=False,
    )
```

time: 196 us -> 150 us (0.77)
  blocking collectives: 26.6 us -> 0 us
  waiting for transfers between devices: 110 us -> 90.3 us
  starting transfers between devices: 18.8 us -> 36.8 us
  between operations: 14.1 us -> 0.74 us
  local copies, waits for them, and re-layouts: 5.72 us -> 1.49 us
  matrix products: 16.4 us -> 14.1 us
    all_gather x1 -> x0, waiting for transfers between devices: 63.5 us -> none  [stacked_from(): blocks = lax.all_gather(blocks, axes[k])]
    ppermute x0 -> x1, waiting for transfers between devices: none -> 39.4 us  [on_device(): far = lax.ppermute(near, 'seq_1', [(y, y ^ 1) for y in range(y_count)])]
    all_gather x2 -> x0, blocking collectives: 26.6 us -> none  [stacked_from(): blocks = lax.all_gather(blocks, axes[k])]
    all_to_all x2 -> x3, starting transfers between devices: 18.8 us -> 31.4 us  [exchange(): lax.all_to_all(blocks, SEQ_GRP, split_axis=0, concat_axis=0, tiled=True,...]
    ppermute x0 -> x1, starting transfers between devices: none -> 5.39 us  [on_device(): far = lax.ppermute(near, 'seq_1', [(y, y ^ 1) for y in range(y_count)])]
    all_to_all x2 -> x3, waiting for transfers between devices: 46.2 us -> 50.9 us  [exchange(): lax.all_to_all(blocks, SEQ_GRP, split_axis=0, concat_axis=0, tiled=True,...]
    unnamed x7 -> x4, local copies, waits for them, and re-layouts: 3.95 us -> 0.01 us
    dot_general x5 -> x6, matrix products: 16.4 us -> 14.1 us  [the longest x1 3.98 us: on_device(): lax.dot_general(cotangent, activations, tokens_first, preferred_element_t...]
  transfers between devices with their start and end apart: 3 -> 4, of which waited for: 2 -> 3; matrix products, arithmetic and copies ran while one was open for 10% -> 9% of each run, Pallas kernels for 0% -> 0%
where the time goes in v1:
time: 150 us; the launch traced here: 148 us
  waiting for transfers between devices  90.3 us (60%)
  starting transfers between devices  36.8 us (25%)
  matrix products  14.1 us (9%)
  other arithmetic  4.86 us (3%)
    all_to_all x3, waiting for transfers between devices, exchange(): lax.all_to_all(blocks, SEQ_GRP, split_axis=0, concat_axis=0, tiled=True,...  50.9 us
    ppermute x1, waiting for transfers between devices, on_device(): far = lax.ppermute(near, 'seq_1', [(y, y ^ 1) for y in range(y_count)])  39.4 us
    all_to_all x3, starting transfers between devices, exchange(): lax.all_to_all(blocks, SEQ_GRP, split_axis=0, concat_axis=0, tiled=True,...  31.4 us
    ppermute x1, starting transfers between devices, on_device(): far = lax.ppermute(near, 'seq_1', [(y, y ^ 1) for y in range(y_count)])  5.39 us
    dot_general x1, matrix products, on_device(): lax.dot_general(cotangent, activations, tokens_first, preferred_element_t...  3.98 us
    dot_general x1, matrix products, on_device(): jnp.dot(whitened, activations, preferred_element_type=f32).astype(bf16)  3.4 us
  transfers between devices with their start and end apart: 4, of which 3 were waited for; matrix products, arithmetic and copies ran while one was open for 9% of the time, Pallas kernels for 0%

profile of v1, /device:TPU:6, one launch (start us, length us, event | category | flops | bytes accessed | tf_op | source)
XLA Modules:
  0.0 148.3 jit_solution(5481812859383862377)
XLA Ops:
  0.6 0.0 copy-start
  0.6 1.0 convert_bitcast_fusion
  1.6 1.1 broadcast_in_dim.2
  2.7 15.2 %all-to-all-start = ((bf16[32,16,1024]{2,1,0:T(8,128)(2,1)}), bf16[32,16,1024]{2,1,0:T(8,128)(2,1)S(1)}, u32[]{:S(2)}, u32[]{:S(2)}) async-start(bf16[32,16,1024]{2,1,0:T(8,128)(2,1)} %broadcast_in_dim.2), calls=%async_computation | async-start | bytes 2097152 | tf_op jit(solution)/shard_map/all_to_all | solution.py:20
  17.9 0.0 copy-done
  18.0 4.0 %convolution_convert_fusion = bf16[1024,1024]{1,0:T(8,128)(2,1)S(1)} fusion(bf16[1024,1024]{1,0:T(8,128)(2,1)} %param.4, bf16[1024,1024]{1,0:T(8,128)(2,1)S(1)} %copy-done), kind=kOutput, calls=%fused_computation.1 | convolution fusion | flops 2148532224 | bytes 6291456 | tf_op jit(solution)/shard_map/dot_general | solution.py:51
  21.9 0.3 fusion.13
  22.3 0.1 dynamic-slice_bitcast_fusion
  22.3 1.1 pad_maximum_fusion
  23.4 25.1 %all-to-all-done = bf16[32,16,1024]{2,1,0:T(8,128)(2,1)S(1)} async-done(((bf16[32,16,1024]{2,1,0:T(8,128)(2,1)}), bf16[32,16,1024]{2,1,0:T(8,128)(2,1)S(1)}, u32[]{:S(2)}, u32[]{:S(2)}) %all-to-all-start) | async-done | bytes 1048608 | tf_op jit(solution)/shard_map/all_to_all | solution.py:20
  48.5 8.0 %all-to-all-start.2 = ((bf16[32,16,1024]{2,1,0:T(8,128)(2,1)}), bf16[32,16,1024]{2,1,0:T(8,128)(2,1)}, u32[]{:S(2)}, u32[]{:S(2)}) async-start(bf16[32,16,1024]{2,1,0:T(8,128)(2,1)} %bitcast.43), calls=%async_computation.2 | async-start | bytes 2097152 | tf_op jit(solution)/shard_map/all_to_all | solution.py:20
  56.5 3.4 %convolution_convert_fusion.1 = bf16[512,1024]{1,0:T(8,128)(2,1)} fusion(bf16[1024,1024]{1,0:T(8,128)(2,1)S(1)} %copy-done, bf16[512,1024]{1,0:T(8,128)(2,1)S(1)} %bitcast.39), kind=kOutput, calls=%fused_computation.2 | convolution fusion | flops 2148532224 | bytes 4194304 | tf_op jit(solution)/shard_map/dot_general | solution.py:59
  59.9 25.8 %all-to-all-done.2 = bf16[32,16,1024]{2,1,0:T(8,128)(2,1)} async-done(((bf16[32,16,1024]{2,1,0:T(8,128)(2,1)}), bf16[32,16,1024]{2,1,0:T(8,128)(2,1)}, u32[]{:S(2)}, u32[]{:S(2)}) %all-to-all-start.2) | async-done | bytes 1048608 | tf_op jit(solution)/shard_map/all_to_all | solution.py:20
  85.6 8.3 %all-to-all-start.1 = ((bf16[32,16,1024]{2,1,0:T(8,128)(2,1)}), bf16[32,16,1024]{2,1,0:T(8,128)(2,1)}, u32[]{:S(2)}, u32[]{:S(2)}) async-start(bf16[32,16,1024]{2,1,0:T(8,128)(2,1)} %bitcast.45), calls=%async_computation.1 | async-start | bytes 2097152 | tf_op jit(solution)/shard_map/all_to_all | solution.py:20
  93.9 5.4 %collective-permute-start = (bf16[512,1024]{1,0:T(8,128)(2,1)S(1)}, bf16[512,1024]{1,0:T(8,128)(2,1)}, u32[]{:S(2)}, u32[]{:S(2)}) collective-permute-start(bf16[512,1024]{1,0:T(8,128)(2,1)S(1)} %bitcast.40), channel_id=1, source_target_pairs={{0,16},{16,0},{32,48},{48,32},{64,80},{80,64},{96,112},{112,96},{1... | collective-permute-start | bytes 3145736 | tf_op jit(solution)/shard_map/ppermute | solution.py:56
  99.4 1.4 reduce_sum.22
  100.7 0.6 fusion.5
  101.3 0.0 copy-start.1
  101.3 39.4 %collective-permute-done = bf16[512,1024]{1,0:T(8,128)(2,1)} collective-permute-done((bf16[512,1024]{1,0:T(8,128)(2,1)S(1)}, bf16[512,1024]{1,0:T(8,128)(2,1)}, u32[]{:S(2)}, u32[]{:S(2)}) %collective-permute-start) | collective-permute-done | bytes 1048608 | tf_op jit(solution)/shard_map/ppermute | solution.py:56
  140.8 2.8 %fusion = f32[1024,16]{0,1:T(8,128)} fusion(f32[16,1024]{1,0:T(8,128)S(1)} %fusion.5, bf16[512,1024]{1,0:T(8,128)(2,1)} %collective-permute-done, bf16[16,1024]{1,0:T(8,128)(2,1)S(1)} %reduce_sum.22), kind=kOutput, calls=%fused_computation.5 | convolution fusion | flops 33579008 | bytes 1212416 | tf_op jit(solution)/shard_map/dot_general | solution.py:65
  143.5 0.0 all-to-all-done.1
  143.5 1.4 convert_reduce_fusion
  144.9 0.0 copy-done.1
  144.9 0.6 fusion.6
  145.5 2.8 %fusion.3 = f32[1024,16]{0,1:T(8,128)} fusion(f32[1024,16]{0,1:T(8,128)S(1)} %copy-done.1, f32[16,1024]{1,0:T(8,128)S(1)} %fusion.6, bf16[512,1024]{1,0:T(8,128)(2,1)} %collective-permute-done, f32[16,1024]{1,0:T(8,128)S(1)} %convert_reduce_fusion), kind=kOutput, calls=%fused_computation.9 | convolution fusion | flops 33710080 | bytes 1310720 | tf_op jit(solution)/shard_map/dot_general | solution.py:80
  (1 shorter events, 0.0 us)
Async XLA Ops:
  0.6 17.3 %copy-start = (bf16[1024,1024]{1,0:T(8,128)(2,1)S(1)}, bf16[1024,1024]{1,0:T(8,128)(2,1)}, u32[]{:S(2)}) copy-start(bf16[1024,1024]{1,0:T(8,128)(2,1)} %param.3) | copy-start | bytes 6291460
  2.7 45.8 %all-to-all-start = ((bf16[32,16,1024]{2,1,0:T(8,128)(2,1)}), bf16[32,16,1024]{2,1,0:T(8,128)(2,1)S(1)}, u32[]{:S(2)}, u32[]{:S(2)}) async-start(bf16[32,16,1024]{2,1,0:T(8,128)(2,1)} %broadcast_in_dim.2), calls=%async_computation | async-start | bytes 2097152 | tf_op jit(solution)/shard_map/all_to_all | solution.py:20
  48.5 37.1 %all-to-all-start.2 = ((bf16[32,16,1024]{2,1,0:T(8,128)(2,1)}), bf16[32,16,1024]{2,1,0:T(8,128)(2,1)}, u32[]{:S(2)}, u32[]{:S(2)}) async-start(bf16[32,16,1024]{2,1,0:T(8,128)(2,1)} %bitcast.43), calls=%async_computation.2 | async-start | bytes 2097152 | tf_op jit(solution)/shard_map/all_to_all | solution.py:20
  85.6 57.9 %all-to-all-start.1 = ((bf16[32,16,1024]{2,1,0:T(8,128)(2,1)}), bf16[32,16,1024]{2,1,0:T(8,128)(2,1)}, u32[]{:S(2)}, u32[]{:S(2)}) async-start(bf16[32,16,1024]{2,1,0:T(8,128)(2,1)} %bitcast.45), calls=%async_computation.1 | async-start | bytes 2097152 | tf_op jit(solution)/shard_map/all_to_all | solution.py:20
  93.9 46.8 %collective-permute-start = (bf16[512,1024]{1,0:T(8,128)(2,1)S(1)}, bf16[512,1024]{1,0:T(8,128)(2,1)}, u32[]{:S(2)}, u32[]{:S(2)}) collective-permute-start(bf16[512,1024]{1,0:T(8,128)(2,1)S(1)} %bitcast.40), channel_id=1, source_target_pairs={{0,16},{16,0},{32,48},{48,32},{64,80},{80,64},{96,112},{112,96},{1... | collective-permute-start | bytes 3145736 | tf_op jit(solution)/shard_map/ppermute | solution.py:56
  101.3 43.6 %copy-start.1 = (f32[1024,16]{0,1:T(8,128)S(1)}, f32[1024,16]{0,1:T(8,128)}, u32[]{:S(2)}) copy-start(f32[1024,16]{0,1:T(8,128)} %param.5) | copy-start | bytes 196612

commit v2 on v1

v2 whole, which is shorter than its diff:
```python
import functools

import jax
import jax.numpy as jnp
from jax import lax
from jax.experimental import pallas as pl
from jax.experimental.pallas import tpu as pltpu
from jax.sharding import Mesh
from jax.sharding import PartitionSpec as P

SEQ = ("seq_0", "seq_1")
SEQ_GRP = ("seq_0", "seq_1", "grp")


damping = 0.25
step_size = 0.4

f32, bf16 = jnp.float32, jnp.bfloat16
VMEM_LIMIT = 16 * 1024 * 1024
ROWS_ROWS = (((1,), (1,)), ((), ()))
TOKENS_FIRST = (((0,), (0,)), ((), ()))


def member(z_low, y, grp):
    return (z_low * 8 + y) * 2 + grp


def of_class(h, yh, zh, a, b):
    return member(2 * zh + b, 2 * yh + a, h ^ (yh & 1))


SQUARES = [
    [of_class(h, yh, zh, a, b) for a in range(2) for b in range(2)]
    for h in range(2)
    for yh in range(4)
    for zh in range(2)
]
FAR_GROUPS = [
    [of_class(h, yh, zh, a, b) for yh in range(4) for zh in range(2)]
    for h in range(2)
    for a in range(2)
    for b in range(2)
]
ACROSS = [(y, (y + 1) % 8 if y % 2 else (y - 1) % 8) for y in range(8)]
ALL_MEMBERS = [(z, y, g) for z in range(4) for y in range(8) for g in range(2)]
TURNED = {
    d: [(member(z, y, g), member(z ^ (d & 1), y ^ (d >> 1), g)) for z, y, g in ALL_MEMBERS]
    for d in (1, 2, 3)
}


def exchange(blocks, groups):
    return lax.all_to_all(
        blocks, SEQ_GRP, split_axis=0, concat_axis=0, tiled=True, axis_index_groups=groups
    )


def vmem():
    return pl.BlockSpec(memory_space=pltpu.VMEM)


def position():
    z_low, y, grp = lax.axis_index("seq_0"), lax.axis_index("seq_1"), lax.axis_index("grp")
    yh = y // 2
    return y % 2, z_low % 2, yh, z_low // 2, (grp + yh) % 2


def pick_kernel(rows_ref, *out_refs):
    a, b, _, _, h = position()
    for d, out_ref in enumerate(out_refs):
        a_there = 1 - a if d & 2 else a
        b_there = 1 - b if d & 1 else b
        for f in range(8):
            row, column = f >> 1, f & 1
            grp = 1 - h if row & 1 else h
            out_ref[f] = rows_ref[member(2 * column + b_there, 2 * row + a_there, grp)]


def pick(rows):
    shape = jax.ShapeDtypeStruct((8,) + rows.shape[1:], rows.dtype)
    return pl.pallas_call(
        pick_kernel,
        out_shape=[shape] * 4,
        in_specs=[vmem()],
        out_specs=[vmem()] * 4,
        compiler_params=pltpu.CompilerParams(vmem_limit_bytes=VMEM_LIMIT),
        name="pick",
    )(rows)


def join_kernel(moment_ref, own_ref, *refs):
    others, out_ref = refs[:3], refs[3]
    for f in range(8):
        total = moment_ref[0, f].astype(f32)
        for k in range(1, 4):
            total = total + moment_ref[k, f].astype(f32)
        out_ref[f, :16] = total.astype(bf16)
        total = own_ref[f].astype(f32)
        for other in others:
            total = total + other[f].astype(f32)
        out_ref[f, 16:] = total.astype(bf16)


def join(moment, own, others):
    return pl.pallas_call(
        join_kernel,
        out_shape=jax.ShapeDtypeStruct((8, 32, own.shape[2]), bf16),
        in_specs=[vmem()] * 5,
        out_specs=vmem(),
        compiler_params=pltpu.CompilerParams(vmem_limit_bytes=VMEM_LIMIT),
        name="join",
    )(moment, own, *others)


def finish_kernel(tokens, sums_ref, near_ref, far_ref, own_ref, new_ref, direction_ref):
    a, b, yh, zh, _ = position()
    at = ((2 * a + b) * 8 + 2 * yh + zh) * 16
    own = own_ref[...]
    total = sums_ref[0].astype(f32)
    for k in range(1, 8):
        total = total + sums_ref[k].astype(f32)
    inner = total[:16] / tokens + damping * own.astype(bf16).astype(f32)
    high = inner.astype(bf16)
    low = (inner - high.astype(f32)).astype(bf16)
    left = jnp.concatenate([high, low, total[16:].astype(bf16)], axis=0)
    result = jnp.zeros((32, own.shape[1]), f32)
    for k, ref in enumerate((near_ref, far_ref)):
        rows = ref[...]
        product = lax.dot_general(left, rows, ROWS_ROWS, preferred_element_type=f32)
        curve = product[:16] + product[16:32]
        if k == 0:
            column = lax.broadcasted_iota(jnp.int32, curve.shape, 1)
            row = lax.broadcasted_iota(jnp.int32, curve.shape, 0)
            curve = curve - (column == row + at).astype(f32)
        right = jnp.concatenate([curve.astype(bf16), product[32:].astype(bf16)], axis=0)
        result = result + jnp.dot(right, rows, preferred_element_type=f32)
    new_ref[...] = own - 0.5 * step_size * result[:16]
    direction_ref[...] = result[16:]


def finish(tokens, sums, near, far, own):
    return pl.pallas_call(
        functools.partial(finish_kernel, tokens),
        out_shape=[jax.ShapeDtypeStruct(own.shape, f32)] * 2,
        in_specs=[vmem()] * 4,
        out_specs=[vmem()] * 2,
        compiler_params=pltpu.CompilerParams(vmem_limit_bytes=VMEM_LIMIT),
        name="finish",
    )(sums, near, far, own)


def on_device(activations, cotangent, factor):
    seq_count = lax.axis_size(SEQ)
    owned = factor.shape[1]
    width = factor.shape[0]
    half_width = width // 2
    total_tokens = activations.shape[0] * seq_count

    own = factor.T
    own_low = own.astype(bf16)
    square = exchange(jnp.broadcast_to(own_low[None], (8, owned, width)), FAR_GROUPS)
    square = square.reshape(1, 8 * owned, width)
    near = exchange(jnp.broadcast_to(square, (4, 8 * owned, width)), SQUARES)
    near = near.reshape(half_width, width)

    gradient_part = lax.dot_general(
        cotangent, activations, TOKENS_FIRST, preferred_element_type=f32
    ).astype(bf16)
    parts = pick(gradient_part.reshape(2 * seq_count, owned, width))
    arrived = [lax.ppermute(parts[d], SEQ_GRP, TURNED[d]) for d in (1, 2, 3)]

    whitened = lax.dot_general(near, activations, ROWS_ROWS, preferred_element_type=f32).astype(bf16)
    moment = jnp.dot(whitened, activations, preferred_element_type=f32).astype(bf16)
    moment = exchange(moment.reshape(4, 8 * owned, width), SQUARES)
    far = lax.ppermute(near, "seq_1", ACROSS)
    sums = exchange(join(moment.reshape(4, 8, owned, width), parts[0], arrived), FAR_GROUPS)

    new_factor, direction = finish(total_tokens, sums, near, far, own)
    return (new_factor.T, direction.T)


def solution(mesh):
    torus = Mesh(
        mesh.devices.reshape(4, 8, mesh.shape["blk"], mesh.shape["grp"]),
        ("seq_0", "seq_1", "blk", "grp"),
    )
    return jax.shard_map(
        on_device,
        mesh=torus,
        in_specs=(P(SEQ, "blk"), P(SEQ, None), P("blk", SEQ_GRP)),
        out_specs=(P("blk", SEQ_GRP), P("blk", SEQ_GRP)),
        check_vma=False,
    )
```

time: 150 us -> 116 us (0.77)
  waiting for transfers between devices: 90.3 us -> 27 us
  blocking collectives: 0 us -> 45 us
  starting transfers between devices: 36.8 us -> 21.5 us
  local copies, waits for them, and re-layouts: 1.49 us -> 7.72 us
  matrix products: 14.1 us -> 8.55 us
  other arithmetic: 4.86 us -> 0.99 us
  Pallas kernels: 0 us -> 3.7 us
    all_to_all x0 -> x2, blocking collectives: none -> 45 us  [exchange(): lax.all_to_all(blocks, SEQ_GRP, split_axis=0, concat_axis=0, tiled=True,...]
    all_to_all x3 -> x2, waiting for transfers between devices: 50.9 us -> 10.9 us  [exchange(): lax.all_to_all(blocks, SEQ_GRP, split_axis=0, concat_axis=0, tiled=True,...]
    ppermute x1 -> x4, waiting for transfers between devices: 39.4 us -> 16.1 us  [the longest x1 10.3 us: on_device(): far = lax.ppermute(near, 'seq_1', ACROSS)]
    all_to_all x3 -> x2, starting transfers between devices: 31.4 us -> 8.51 us  [exchange(): lax.all_to_all(blocks, SEQ_GRP, split_axis=0, concat_axis=0, tiled=True,...]
    ppermute x1 -> x4, starting transfers between devices: 5.39 us -> 13 us  [the longest x3 9.21 us: on_device(): arrived = [lax.ppermute(parts[d], SEQ_GRP, TURNED[d]) for d in (1, 2, 3)]]
    unnamed x4 -> x22, local copies, waits for them, and re-layouts: 0.01 us -> 7.59 us
    dot_general x5 -> x1, matrix products: 10.7 us -> 3.98 us  [on_device(): lax.dot_general(cotangent, activations, TOKENS_FIRST, preferred_element_t...]
    pallas_call x0 -> x3, Pallas kernels: none -> 3.7 us  [the longest x1 3.35 us: finish(): pl.pallas_call(functools.partial(finish_kernel, tokens), out_shape=[jax.S...]
  transfers between devices with their start and end apart: 4 -> 6, of which waited for: 3 -> 4; matrix products, arithmetic and copies ran while one was open for 9% -> 3% of each run, Pallas kernels for 0% -> 0%
where the time goes in v2:
time: 116 us; the launch traced here: 115 us
  blocking collectives  45 us (39%)
  waiting for transfers between devices  27 us (23%)
  starting transfers between devices  21.5 us (19%)
  matrix products  8.55 us (7%)
  local copies, waits for them, and re-layouts  7.72 us (7%)
  Pallas kernels  3.7 us (3%)
    all_to_all x2, blocking collectives, exchange(): lax.all_to_all(blocks, SEQ_GRP, split_axis=0, concat_axis=0, tiled=True,...  45 us
    all_to_all x2, waiting for transfers between devices, exchange(): lax.all_to_all(blocks, SEQ_GRP, split_axis=0, concat_axis=0, tiled=True,...  10.9 us
    ppermute x1, waiting for transfers between devices, on_device(): far = lax.ppermute(near, 'seq_1', ACROSS)  10.3 us
    ppermute x3, starting transfers between devices, on_device(): arrived = [lax.ppermute(parts[d], SEQ_GRP, TURNED[d]) for d in (1, 2, 3)]  9.21 us
    all_to_all x2, starting transfers between devices, exchange(): lax.all_to_all(blocks, SEQ_GRP, split_axis=0, concat_axis=0, tiled=True,...  8.51 us
    unnamed x22, local copies, waits for them, and re-layouts  7.59 us
    ppermute x3, waiting for transfers between devices, on_device(): arrived = [lax.ppermute(parts[d], SEQ_GRP, TURNED[d]) for d in (1, 2, 3)]  5.81 us
    dot_general x1, matrix products, on_device(): jnp.dot(whitened, activations, preferred_element_type=f32).astype(bf16)  4.57 us
  transfers between devices with their start and end apart: 6, of which 4 were waited for; matrix products, arithmetic and copies ran while one was open for 3% of the time, Pallas kernels for 0%

profile of v2, /device:TPU:6, one launch (start us, length us, event | category | flops | bytes accessed | tf_op | source)
XLA Modules:
  0.0 115.2 jit_solution(15415466154470312178)
XLA Ops:
  0.6 0.0 copy-start
  0.6 1.0 bitcast_convert_fusion
  1.7 27.9 %all_to_all.20 = bf16[8,16,1024]{2,1,0:T(8,128)(2,1)S(1)} all-to-all(bf16[8,16,1024]{2,1,0:T(8,128)(2,1)S(1)} %broadcast_in_dim.6), channel_id=1, replica_groups={{0,256,33,289,64,320,97,353},{128,384,161,417,192,448,225,481},{16,272,..., dimensions={0} | all-to-all | bytes 524288 | tf_op jit(solution)/shard_map/all_to_all | solution.py:53
  29.6 0.1 broadcast_in_dim.15
  29.7 17.1 %all_to_all.21 = bf16[4,128,1024]{2,1,0:T(8,128)(2,1)} all-to-all(bf16[4,128,1024]{2,1,0:T(8,128)(2,1)S(1)} %broadcast_in_dim.15), channel_id=1, replica_groups={{0,128,16,144},{256,384,272,400},{33,161,49,177},{289,417,305,433},{64,..., dimensions={0} | all-to-all | bytes 2097152 | tf_op jit(solution)/shard_map/all_to_all | solution.py:53
  46.8 4.6 %convolution_convert_fusion.1 = bf16[512,1024]{1,0:T(8,128)(2,1)} fusion(bf16[1024,1024]{1,0:T(8,128)(2,1)S(1)} %copy-done, bf16[512,1024]{1,0:T(8,128)(2,1)} %bitcast.2.near_ref), kind=kOutput, calls=%fused_computation.1 | convolution fusion | flops 2148532224 | bytes 4194304 | tf_op jit(solution)/shard_map/dot_general | solution.py:173
  51.4 3.5 %all-to-all-start.2 = ((bf16[4,128,1024]{2,1,0:T(8,128)(2,1)}), bf16[4,128,1024]{2,1,0:T(8,128)(2,1)S(1)}, u32[]{:S(2)}, u32[]{:S(2)}) async-start(bf16[4,128,1024]{2,1,0:T(8,128)(2,1)} %bitcast.18), calls=%async_computation.2 | async-start | bytes 2097152 | tf_op jit(solution)/shard_map/all_to_all | solution.py:53
  54.9 4.0 %convolution_convert_fusion = bf16[1024,1024]{1,0:T(8,128)(2,1)S(1)} fusion(bf16[1024,1024]{1,0:T(8,128)(2,1)} %param.4, bf16[1024,1024]{1,0:T(8,128)(2,1)S(1)} %copy-done), kind=kOutput, calls=%fused_computation | convolution fusion | flops 2148532224 | bytes 6291456 | tf_op jit(solution)/shard_map/dot_general | solution.py:166
  58.9 0.0 copy-start.10
  58.9 0.1 pick.1
  59.0 3.9 %collective-permute-start = (bf16[8,16,1024]{2,1,0:T(8,128)(2,1)S(1)}, bf16[8,16,1024]{2,1,0:T(8,128)(2,1)S(1)}, u32[]{:S(2)}, u32[]{:S(2)}) collective-permute-start(bf16[8,16,1024]{2,1,0:T(8,128)(2,1)S(1)} %get-tuple-element.9), channel_id=1, source_target_pairs={{0,128},{1,129},{16,144},{17,145},{32,160},{33,161},{48,176},{49,1... | collective-permute-start | bytes 786440 | tf_op jit(solution)/shard_map/ppermute | solution.py:170
  62.9 3.4 %collective-permute-start.1 = (bf16[8,16,1024]{2,1,0:T(8,128)(2,1)S(1)}, bf16[8,16,1024]{2,1,0:T(8,128)(2,1)S(1)}, u32[]{:S(2)}, u32[]{:S(2)}) collective-permute-start(bf16[8,16,1024]{2,1,0:T(8,128)(2,1)S(1)} %get-tuple-element.10), channel_id=1, source_target_pairs={{0,16},{1,17},{16,0},{17,1},{32,48},{33,49},{48,32},{49,33},{64,80... | collective-permute-start | bytes 786440 | tf_op jit(solution)/shard_map/ppermute | solution.py:170
  66.3 1.9 %collective-permute-start.2 = (bf16[8,16,1024]{2,1,0:T(8,128)(2,1)S(1)}, bf16[8,16,1024]{2,1,0:T(8,128)(2,1)S(1)}, u32[]{:S(2)}, u32[]{:S(2)}) collective-permute-start(bf16[8,16,1024]{2,1,0:T(8,128)(2,1)S(1)} %get-tuple-element.11), channel_id=1, source_target_pairs={{0,144},{1,145},{16,128},{17,129},{32,176},{33,177},{48,160},{49,1... | collective-permute-start | bytes 786440 | tf_op jit(solution)/shard_map/ppermute | solution.py:170
  68.2 3.8 %collective-permute-start.3 = (bf16[512,1024]{1,0:T(8,128)(2,1)}, bf16[512,1024]{1,0:T(8,128)(2,1)}, u32[]{:S(2)}, u32[]{:S(2)}) collective-permute-start(bf16[512,1024]{1,0:T(8,128)(2,1)} %bitcast.2.near_ref), channel_id=1, source_target_pairs={{0,112},{16,32},{32,16},{48,64},{64,48},{80,96},{96,80},{112,0},{1... | collective-permute-start | bytes 3145736 | tf_op jit(solution)/shard_map/ppermute | solution.py:175
  72.0 2.5 %collective-permute-done.refs_0_ = bf16[8,16,1024]{2,1,0:T(8,128)(2,1)S(1)} collective-permute-done((bf16[8,16,1024]{2,1,0:T(8,128)(2,1)S(1)}, bf16[8,16,1024]{2,1,0:T(8,128)(2,1)S(1)}, u32[]{:S(2)}, u32[]{:S(2)}) %collective-permute-start) | collective-permute-done | bytes 262176 | tf_op jit(solution)/shard_map/ppermute | solution.py:170
  74.5 0.7 copy-done.4
  75.2 0.0 collective-permute-done.1.refs_1_
  75.2 0.7 copy-done.6
  75.9 3.3 %collective-permute-done.2.refs_2_ = bf16[8,16,1024]{2,1,0:T(8,128)(2,1)S(1)} collective-permute-done((bf16[8,16,1024]{2,1,0:T(8,128)(2,1)S(1)}, bf16[8,16,1024]{2,1,0:T(8,128)(2,1)S(1)}, u32[]{:S(2)}, u32[]{:S(2)}) %collective-permute-start.2) | collective-permute-done | bytes 262176 | tf_op jit(solution)/shard_map/ppermute | solution.py:170
  79.2 0.7 copy-done.8
  79.9 0.0 all-to-all-done.2
  79.9 0.9 copy-done.5
  80.9 0.9 copy-done.7
  81.8 0.9 copy-done.9
  82.8 0.3 join.1
  83.1 0.8 copy-done.1
  83.9 5.0 %all-to-all-start.3 = ((bf16[8,32,1024]{2,1,0:T(8,128)(2,1)}), bf16[8,32,1024]{2,1,0:T(8,128)(2,1)S(1)}, u32[]{:S(2)}, u32[]{:S(2)}) async-start(bf16[8,32,1024]{2,1,0:T(8,128)(2,1)} %copy-done.1), calls=%async_computation.3 | async-start | bytes 1048576 | tf_op jit(solution)/shard_map/all_to_all | solution.py:53
  88.9 10.3 %collective-permute-done.3.far_ref = bf16[512,1024]{1,0:T(8,128)(2,1)} collective-permute-done((bf16[512,1024]{1,0:T(8,128)(2,1)}, bf16[512,1024]{1,0:T(8,128)(2,1)}, u32[]{:S(2)}, u32[]{:S(2)}) %collective-permute-start.3) | collective-permute-done | bytes 1048608 | tf_op jit(solution)/shard_map/ppermute | solution.py:175
  99.1 10.9 %all-to-all-done.3.sums_ref = bf16[8,32,1024]{2,1,0:T(8,128)(2,1)S(1)} async-done(((bf16[8,32,1024]{2,1,0:T(8,128)(2,1)}), bf16[8,32,1024]{2,1,0:T(8,128)(2,1)S(1)}, u32[]{:S(2)}, u32[]{:S(2)}) %all-to-all-start.3) | async-done | bytes 524320 | tf_op jit(solution)/shard_map/all_to_all | solution.py:53
  110.0 0.8 copy-done.2
  110.8 1.0 copy-done.3
  111.9 3.4 %finish.1 = (f32[16,1024]{1,0:T(8,128)}, f32[16,1024]{1,0:T(8,128)}) custom-call(bf16[8,32,1024]{2,1,0:T(8,128)(2,1)S(1)} %copy-done.3, bf16[512,1024]{1,0:T(8,128)(2,1)} %bitcast.2.near_ref, bf16[512,1024]{1,0:T(8,128)(2,1)} %collective-permute-done.3.far_ref, f32[16,1024]{1,0:T(8,128)S(1)} %bitcast.16), custom_call_target="tpu_custom_call" | custom-call | tf_op jit(solution)/shard_map/finish/pallas_call | solution.py:142
  (12 shorter events, 0.0 us)
Async XLA Ops:
  0.6 46.2 %copy-start = (bf16[1024,1024]{1,0:T(8,128)(2,1)S(1)}, bf16[1024,1024]{1,0:T(8,128)(2,1)}, u32[]{:S(2)}) copy-start(bf16[1024,1024]{1,0:T(8,128)(2,1)} %param.3) | copy-start | bytes 6291460
  51.4 28.6 %all-to-all-start.2 = ((bf16[4,128,1024]{2,1,0:T(8,128)(2,1)}), bf16[4,128,1024]{2,1,0:T(8,128)(2,1)S(1)}, u32[]{:S(2)}, u32[]{:S(2)}) async-start(bf16[4,128,1024]{2,1,0:T(8,128)(2,1)} %bitcast.18), calls=%async_computation.2 | async-start | bytes 2097152 | tf_op jit(solution)/shard_map/all_to_all | solution.py:53
  58.9 51.9 %copy-start.10 = (f32[1024,16]{0,1:T(8,128)S(1)}, f32[1024,16]{0,1:T(8,128)}, u32[]{:S(2)}) copy-start(f32[1024,16]{0,1:T(8,128)} %param.5) | copy-start | bytes 196612
  59.0 15.5 %collective-permute-start = (bf16[8,16,1024]{2,1,0:T(8,128)(2,1)S(1)}, bf16[8,16,1024]{2,1,0:T(8,128)(2,1)S(1)}, u32[]{:S(2)}, u32[]{:S(2)}) collective-permute-start(bf16[8,16,1024]{2,1,0:T(8,128)(2,1)S(1)} %get-tuple-element.9), channel_id=1, source_target_pairs={{0,128},{1,129},{16,144},{17,145},{32,160},{33,161},{48,176},{49,1... | collective-permute-start | bytes 786440 | tf_op jit(solution)/shard_map/ppermute | solution.py:170
  62.9 12.3 %collective-permute-start.1 = (bf16[8,16,1024]{2,1,0:T(8,128)(2,1)S(1)}, bf16[8,16,1024]{2,1,0:T(8,128)(2,1)S(1)}, u32[]{:S(2)}, u32[]{:S(2)}) collective-permute-start(bf16[8,16,1024]{2,1,0:T(8,128)(2,1)S(1)} %get-tuple-element.10), channel_id=1, source_target_pairs={{0,16},{1,17},{16,0},{17,1},{32,48},{33,49},{48,32},{49,33},{64,80... | collective-permute-start | bytes 786440 | tf_op jit(solution)/shard_map/ppermute | solution.py:170
  66.3 13.0 %collective-permute-start.2 = (bf16[8,16,1024]{2,1,0:T(8,128)(2,1)S(1)}, bf16[8,16,1024]{2,1,0:T(8,128)(2,1)S(1)}, u32[]{:S(2)}, u32[]{:S(2)}) collective-permute-start(bf16[8,16,1024]{2,1,0:T(8,128)(2,1)S(1)} %get-tuple-element.11), channel_id=1, source_target_pairs={{0,144},{1,145},{16,128},{17,129},{32,176},{33,177},{48,160},{49,1... | collective-permute-start | bytes 786440 | tf_op jit(solution)/shard_map/ppermute | solution.py:170
  68.2 30.9 %collective-permute-start.3 = (bf16[512,1024]{1,0:T(8,128)(2,1)}, bf16[512,1024]{1,0:T(8,128)(2,1)}, u32[]{:S(2)}, u32[]{:S(2)}) collective-permute-start(bf16[512,1024]{1,0:T(8,128)(2,1)} %bitcast.2.near_ref), channel_id=1, source_target_pairs={{0,112},{16,32},{32,16},{48,64},{64,48},{80,96},{96,80},{112,0},{1... | collective-permute-start | bytes 3145736 | tf_op jit(solution)/shard_map/ppermute | solution.py:175
  74.5 0.7 copy-start.4
  75.2 0.7 copy-start.6
  79.2 0.7 copy-start.8
  79.9 1.0 copy-start.5
  80.9 0.9 copy-start.7
  81.8 0.9 copy-start.9
  83.1 0.8 copy-start.1
  83.9 26.2 %all-to-all-start.3 = ((bf16[8,32,1024]{2,1,0:T(8,128)(2,1)}), bf16[8,32,1024]{2,1,0:T(8,128)(2,1)S(1)}, u32[]{:S(2)}, u32[]{:S(2)}) async-start(bf16[8,32,1024]{2,1,0:T(8,128)(2,1)} %copy-done.1), calls=%async_computation.3 | async-start | bytes 1048576 | tf_op jit(solution)/shard_map/all_to_all | solution.py:53
  110.0 0.8 copy-start.2
  110.8 1.0 copy-start.3

commit v3 on v2

--- a/solution.py
+++ b/solution.py
@@ -29,12 +29,6 @@
     return member(2 * zh + b, 2 * yh + a, h ^ (yh & 1))
 
 
-SQUARES = [
-    [of_class(h, yh, zh, a, b) for a in range(2) for b in range(2)]
-    for h in range(2)
-    for yh in range(4)
-    for zh in range(2)
-]
 FAR_GROUPS = [
     [of_class(h, yh, zh, a, b) for yh in range(4) for zh in range(2)]
     for h in range(2)
@@ -88,33 +82,52 @@
     )(rows)
 
 
-def join_kernel(moment_ref, own_ref, *refs):
-    others, out_ref = refs[:3], refs[3]
+def moment_kernel(rows_ref, x_ref, out_ref):
+    x = x_ref[...]
+    whitened = lax.dot_general(rows_ref[...], x, ROWS_ROWS, preferred_element_type=f32)
+    out_ref[...] = jnp.dot(whitened.astype(bf16), x, preferred_element_type=f32).astype(bf16)
+
+
+def moment_of(rows, x):
+    return pl.pallas_call(
+        moment_kernel,
+        out_shape=jax.ShapeDtypeStruct(rows.shape, bf16),
+        in_specs=[vmem()] * 2,
+        out_specs=vmem(),
+        compiler_params=pltpu.CompilerParams(vmem_limit_bytes=VMEM_LIMIT),
+        cost_estimate=pl.CostEstimate(
+            flops=4 * rows.size * x.shape[0], bytes_accessed=2 * x.size, transcendentals=0
+        ),
+        name="moment",
+    )(rows, x)
+
+
+def join_kernel(*refs):
+    ins, out_ref = refs[:8], refs[8]
     for f in range(8):
-        total = moment_ref[0, f].astype(f32)
-        for k in range(1, 4):
-            total = total + moment_ref[k, f].astype(f32)
-        out_ref[f, :16] = total.astype(bf16)
-        total = own_ref[f].astype(f32)
-        for other in others:
-            total = total + other[f].astype(f32)
-        out_ref[f, 16:] = total.astype(bf16)
-
-
-def join(moment, own, others):
+        for first, parts in ((0, ins[:4]), (16, ins[4:])):
+            total = parts[0][f].astype(f32)
+            for part in parts[1:]:
+                total = total + part[f].astype(f32)
+            out_ref[f, first : first + 16] = total.astype(bf16)
+
+
+def join(moments, gradients):
+    width = gradients[0].shape[2]
+    moments = [m.reshape(8, 16, width) for m in moments]
     return pl.pallas_call(
         join_kernel,
-        out_shape=jax.ShapeDtypeStruct((8, 32, own.shape[2]), bf16),
-        in_specs=[vmem()] * 5,
+        out_shape=jax.ShapeDtypeStruct((8, 32, width), bf16),
+        in_specs=[vmem()] * 8,
         out_specs=vmem(),
         compiler_params=pltpu.CompilerParams(vmem_limit_bytes=VMEM_LIMIT),
         name="join",
-    )(moment, own, *others)
+    )(*moments, *gradients)
 
 
 def finish_kernel(tokens, sums_ref, near_ref, far_ref, own_ref, new_ref, direction_ref):
-    a, b, yh, zh, _ = position()
-    at = ((2 * a + b) * 8 + 2 * yh + zh) * 16
+    _, _, yh, zh, _ = position()
+    at = (2 * yh + zh) * 16
     own = own_ref[...]
     total = sums_ref[0].astype(f32)
     for k in range(1, 8):
@@ -153,27 +166,35 @@
     seq_count = lax.axis_size(SEQ)
     owned = factor.shape[1]
     width = factor.shape[0]
-    half_width = width // 2
     total_tokens = activations.shape[0] * seq_count
+
+    def turn(block, d):
+        return lax.ppermute(block, SEQ_GRP, TURNED[d])
 
     own = factor.T
     own_low = own.astype(bf16)
-    square = exchange(jnp.broadcast_to(own_low[None], (8, owned, width)), FAR_GROUPS)
-    square = square.reshape(1, 8 * owned, width)
-    near = exchange(jnp.broadcast_to(square, (4, 8 * owned, width)), SQUARES)
-    near = near.reshape(half_width, width)
+    with jax.named_scope("k_far"):
+        block = exchange(jnp.broadcast_to(own_low[None], (8, owned, width)), FAR_GROUPS)
 
     gradient_part = lax.dot_general(
         cotangent, activations, TOKENS_FIRST, preferred_element_type=f32
     ).astype(bf16)
     parts = pick(gradient_part.reshape(2 * seq_count, owned, width))
-    arrived = [lax.ppermute(parts[d], SEQ_GRP, TURNED[d]) for d in (1, 2, 3)]
-
-    whitened = lax.dot_general(near, activations, ROWS_ROWS, preferred_element_type=f32).astype(bf16)
-    moment = jnp.dot(whitened, activations, preferred_element_type=f32).astype(bf16)
-    moment = exchange(moment.reshape(4, 8 * owned, width), SQUARES)
-    far = lax.ppermute(near, "seq_1", ACROSS)
-    sums = exchange(join(moment.reshape(4, 8, owned, width), parts[0], arrived), FAR_GROUPS)
+    block, *parts = lax.optimization_barrier((block, *parts))
+    with jax.named_scope("g_near"):
+        gradients = [parts[0]] + [turn(parts[d], d) for d in (1, 2, 3)]
+
+    block = block.reshape(8 * owned, width)
+    with jax.named_scope("k_near"):
+        blocks = [block] + [turn(block, d) for d in (1, 2, 3)]
+    moments = [moment_of(rows, activations) for rows in blocks]
+    with jax.named_scope("p_near"):
+        moments = [moments[0]] + [turn(moments[d], d) for d in (1, 2, 3)]
+    near = jnp.concatenate(blocks, axis=0)
+    with jax.named_scope("k_across"):
+        far = lax.ppermute(near, "seq_1", ACROSS)
+    with jax.named_scope("p_far"):
+        sums = exchange(join(moments, gradients), FAR_GROUPS)
 
     new_factor, direction = finish(total_tokens, sums, near, far, own)
     return (new_factor.T, direction.T)

time: 116 us -> 108 us (0.931)
  blocking collectives: 45 us -> 0 us
  starting transfers between devices: 21.5 us -> 49.4 us
  waiting for transfers between devices: 27 us -> 39.2 us
  Pallas kernels: 3.7 us -> 8.8 us
  matrix products: 8.55 us -> 3.98 us
  local copies, waits for them, and re-layouts: 7.72 us -> 3.83 us
    all_to_all x2 -> x0, blocking collectives: 45 us -> none  [exchange(): lax.all_to_all(blocks, SEQ_GRP, split_axis=0, concat_axis=0, tiled=True,...]
    ppermute x3 -> x9, starting transfers between devices: 9.21 us -> 27.9 us  [turn(): return lax.ppermute(block, SEQ_GRP, TURNED[d])]
    ppermute x1, waiting for transfers between devices: 10.3 us -> 21.4 us  [on_device(): far = lax.ppermute(near, 'seq_1', ACROSS)]
    all_to_all x2, starting transfers between devices: 8.51 us -> 18.8 us  [exchange(): lax.all_to_all(blocks, SEQ_GRP, split_axis=0, concat_axis=0, tiled=True,...]
    dot_general x1 -> x0, matrix products: 4.57 us -> none  [on_device(): jnp.dot(whitened, activations, preferred_element_type=f32).astype(bf16)]
    unnamed x22 -> x14, local copies, waits for them, and re-layouts: 7.59 us -> 3.11 us
    pallas_call x1 -> x5, Pallas kernels: 0.26 us -> 4.7 us  [the longest x4 4.44 us: moment_of(): pl.pallas_call(moment_kernel, out_shape=jax.ShapeDtypeStruct(rows.shape,...]
    all_to_all x2, waiting for transfers between devices: 10.9 us -> 14 us  [exchange(): lax.all_to_all(blocks, SEQ_GRP, split_axis=0, concat_axis=0, tiled=True,...]
  transfers between devices with their start and end apart: 6 -> 12, of which waited for: 4 -> 4; matrix products, arithmetic and copies ran while one was open for 3% -> 4% of each run, Pallas kernels for 0% -> 5%
where the time goes in v3:
time: 108 us; the launch traced here: 107 us
  starting transfers between devices  49.4 us (46%)
  waiting for transfers between devices  39.2 us (36%)
  Pallas kernels  8.8 us (8%)
  matrix products  3.98 us (4%)
  local copies, waits for them, and re-layouts  3.83 us (4%)
    ppermute x9, starting transfers between devices, turn(): return lax.ppermute(block, SEQ_GRP, TURNED[d])  27.9 us
    ppermute x1, waiting for transfers between devices, on_device(): far = lax.ppermute(near, 'seq_1', ACROSS)  21.4 us
    all_to_all x2, starting transfers between devices, exchange(): lax.all_to_all(blocks, SEQ_GRP, split_axis=0, concat_axis=0, tiled=True,...  18.8 us
    all_to_all x2, waiting for transfers between devices, exchange(): lax.all_to_all(blocks, SEQ_GRP, split_axis=0, concat_axis=0, tiled=True,...  14 us
    pallas_call x4, Pallas kernels, moment_of(): pl.pallas_call(moment_kernel, out_shape=jax.ShapeDtypeStruct(rows.shape,...  4.44 us
    dot_general x1, matrix products, on_device(): lax.dot_general(cotangent, activations, TOKENS_FIRST, preferred_element_t...  3.98 us
    ppermute x9, waiting for transfers between devices, turn(): return lax.ppermute(block, SEQ_GRP, TURNED[d])  3.82 us
    pallas_call x1, Pallas kernels, finish(): pl.pallas_call(functools.partial(finish_kernel, tokens), out_shape=[jax.S...  3.2 us
  transfers between devices with their start and end apart: 12, of which 4 were waited for; matrix products, arithmetic and copies ran while one was open for 4% of the time, Pallas kernels for 5%

profile of v3, /device:TPU:6, one launch (start us, length us, event | category | flops | bytes accessed | tf_op | source)
XLA Modules:
  0.0 107.2 jit_solution(3267709598634642108)
XLA Ops:
  0.6 0.0 copy-start
  0.6 1.0 bitcast_convert_fusion
  1.6 0.7 broadcast_in_dim.2
  2.4 14.0 %all-to-all-start = ((bf16[8,16,1024]{2,1,0:T(8,128)(2,1)}), bf16[8,16,1024]{2,1,0:T(8,128)(2,1)S(1)}, u32[]{:S(2)}, u32[]{:S(2)}) async-start(bf16[8,16,1024]{2,1,0:T(8,128)(2,1)} %broadcast_in_dim.2), calls=%async_computation | async-start | bytes 524288 | tf_op jit(solution)/shard_map/k_far/all_to_all | solution.py:47
  16.4 4.0 %convolution_convert_fusion = bf16[1024,1024]{1,0:T(8,128)(2,1)S(1)} fusion(bf16[1024,1024]{1,0:T(8,128)(2,1)S(1)} %copy-done, bf16[1024,1024]{1,0:T(8,128)(2,1)} %x_ref.7), kind=kOutput, calls=%fused_computation | convolution fusion | flops 2148532224 | bytes 6291456 | tf_op jit(solution)/shard_map/dot_general | solution.py:179
  20.4 0.9 pick.1
  21.2 0.7 copy-done.4
  21.9 8.6 %all-to-all-done = bf16[8,16,1024]{2,1,0:T(8,128)(2,1)S(1)} async-done(((bf16[8,16,1024]{2,1,0:T(8,128)(2,1)}), bf16[8,16,1024]{2,1,0:T(8,128)(2,1)S(1)}, u32[]{:S(2)}, u32[]{:S(2)}) %all-to-all-start) | async-done | bytes 262176 | tf_op jit(solution)/shard_map/k_far/all_to_all | solution.py:47
  30.5 3.4 %collective-permute-start = (bf16[128,1024]{1,0:T(8,128)(2,1)S(1)}, bf16[128,1024]{1,0:T(8,128)(2,1)S(1)}, u32[]{:S(2)}, u32[]{:S(2)}) collective-permute-start(bf16[128,1024]{1,0:T(8,128)(2,1)S(1)} %bitcast.12), channel_id=1, source_target_pairs={{0,128},{1,129},{16,144},{17,145},{32,160},{33,161},{48,176},{49,1... | collective-permute-start | bytes 786440 | tf_op jit(solution)/shard_map/k_near/ppermute | solution.py:172
  33.9 2.1 %collective-permute-start.2 = (bf16[128,1024]{1,0:T(8,128)(2,1)S(1)}, bf16[128,1024]{1,0:T(8,128)(2,1)S(1)}, u32[]{:S(2)}, u32[]{:S(2)}) collective-permute-start(bf16[128,1024]{1,0:T(8,128)(2,1)S(1)} %bitcast.13), channel_id=1, source_target_pairs={{0,16},{1,17},{16,0},{17,1},{32,48},{33,49},{48,32},{49,33},{64,80... | collective-permute-start | bytes 786440 | tf_op jit(solution)/shard_map/k_near/ppermute | solution.py:172
  36.0 3.7 %collective-permute-start.4 = (bf16[128,1024]{1,0:T(8,128)(2,1)S(1)}, bf16[128,1024]{1,0:T(8,128)(2,1)S(1)}, u32[]{:S(2)}, u32[]{:S(2)}) collective-permute-start(bf16[128,1024]{1,0:T(8,128)(2,1)S(1)} %bitcast.14), channel_id=1, source_target_pairs={{0,144},{1,145},{16,128},{17,129},{32,176},{33,177},{48,160},{49,1... | collective-permute-start | bytes 786440 | tf_op jit(solution)/shard_map/k_near/ppermute | solution.py:172
  39.7 3.4 %collective-permute-start.6 = (bf16[8,16,1024]{2,1,0:T(8,128)(2,1)S(1)}, bf16[8,16,1024]{2,1,0:T(8,128)(2,1)S(1)}, u32[]{:S(2)}, u32[]{:S(2)}) collective-permute-start(bf16[8,16,1024]{2,1,0:T(8,128)(2,1)S(1)} %get-tuple-element.19), channel_id=1, source_target_pairs={{0,128},{1,129},{16,144},{17,145},{32,160},{33,161},{48,176},{49,1... | collective-permute-start | bytes 786440 | tf_op jit(solution)/shard_map/g_near/ppermute | solution.py:172
  43.1 2.1 %collective-permute-start.7 = (bf16[8,16,1024]{2,1,0:T(8,128)(2,1)}, bf16[8,16,1024]{2,1,0:T(8,128)(2,1)S(1)}, u32[]{:S(2)}, u32[]{:S(2)}) collective-permute-start(bf16[8,16,1024]{2,1,0:T(8,128)(2,1)} %get-tuple-element.20), channel_id=1, source_target_pairs={{0,16},{1,17},{16,0},{17,1},{32,48},{33,49},{48,32},{49,33},{64,80... | collective-permute-start | bytes 786440 | tf_op jit(solution)/shard_map/g_near/ppermute | solution.py:172
  45.2 3.7 %collective-permute-start.8 = (bf16[8,16,1024]{2,1,0:T(8,128)(2,1)}, bf16[8,16,1024]{2,1,0:T(8,128)(2,1)S(1)}, u32[]{:S(2)}, u32[]{:S(2)}) collective-permute-start(bf16[8,16,1024]{2,1,0:T(8,128)(2,1)} %get-tuple-element.21), channel_id=1, source_target_pairs={{0,144},{1,145},{16,128},{17,129},{32,176},{33,177},{48,160},{49,1... | collective-permute-start | bytes 786440 | tf_op jit(solution)/shard_map/g_near/ppermute | solution.py:172
  49.0 1.6 %copy-done.1 = bf16[1024,1024]{1,0:T(8,128)(2,1)S(1)} copy-done((bf16[1024,1024]{1,0:T(8,128)(2,1)S(1)}, bf16[1024,1024]{1,0:T(8,128)(2,1)}, u32[]{:S(2)}) %copy-start.1) | copy-done | bytes 2097176
  50.6 1.1 %moment.5 = bf16[128,1024]{1,0:T(8,128)(2,1)S(1)} custom-call(bf16[128,1024]{1,0:T(8,128)(2,1)S(1)} %collective-permute-done.rows_ref, bf16[1024,1024]{1,0:T(8,128)(2,1)S(1)} %copy-done.1), custom_call_target="tpu_custom_call" | custom-call | flops 536870912 | bytes 2097152 | tf_op jit(solution)/shard_map/moment/pallas_call | solution.py:92
  51.7 3.4 %collective-permute-start.1 = (bf16[128,1024]{1,0:T(8,128)(2,1)S(1)}, bf16[128,1024]{1,0:T(8,128)(2,1)S(1)}, u32[]{:S(2)}, u32[]{:S(2)}) collective-permute-start(bf16[128,1024]{1,0:T(8,128)(2,1)S(1)} %moment.5), channel_id=1, source_target_pairs={{0,128},{1,129},{16,144},{17,145},{32,160},{33,161},{48,176},{49,1... | collective-permute-start | bytes 786440 | tf_op jit(solution)/shard_map/p_near/ppermute | solution.py:172
  55.1 1.1 %moment.6 = bf16[128,1024]{1,0:T(8,128)(2,1)S(1)} custom-call(bf16[128,1024]{1,0:T(8,128)(2,1)S(1)} %collective-permute-done.2.rows_ref, bf16[1024,1024]{1,0:T(8,128)(2,1)S(1)} %copy-done.1), custom_call_target="tpu_custom_call" | custom-call | flops 536870912 | bytes 2097152 | tf_op jit(solution)/shard_map/moment/pallas_call | solution.py:92
  56.2 2.2 %collective-permute-start.3 = (bf16[128,1024]{1,0:T(8,128)(2,1)S(1)}, bf16[128,1024]{1,0:T(8,128)(2,1)S(1)}, u32[]{:S(2)}, u32[]{:S(2)}) collective-permute-start(bf16[128,1024]{1,0:T(8,128)(2,1)S(1)} %moment.6), channel_id=1, source_target_pairs={{0,16},{1,17},{16,0},{17,1},{32,48},{33,49},{48,32},{49,33},{64,80... | collective-permute-start | bytes 786440 | tf_op jit(solution)/shard_map/p_near/ppermute | solution.py:172
  58.5 1.1 %moment.7 = bf16[128,1024]{1,0:T(8,128)(2,1)S(1)} custom-call(bf16[128,1024]{1,0:T(8,128)(2,1)S(1)} %collective-permute-done.4.rows_ref, bf16[1024,1024]{1,0:T(8,128)(2,1)S(1)} %copy-done.1), custom_call_target="tpu_custom_call" | custom-call | flops 536870912 | bytes 2097152 | tf_op jit(solution)/shard_map/moment/pallas_call | solution.py:92
  59.6 3.9 %collective-permute-start.5 = (bf16[128,1024]{1,0:T(8,128)(2,1)S(1)}, bf16[128,1024]{1,0:T(8,128)(2,1)S(1)}, u32[]{:S(2)}, u32[]{:S(2)}) collective-permute-start(bf16[128,1024]{1,0:T(8,128)(2,1)S(1)} %moment.7), channel_id=1, source_target_pairs={{0,144},{1,145},{16,128},{17,129},{32,176},{33,177},{48,160},{49,1... | collective-permute-start | bytes 786440 | tf_op jit(solution)/shard_map/p_near/ppermute | solution.py:172
  63.5 0.1 pad_maximum_fusion.near_ref
  63.6 2.7 %collective-permute-start.9 = (bf16[512,1024]{1,0:T(8,128)(2,1)S(1)}, bf16[512,1024]{1,0:T(8,128)(2,1)}, u32[]{:S(2)}, u32[]{:S(2)}) collective-permute-start(bf16[512,1024]{1,0:T(8,128)(2,1)S(1)} %pad_maximum_fusion.near_ref), channel_id=1, source_target_pairs={{0,112},{16,32},{32,16},{48,64},{64,48},{80,96},{96,80},{112,0},{1... | collective-permute-start | bytes 3145736 | tf_op jit(solution)/shard_map/k_across/ppermute | solution.py:195
  66.3 1.1 %moment.4 = bf16[128,1024]{1,0:T(8,128)(2,1)S(1)} custom-call(bf16[128,1024]{1,0:T(8,128)(2,1)S(1)} %bitcast.16, bf16[1024,1024]{1,0:T(8,128)(2,1)S(1)} %copy-done.2), custom_call_target="tpu_custom_call" | custom-call | flops 536870912 | bytes 2097152 | tf_op jit(solution)/shard_map/moment/pallas_call | solution.py:92
  67.4 0.0 collective-permute-done.3
  67.5 3.8 %collective-permute-done.5 = bf16[128,1024]{1,0:T(8,128)(2,1)S(1)} collective-permute-done((bf16[128,1024]{1,0:T(8,128)(2,1)S(1)}, bf16[128,1024]{1,0:T(8,128)(2,1)S(1)}, u32[]{:S(2)}, u32[]{:S(2)}) %collective-permute-start.5) | collective-permute-done | bytes 262176 | tf_op jit(solution)/shard_map/p_near/ppermute | solution.py:172
  71.2 0.3 join.1
  71.5 0.8 copy-done.3
  72.3 4.8 %all-to-all-start.1 = ((bf16[8,32,1024]{2,1,0:T(8,128)(2,1)}), bf16[8,32,1024]{2,1,0:T(8,128)(2,1)}, u32[]{:S(2)}, u32[]{:S(2)}) async-start(bf16[8,32,1024]{2,1,0:T(8,128)(2,1)} %copy-done.3), calls=%async_computation.1 | async-start | bytes 1048576 | tf_op jit(solution)/shard_map/p_far/all_to_all | solution.py:47
  77.1 21.4 %collective-permute-done.9.far_ref = bf16[512,1024]{1,0:T(8,128)(2,1)} collective-permute-done((bf16[512,1024]{1,0:T(8,128)(2,1)S(1)}, bf16[512,1024]{1,0:T(8,128)(2,1)}, u32[]{:S(2)}, u32[]{:S(2)}) %collective-permute-start.9) | collective-permute-done | bytes 1048608 | tf_op jit(solution)/shard_map/k_across/ppermute | solution.py:195
  98.5 5.5 %all-to-all-done.1.sums_ref = bf16[8,32,1024]{2,1,0:T(8,128)(2,1)} async-done(((bf16[8,32,1024]{2,1,0:T(8,128)(2,1)}), bf16[8,32,1024]{2,1,0:T(8,128)(2,1)}, u32[]{:S(2)}, u32[]{:S(2)}) %all-to-all-start.1) | async-done | bytes 524320 | tf_op jit(solution)/shard_map/p_far/all_to_all | solution.py:47
  104.0 3.2 %finish.1 = (f32[16,1024]{1,0:T(8,128)}, f32[16,1024]{1,0:T(8,128)}) custom-call(bf16[8,32,1024]{2,1,0:T(8,128)(2,1)} %all-to-all-done.1.sums_ref, bf16[512,1024]{1,0:T(8,128)(2,1)S(1)} %pad_maximum_fusion.near_ref, bf16[512,1024]{1,0:T(8,128)(2,1)} %collective-permute-done.9.far_ref, f32[16,1024]{1,0:T(8,128)S(1)} %bitcast.22), custom_call_target="tpu_custom_call" | custom-call | tf_op jit(solution)/shard_map/finish/pallas_call | solution.py:155
  (17 shorter events, 0.0 us)
Async XLA Ops:
  0.6 15.7 %copy-start = (bf16[1024,1024]{1,0:T(8,128)(2,1)S(1)}, bf16[1024,1024]{1,0:T(8,128)(2,1)}, u32[]{:S(2)}) copy-start(bf16[1024,1024]{1,0:T(8,128)(2,1)} %param.4) | copy-start | bytes 6291460
  2.4 28.1 %all-to-all-start = ((bf16[8,16,1024]{2,1,0:T(8,128)(2,1)}), bf16[8,16,1024]{2,1,0:T(8,128)(2,1)S(1)}, u32[]{:S(2)}, u32[]{:S(2)}) async-start(bf16[8,16,1024]{2,1,0:T(8,128)(2,1)} %broadcast_in_dim.2), calls=%async_computation | async-start | bytes 524288 | tf_op jit(solution)/shard_map/k_far/all_to_all | solution.py:47
  21.2 0.7 copy-start.4
  30.5 14.7 %collective-permute-start = (bf16[128,1024]{1,0:T(8,128)(2,1)S(1)}, bf16[128,1024]{1,0:T(8,128)(2,1)S(1)}, u32[]{:S(2)}, u32[]{:S(2)}) collective-permute-start(bf16[128,1024]{1,0:T(8,128)(2,1)S(1)} %bitcast.12), channel_id=1, source_target_pairs={{0,128},{1,129},{16,144},{17,145},{32,160},{33,161},{48,176},{49,1... | collective-permute-start | bytes 786440 | tf_op jit(solution)/shard_map/k_near/ppermute | solution.py:172
  33.9 17.8 %collective-permute-start.2 = (bf16[128,1024]{1,0:T(8,128)(2,1)S(1)}, bf16[128,1024]{1,0:T(8,128)(2,1)S(1)}, u32[]{:S(2)}, u32[]{:S(2)}) collective-permute-start(bf16[128,1024]{1,0:T(8,128)(2,1)S(1)} %bitcast.13), channel_id=1, source_target_pairs={{0,16},{1,17},{16,0},{17,1},{32,48},{33,49},{48,32},{49,33},{64,80... | collective-permute-start | bytes 786440 | tf_op jit(solution)/shard_map/k_near/ppermute | solution.py:172
  36.0 20.2 %collective-permute-start.4 = (bf16[128,1024]{1,0:T(8,128)(2,1)S(1)}, bf16[128,1024]{1,0:T(8,128)(2,1)S(1)}, u32[]{:S(2)}, u32[]{:S(2)}) collective-permute-start(bf16[128,1024]{1,0:T(8,128)(2,1)S(1)} %bitcast.14), channel_id=1, source_target_pairs={{0,144},{1,145},{16,128},{17,129},{32,176},{33,177},{48,160},{49,1... | collective-permute-start | bytes 786440 | tf_op jit(solution)/shard_map/k_near/ppermute | solution.py:172
  39.7 19.9 %collective-permute-start.6 = (bf16[8,16,1024]{2,1,0:T(8,128)(2,1)S(1)}, bf16[8,16,1024]{2,1,0:T(8,128)(2,1)S(1)}, u32[]{:S(2)}, u32[]{:S(2)}) collective-permute-start(bf16[8,16,1024]{2,1,0:T(8,128)(2,1)S(1)} %get-tuple-element.19), channel_id=1, source_target_pairs={{0,128},{1,129},{16,144},{17,145},{32,160},{33,161},{48,176},{49,1... | collective-permute-start | bytes 786440 | tf_op jit(solution)/shard_map/g_near/ppermute | solution.py:172
  43.1 20.4 %collective-permute-start.7 = (bf16[8,16,1024]{2,1,0:T(8,128)(2,1)}, bf16[8,16,1024]{2,1,0:T(8,128)(2,1)S(1)}, u32[]{:S(2)}, u32[]{:S(2)}) collective-permute-start(bf16[8,16,1024]{2,1,0:T(8,128)(2,1)} %get-tuple-element.20), channel_id=1, source_target_pairs={{0,16},{1,17},{16,0},{17,1},{32,48},{33,49},{48,32},{49,33},{64,80... | collective-permute-start | bytes 786440 | tf_op jit(solution)/shard_map/g_near/ppermute | solution.py:172
  45.2 22.2 %collective-permute-start.8 = (bf16[8,16,1024]{2,1,0:T(8,128)(2,1)}, bf16[8,16,1024]{2,1,0:T(8,128)(2,1)S(1)}, u32[]{:S(2)}, u32[]{:S(2)}) collective-permute-start(bf16[8,16,1024]{2,1,0:T(8,128)(2,1)} %get-tuple-element.21), channel_id=1, source_target_pairs={{0,144},{1,145},{16,128},{17,129},{32,176},{33,177},{48,160},{49,1... | collective-permute-start | bytes 786440 | tf_op jit(solution)/shard_map/g_near/ppermute | solution.py:172
  49.0 1.6 %copy-start.1 = (bf16[1024,1024]{1,0:T(8,128)(2,1)S(1)}, bf16[1024,1024]{1,0:T(8,128)(2,1)}, u32[]{:S(2)}) copy-start(bf16[1024,1024]{1,0:T(8,128)(2,1)} %x_ref.7) | copy-start | bytes 6291460
  51.7 15.7 %collective-permute-start.1 = (bf16[128,1024]{1,0:T(8,128)(2,1)S(1)}, bf16[128,1024]{1,0:T(8,128)(2,1)S(1)}, u32[]{:S(2)}, u32[]{:S(2)}) collective-permute-start(bf16[128,1024]{1,0:T(8,128)(2,1)S(1)} %moment.5), channel_id=1, source_target_pairs={{0,128},{1,129},{16,144},{17,145},{32,160},{33,161},{48,176},{49,1... | collective-permute-start | bytes 786440 | tf_op jit(solution)/shard_map/p_near/ppermute | solution.py:172
  56.2 10.0 %copy-start.2 = (bf16[1024,1024]{1,0:T(8,128)(2,1)S(1)}, bf16[1024,1024]{1,0:T(8,128)(2,1)}, u32[]{:S(2)}) copy-start(bf16[1024,1024]{1,0:T(8,128)(2,1)} %x_ref.7) | copy-start | bytes 6291460
  56.2 11.2 %collective-permute-start.3 = (bf16[128,1024]{1,0:T(8,128)(2,1)S(1)}, bf16[128,1024]{1,0:T(8,128)(2,1)S(1)}, u32[]{:S(2)}, u32[]{:S(2)}) collective-permute-start(bf16[128,1024]{1,0:T(8,128)(2,1)S(1)} %moment.6), channel_id=1, source_target_pairs={{0,16},{1,17},{16,0},{17,1},{32,48},{33,49},{48,32},{49,33},{64,80... | collective-permute-start | bytes 786440 | tf_op jit(solution)/shard_map/p_near/ppermute | solution.py:172
  59.6 11.6 %copy-start.5 = (bf16[8,16,1024]{2,1,0:T(8,128)(2,1)S(1)}, bf16[8,16,1024]{2,1,0:T(8,128)(2,1)}, u32[]{:S(2)}) copy-start(bf16[8,16,1024]{2,1,0:T(8,128)(2,1)} %copy-done.4) | copy-start | bytes 786436
  59.6 11.6 %collective-permute-start.5 = (bf16[128,1024]{1,0:T(8,128)(2,1)S(1)}, bf16[128,1024]{1,0:T(8,128)(2,1)S(1)}, u32[]{:S(2)}, u32[]{:S(2)}) collective-permute-start(bf16[128,1024]{1,0:T(8,128)(2,1)S(1)} %moment.7), channel_id=1, source_target_pairs={{0,144},{1,145},{16,128},{17,129},{32,176},{33,177},{48,160},{49,1... | collective-permute-start | bytes 786440 | tf_op jit(solution)/shard_map/p_near/ppermute | solution.py:172
  63.6 34.9 %collective-permute-start.9 = (bf16[512,1024]{1,0:T(8,128)(2,1)S(1)}, bf16[512,1024]{1,0:T(8,128)(2,1)}, u32[]{:S(2)}, u32[]{:S(2)}) collective-permute-start(bf16[512,1024]{1,0:T(8,128)(2,1)S(1)} %pad_maximum_fusion.near_ref), channel_id=1, source_target_pairs={{0,112},{16,32},{32,16},{48,64},{64,48},{80,96},{96,80},{112,0},{1... | collective-permute-start | bytes 3145736 | tf_op jit(solution)/shard_map/k_across/ppermute | solution.py:195
  67.4 36.6 %copy-start.6 = (f32[1024,16]{0,1:T(8,128)S(1)}, f32[1024,16]{0,1:T(8,128)}, u32[]{:S(2)}) copy-start(f32[1024,16]{0,1:T(8,128)} %param.5) | copy-start | bytes 196612
  71.5 0.8 copy-start.3
  72.3 31.7 %all-to-all-start.1 = ((bf16[8,32,1024]{2,1,0:T(8,128)(2,1)}), bf16[8,32,1024]{2,1,0:T(8,128)(2,1)}, u32[]{:S(2)}, u32[]{:S(2)}) async-start(bf16[8,32,1024]{2,1,0:T(8,128)(2,1)} %copy-done.3), calls=%async_computation.1 | async-start | bytes 1048576 | tf_op jit(solution)/shard_map/p_far/all_to_all | solution.py:47

commit v4 on v3

v4 whole, which is shorter than its diff:
```python
import functools

import jax
import jax.numpy as jnp
from jax import lax
from jax.experimental import pallas as pl
from jax.experimental.pallas import tpu as pltpu
from jax.sharding import Mesh
from jax.sharding import PartitionSpec as P

SEQ = ("seq_0", "seq_1")
SEQ_GRP = ("seq_0", "seq_1", "grp")


damping = 0.25
step_size = 0.4

f32, bf16 = jnp.float32, jnp.bfloat16
VMEM_LIMIT = 16 * 1024 * 1024
ROWS_ROWS = (((1,), (1,)), ((), ()))
TOKENS_FIRST = (((0,), (0,)), ((), ()))


def member(z_low, y, grp):
    return (z_low * 8 + y) * 2 + grp


def of_class(h, yh, zh, a, b):
    return member(2 * zh + b, 2 * yh + a, h ^ (yh & 1))


FAR_GROUPS = [
    [of_class(h, yh, zh, a, b) for yh in range(4) for zh in range(2)]
    for h in range(2)
    for a in range(2)
    for b in range(2)
]
COSETS = [FAR_GROUPS[k] + FAR_GROUPS[k + 4] for k in range(4)]


def outer(at):
    return (at - 1) % 8 if at % 2 == 0 else (at + 1) % 8


def moves(step_z, step_y):
    pairs = []
    for z in range(8):
        for y in range(8):
            there_z, there_y = step_z(z), step_y(y)
            pairs.append((member(z % 4, y, z // 4), member(there_z % 4, there_y, there_z // 4)))
    return pairs


def stay(at):
    return at


def inner(at):
    return at ^ 1


INNER = {1: moves(inner, stay), 2: moves(stay, inner), 3: moves(inner, inner)}
OUTER = {1: moves(outer, stay), 2: moves(stay, outer), 3: moves(outer, outer)}


def exchange(blocks, groups):
    return lax.all_to_all(
        blocks, SEQ_GRP, split_axis=0, concat_axis=0, tiled=True, axis_index_groups=groups
    )


def vmem():
    return pl.BlockSpec(memory_space=pltpu.VMEM)


def hbm():
    return pl.BlockSpec(memory_space=pltpu.HBM)


def run_copies(pairs, sems):
    copies = [pltpu.make_async_copy(*pair, sems.at[k]) for k, pair in enumerate(pairs)]
    for copy in copies:
        copy.start()
    return copies


def position():
    z_low, y, grp = lax.axis_index("seq_0"), lax.axis_index("seq_1"), lax.axis_index("grp")
    yh = y // 2
    return y % 2, z_low % 2, yh, z_low // 2, (grp + yh) % 2


def call(kernel, out_shape, in_specs, out_specs, *args, **more):
    return pl.pallas_call(
        kernel,
        out_shape=out_shape,
        in_specs=in_specs,
        out_specs=out_specs,
        compiler_params=pltpu.CompilerParams(vmem_limit_bytes=VMEM_LIMIT),
        **more,
    )(*args)


def spread_kernel(own_ref, out_ref, low, sems):
    low[...] = own_ref[...].astype(bf16)
    for copy in run_copies([(low, out_ref.at[k]) for k in range(out_ref.shape[0])], sems):
        copy.wait()


def spread(own, count):
    shape = pltpu.HBM((count,) + own.shape, bf16)
    scratch = [pltpu.VMEM(own.shape, bf16), pltpu.SemaphoreType.DMA((count,))]
    return call(spread_kernel, shape, [vmem()], hbm(), own, scratch_shapes=scratch)


def mine_kernel(blocks_ref, out_ref):
    out_ref[...] = blocks_ref[position()[4]]


def own_class(blocks):
    shape = jax.ShapeDtypeStruct(blocks.shape[1:], bf16)
    return call(mine_kernel, shape, [vmem()], vmem(), blocks)


def others_kernel(blocks_ref, other_ref, side_ref, corner_ref, sems):
    _, b, yh, zh, h = position()
    z_low, grp = 2 * zh + b, (h + yh) % 2
    turn = jnp.where((z_low == 0) | (z_low == 3), 1, 0)
    side_class = (grp + turn + yh) % 2
    pairs = [
        (blocks_ref.at[1 - h], other_ref),
        (blocks_ref.at[1 - side_class], side_ref),
        (blocks_ref.at[side_class], corner_ref),
    ]
    for copy in run_copies(pairs, sems):
        copy.wait()


def others(blocks):
    shape = pltpu.HBM(blocks.shape[1:], bf16)
    scratch = [pltpu.SemaphoreType.DMA((3,))]
    return call(others_kernel, [shape] * 3, [vmem()], [hbm()] * 3, blocks, scratch_shapes=scratch)


def pick_kernel(rows_ref, *refs):
    out_refs, sems = refs[:4], refs[4]
    a, b, _, _, h = position()
    pairs = []
    for d, out_ref in enumerate(out_refs):
        a_there = 1 - a if d & 2 else a
        b_there = 1 - b if d & 1 else b
        for f in range(8):
            row, column = f >> 1, f & 1
            grp = 1 - h if row & 1 else h
            there = member(2 * column + b_there, 2 * row + a_there, grp)
            pairs.append((rows_ref.at[there], out_ref.at[f]))
    for copy in run_copies(pairs, sems):
        copy.wait()


def pick(rows):
    shape = pltpu.HBM((8,) + rows.shape[1:], rows.dtype)
    scratch = [pltpu.SemaphoreType.DMA((32,))]
    return call(pick_kernel, [shape] * 4, [vmem()], [hbm()] * 4, rows, scratch_shapes=scratch)


def moment_kernel(rows_ref, x_ref, out_ref):
    x = x_ref[...]
    whitened = lax.dot_general(rows_ref[...], x, ROWS_ROWS, preferred_element_type=f32)
    out_ref[...] = jnp.dot(whitened.astype(bf16), x, preferred_element_type=f32).astype(bf16)


def moment_of(rows, x):
    return pl.pallas_call(
        moment_kernel,
        out_shape=jax.ShapeDtypeStruct(rows.shape, bf16),
        in_specs=[vmem()] * 2,
        out_specs=vmem(),
        compiler_params=pltpu.CompilerParams(vmem_limit_bytes=VMEM_LIMIT),
        cost_estimate=pl.CostEstimate(
            flops=4 * rows.size * x.shape[0], bytes_accessed=2 * x.size, transcendentals=0
        ),
        name="moment",
    )(rows, x)


def join_kernel(*refs):
    moments, far_gradients, out_ref = refs[:4], refs[4:8], refs[8]
    gradients, staged, sems, out_sems = refs[9:]
    arriving = run_copies([(ref, gradients.at[d]) for d, ref in enumerate(far_gradients)], sems)
    for f in range(8):
        total = moments[0][f].astype(f32)
        for part in moments[1:]:
            total = total + part[f].astype(f32)
        staged[f, :16] = total.astype(bf16)
    for copy in arriving:
        copy.wait()
    leaving = []
    for f in range(8):
        total = gradients[0, f].astype(f32)
        for d in range(1, 4):
            total = total + gradients[d, f].astype(f32)
        staged[f, 16:] = total.astype(bf16)
        copy = pltpu.make_async_copy(staged.at[f], out_ref.at[f], out_sems.at[f])
        copy.start()
        leaving.append(copy)
    for copy in leaving:
        copy.wait()


def join(moments, gradients):
    width = gradients[0].shape[2]
    moments = [m.reshape(8, 16, width) for m in moments]
    shape = pltpu.HBM((8, 32, width), bf16)
    scratch = [
        pltpu.VMEM((4, 8, 16, width), bf16),
        pltpu.VMEM(shape.shape, bf16),
        pltpu.SemaphoreType.DMA((4,)),
        pltpu.SemaphoreType.DMA((8,)),
    ]
    specs = [vmem()] * 4 + [hbm()] * 4
    gradients = [pltpu.with_memory_space_constraint(g, pltpu.HBM) for g in gradients]
    return call(join_kernel, shape, specs, hbm(), *moments, *gradients, scratch_shapes=scratch)


def finish_kernel(tokens, *refs):
    sums_ref, own_ref, blocks = refs[0], refs[1], refs[2:10]
    new_ref, direction_ref, rows, sems = refs[10:]
    pairs = [(block, rows.at[pl.ds(k * 128, 128)]) for k, block in enumerate(blocks)]
    copies = run_copies(pairs, sems)
    _, _, yh, zh, _ = position()
    at = (2 * yh + zh) * 16
    own = own_ref[...]
    total = sums_ref[0].astype(f32)
    for k in range(1, 8):
        total = total + sums_ref[k].astype(f32)
    inner_rows = total[:16] / tokens + damping * own.astype(bf16).astype(f32)
    high = inner_rows.astype(bf16)
    low = (inner_rows - high.astype(f32)).astype(bf16)
    left = jnp.concatenate([high, low, total[16:].astype(bf16)], axis=0)
    for copy in copies:
        copy.wait()
    product = lax.dot_general(left, rows[...], ROWS_ROWS, preferred_element_type=f32)
    curve = product[:16] + product[16:32]
    column = lax.broadcasted_iota(jnp.int32, curve.shape, 1)
    row = lax.broadcasted_iota(jnp.int32, curve.shape, 0)
    curve = curve - (column == row + at).astype(f32)
    right = jnp.concatenate([curve.astype(bf16), product[32:].astype(bf16)], axis=0)
    result = jnp.dot(right, rows[...], preferred_element_type=f32)
    new_ref[...] = own - 0.5 * step_size * result[:16]
    direction_ref[...] = result[16:]


def finish(tokens, sums, own, blocks):
    blocks = [pltpu.with_memory_space_constraint(block, pltpu.HBM) for block in blocks]
    scratch = [
        pltpu.VMEM((8 * 128, own.shape[1]), bf16),
        pltpu.SemaphoreType.DMA((8,)),
    ]
    return call(
        functools.partial(finish_kernel, tokens),
        [jax.ShapeDtypeStruct(own.shape, f32)] * 2,
        [vmem()] * 2 + [hbm()] * 8,
        [vmem()] * 2,
        sums,
        own,
        *blocks,
        scratch_shapes=scratch,
    )


def on_device(activations, cotangent, factor):
    seq_count = lax.axis_size(SEQ)
    owned = factor.shape[1]
    width = factor.shape[0]
    total_tokens = activations.shape[0] * seq_count

    def turn(block, pairs):
        return lax.ppermute(block, SEQ_GRP, pairs)

    own = factor.T
    blocks = exchange(spread(own, 16), COSETS)

    gradient_part = lax.dot_general(
        cotangent, activations, TOKENS_FIRST, preferred_element_type=f32
    ).astype(bf16)
    parts = pick(gradient_part.reshape(2 * seq_count, owned, width))
    gradients = [parts[0]]
    for d in (1, 2, 3):
        gradients.append(turn(parts[d], INNER[d]))

    blocks = blocks.reshape(2, 8 * owned, width)
    mine = own_class(blocks)
    near = [mine]
    for d in (1, 2, 3):
        near.append(turn(mine, INNER[d]))
    moments = [moment_of(mine, activations)]
    for d in (1, 2, 3):
        moment = moment_of(near[d], activations)
        moments.append(turn(moment, INNER[d]))
    other, side, corner = others(blocks)
    far = [other]
    for d, block in ((1, side), (2, mine), (3, corner)):
        far.append(turn(block, OUTER[d]))
    joined = join(moments, gradients)
    sums = exchange(joined, FAR_GROUPS)

    new_factor, direction = finish(total_tokens, sums, own, near + far)
    return (new_factor.T, direction.T)


def solution(mesh):
    torus = Mesh(
        mesh.devices.reshape(4, 8, mesh.shape["blk"], mesh.shape["grp"]),
        ("seq_0", "seq_1", "blk", "grp"),
    )
    return jax.shard_map(
        on_device,
        mesh=torus,
        in_specs=(P(SEQ, "blk"), P(SEQ, None), P("blk", SEQ_GRP)),
        out_specs=(P("blk", SEQ_GRP), P("blk", SEQ_GRP)),
        check_vma=False,
    )
```

time: 108 us -> 124 us (1.15)
  blocking collectives: 0 us -> 34.9 us
  waiting for transfers between devices: 39.2 us -> 18.2 us
  Pallas kernels: 8.8 us -> 13.2 us
  local copies, waits for them, and re-layouts: 3.83 us -> 1.74 us
  matrix products: 3.98 us -> 2.41 us
  starting transfers between devices: 49.4 us -> 50.7 us
    all_to_all x0 -> x1, blocking collectives: none -> 34.9 us  [exchange(): lax.all_to_all(blocks, SEQ_GRP, split_axis=0, concat_axis=0, tiled=True,...]
    all_to_all x2 -> x1, waiting for transfers between devices: 14 us -> 0.01 us  [exchange(): lax.all_to_all(blocks, SEQ_GRP, split_axis=0, concat_axis=0, tiled=True,...]
    ppermute x10 -> x12, starting transfers between devices: 30.6 us -> 42.7 us  [turn(): return lax.ppermute(block, SEQ_GRP, pairs)]
    all_to_all x2 -> x1, starting transfers between devices: 18.8 us -> 7.96 us  [exchange(): lax.all_to_all(blocks, SEQ_GRP, split_axis=0, concat_axis=0, tiled=True,...]
    ppermute x10 -> x12, waiting for transfers between devices: 25.2 us -> 18.2 us  [turn(): return lax.ppermute(block, SEQ_GRP, pairs)]
    pallas_call x3 -> x6, Pallas kernels: 4.35 us -> 8.72 us  [call(): pl.pallas_call(kernel, out_shape=out_shape, in_specs=in_specs, out_specs=...]
    dot_general x1, matrix products: 3.98 us -> 2.41 us  [on_device(): lax.dot_general(cotangent, activations, TOKENS_FIRST, preferred_element_t...]
    unnamed x14 -> x28, local copies, waits for them, and re-layouts: 3.11 us -> 1.74 us
  transfers between devices with their start and end apart: 12 -> 13, of which waited for: 4 -> 6; matrix products, arithmetic and copies ran while one was open for 4% -> 2% of each run, Pallas kernels for 5% -> 5%
where the time goes in v4:
time: 124 us; the launch traced here: 122 us
  starting transfers between devices  50.7 us (41%)
  blocking collectives  34.9 us (28%)
  waiting for transfers between devices  18.2 us (15%)
  Pallas kernels  13.2 us (11%)
  matrix products  2.41 us (2%)
  local copies, waits for them, and re-layouts  1.74 us (1%)
    ppermute x12, starting transfers between devices, turn(): return lax.ppermute(block, SEQ_GRP, pairs)  42.7 us
    all_to_all x1, blocking collectives, exchange(): lax.all_to_all(blocks, SEQ_GRP, split_axis=0, concat_axis=0, tiled=True,...  34.9 us
    ppermute x12, waiting for transfers between devices, turn(): return lax.ppermute(block, SEQ_GRP, pairs)  18.2 us
    pallas_call x6, Pallas kernels, call(): pl.pallas_call(kernel, out_shape=out_shape, in_specs=in_specs, out_specs=...  8.72 us
    all_to_all x1, starting transfers between devices, exchange(): lax.all_to_all(blocks, SEQ_GRP, split_axis=0, concat_axis=0, tiled=True,...  7.96 us
    pallas_call x4, Pallas kernels, moment_of(): pl.pallas_call(moment_kernel, out_shape=jax.ShapeDtypeStruct(rows.shape,...  4.44 us
  transfers between devices with their start and end apart: 13, of which 6 were waited for; matrix products, arithmetic and copies ran while one was open for 2% of the time, Pallas kernels for 5%

profile of v4, /device:TPU:6, one launch (start us, length us, event | category | flops | bytes accessed | tf_op | source)
XLA Modules:
  0.0 122.1 jit_solution(712194441625151035)
XLA Ops:
  0.7 1.0 copy-done.6
  1.6 1.0 shard_map.50
  2.6 34.9 %all_to_all.10 = bf16[16,16,1024]{2,1,0:T(8,128)(2,1)S(1)} all-to-all(bf16[16,16,1024]{2,1,0:T(8,128)(2,1)} %shard_map.50), channel_id=1, replica_groups={{0,256,33,289,64,320,97,353,1,257,32,288,65,321,96,352},{128,384,161,41..., dimensions={0} | all-to-all | bytes 1048576 | tf_op jit(solution)/shard_map/all_to_all | solution.py:67
  37.6 3.2 %collective-permute-start = (bf16[128,1024]{1,0:T(8,128)(2,1)S(1)}, bf16[128,1024]{1,0:T(8,128)(2,1)S(1)}, u32[]{:S(2)}, u32[]{:S(2)}) collective-permute-start(bf16[128,1024]{1,0:T(8,128)(2,1)S(1)} %shard_map.51.rows_ref.refs_2_), channel_id=1, source_target_pairs={{0,128},{16,144},{32,160},{48,176},{64,192},{80,208},{96,224},{112... | collective-permute-start | bytes 786440 | tf_op jit(solution)/shard_map/ppermute | solution.py:279
  40.8 1.9 %collective-permute-start.2 = (bf16[128,1024]{1,0:T(8,128)(2,1)S(1)}, bf16[128,1024]{1,0:T(8,128)(2,1)S(1)}, u32[]{:S(2)}, u32[]{:S(2)}) collective-permute-start(bf16[128,1024]{1,0:T(8,128)(2,1)S(1)} %shard_map.51.rows_ref.refs_2_), channel_id=1, source_target_pairs={{0,16},{16,0},{32,48},{48,32},{64,80},{80,64},{96,112},{112,96},{1... | collective-permute-start | bytes 786440 | tf_op jit(solution)/shard_map/ppermute | solution.py:279
  42.7 4.1 %collective-permute-start.4 = (bf16[128,1024]{1,0:T(8,128)(2,1)S(1)}, bf16[128,1024]{1,0:T(8,128)(2,1)S(1)}, u32[]{:S(2)}, u32[]{:S(2)}) collective-permute-start(bf16[128,1024]{1,0:T(8,128)(2,1)S(1)} %shard_map.51.rows_ref.refs_2_), channel_id=1, source_target_pairs={{0,144},{16,128},{32,176},{48,160},{64,208},{80,192},{96,240},{112... | collective-permute-start | bytes 786440 | tf_op jit(solution)/shard_map/ppermute | solution.py:279
  46.8 2.4 %convolution_convert_fusion = bf16[1024,1024]{1,0:T(8,128)(2,1)S(1)} fusion(bf16[1024,1024]{1,0:T(8,128)(2,1)S(1)} %copy-done, bf16[1024,1024]{1,0:T(8,128)(2,1)S(1)} %copy-done.1), kind=kOutput, calls=%fused_computation | convolution fusion | flops 2148532224 | bytes 6291456 | tf_op jit(solution)/shard_map/dot_general | solution.py:284
  49.3 1.3 %shard_map.52 = (bf16[8,16,1024]{2,1,0:T(8,128)(2,1)}, bf16[8,16,1024]{2,1,0:T(8,128)(2,1)}, bf16[8,16,1024]{2,1,0:T(8,128)(2,1)}, bf16[8,16,1024]{2,1,0:T(8,128)(2,1)}) custom-call(bf16[64,16,1024]{2,1,0:T(8,128)(2,1)S(1)} %bitcast.13), custom_call_target="tpu_custom_call" | custom-call | tf_op jit(solution)/shard_map/pallas_call | solution.py:94
  50.6 3.2 %collective-permute-start.6 = (bf16[8,16,1024]{2,1,0:T(8,128)(2,1)}, bf16[8,16,1024]{2,1,0:T(8,128)(2,1)S(1)}, u32[]{:S(2)}, u32[]{:S(2)}) collective-permute-start(bf16[8,16,1024]{2,1,0:T(8,128)(2,1)} %get-tuple-element.12), channel_id=1, source_target_pairs={{0,128},{16,144},{32,160},{48,176},{64,192},{80,208},{96,224},{112... | collective-permute-start | bytes 786440 | tf_op jit(solution)/shard_map/ppermute | solution.py:279
  53.8 1.9 %collective-permute-start.7 = (bf16[8,16,1024]{2,1,0:T(8,128)(2,1)}, bf16[8,16,1024]{2,1,0:T(8,128)(2,1)S(1)}, u32[]{:S(2)}, u32[]{:S(2)}) collective-permute-start(bf16[8,16,1024]{2,1,0:T(8,128)(2,1)} %get-tuple-element.13), channel_id=1, source_target_pairs={{0,16},{16,0},{32,48},{48,32},{64,80},{80,64},{96,112},{112,96},{1... | collective-permute-start | bytes 786440 | tf_op jit(solution)/shard_map/ppermute | solution.py:279
  55.7 4.1 %collective-permute-start.8 = (bf16[8,16,1024]{2,1,0:T(8,128)(2,1)}, bf16[8,16,1024]{2,1,0:T(8,128)(2,1)S(1)}, u32[]{:S(2)}, u32[]{:S(2)}) collective-permute-start(bf16[8,16,1024]{2,1,0:T(8,128)(2,1)} %get-tuple-element.14), channel_id=1, source_target_pairs={{0,144},{16,128},{32,176},{48,160},{64,208},{80,192},{96,240},{112... | collective-permute-start | bytes 786440 | tf_op jit(solution)/shard_map/ppermute | solution.py:279
  59.8 1.1 moment.5
  60.9 3.2 %collective-permute-start.1 = (bf16[128,1024]{1,0:T(8,128)(2,1)S(1)}, bf16[128,1024]{1,0:T(8,128)(2,1)S(1)}, u32[]{:S(2)}, u32[]{:S(2)}) collective-permute-start(bf16[128,1024]{1,0:T(8,128)(2,1)S(1)} %moment.5), channel_id=1, source_target_pairs={{0,128},{16,144},{32,160},{48,176},{64,192},{80,208},{96,224},{112... | collective-permute-start | bytes 786440 | tf_op jit(solution)/shard_map/ppermute | solution.py:279
  64.2 1.1 moment.6
  65.3 1.9 %collective-permute-start.3 = (bf16[128,1024]{1,0:T(8,128)(2,1)S(1)}, bf16[128,1024]{1,0:T(8,128)(2,1)S(1)}, u32[]{:S(2)}, u32[]{:S(2)}) collective-permute-start(bf16[128,1024]{1,0:T(8,128)(2,1)S(1)} %moment.6), channel_id=1, source_target_pairs={{0,16},{16,0},{32,48},{48,32},{64,80},{80,64},{96,112},{112,96},{1... | collective-permute-start | bytes 786440 | tf_op jit(solution)/shard_map/ppermute | solution.py:279
  67.2 1.1 moment.7
  68.4 4.1 %collective-permute-start.5 = (bf16[128,1024]{1,0:T(8,128)(2,1)S(1)}, bf16[128,1024]{1,0:T(8,128)(2,1)S(1)}, u32[]{:S(2)}, u32[]{:S(2)}) collective-permute-start(bf16[128,1024]{1,0:T(8,128)(2,1)S(1)} %moment.7), channel_id=1, source_target_pairs={{0,144},{16,128},{32,176},{48,160},{64,208},{80,192},{96,240},{112... | collective-permute-start | bytes 786440 | tf_op jit(solution)/shard_map/ppermute | solution.py:279
  72.5 1.1 moment.4
  73.7 0.2 collective-permute-done.1
  73.8 1.4 %collective-permute-done.3 = bf16[128,1024]{1,0:T(8,128)(2,1)S(1)} collective-permute-done((bf16[128,1024]{1,0:T(8,128)(2,1)S(1)}, bf16[128,1024]{1,0:T(8,128)(2,1)S(1)}, u32[]{:S(2)}, u32[]{:S(2)}) %collective-permute-start.3) | collective-permute-done | bytes 262176 | tf_op jit(solution)/shard_map/ppermute | solution.py:279
  75.3 3.1 %collective-permute-done.5 = bf16[128,1024]{1,0:T(8,128)(2,1)S(1)} collective-permute-done((bf16[128,1024]{1,0:T(8,128)(2,1)S(1)}, bf16[128,1024]{1,0:T(8,128)(2,1)S(1)}, u32[]{:S(2)}, u32[]{:S(2)}) %collective-permute-start.5) | collective-permute-done | bytes 262176 | tf_op jit(solution)/shard_map/ppermute | solution.py:279
  78.4 2.2 %shard_map.53 = bf16[8,32,1024]{2,1,0:T(8,128)(2,1)} custom-call(bf16[8,16,1024]{2,1,0:T(8,128)(2,1)S(1)} %bitcast.14, bf16[8,16,1024]{2,1,0:T(8,128)(2,1)S(1)} %bitcast.15, bf16[8,16,1024]{2,1,0:T(8,128)(2,1)S(1)} %bitcast.16, bf16[8,16,1024]{2,1,0:T(8,128)(2,1)S(1)} %bitcast.17, bf16[8,16,1024]{2,1,0:T(8,128)(2,1)} %get-tuple-element.11.refs_4_, ...), custom_call_target="tpu_custom_call" | custom-call | tf_op jit(solution)/shard_map/pallas_call | solution.py:94
  80.6 8.0 %all-to-all-start.1 = ((bf16[8,32,1024]{2,1,0:T(8,128)(2,1)}), bf16[8,32,1024]{2,1,0:T(8,128)(2,1)S(1)}, u32[]{:S(2)}, u32[]{:S(2)}) async-start(bf16[8,32,1024]{2,1,0:T(8,128)(2,1)} %shard_map.53), calls=%async_computation.1 | async-start | bytes 1048576 | tf_op jit(solution)/shard_map/all_to_all | solution.py:67
  88.6 8.6 %collective-permute-start.10 = (bf16[128,1024]{1,0:T(8,128)(2,1)S(1)}, bf16[128,1024]{1,0:T(8,128)(2,1)S(1)}, u32[]{:S(2)}, u32[]{:S(2)}) collective-permute-start(bf16[128,1024]{1,0:T(8,128)(2,1)S(1)} %shard_map.51.rows_ref.refs_2_), channel_id=1, source_target_pairs={{0,112},{16,32},{32,16},{48,64},{64,48},{80,96},{96,80},{112,0},{1... | collective-permute-start | bytes 786440 | tf_op jit(solution)/shard_map/ppermute | solution.py:279
  97.2 1.0 shard_map.54
  98.1 1.9 %collective-permute-start.11 = (bf16[128,1024]{1,0:T(8,128)(2,1)}, bf16[128,1024]{1,0:T(8,128)(2,1)S(1)}, u32[]{:S(2)}, u32[]{:S(2)}) collective-permute-start(bf16[128,1024]{1,0:T(8,128)(2,1)} %get-tuple-element.17), channel_id=1, source_target_pairs={{0,497},{16,417},{32,401},{48,449},{64,433},{80,481},{96,465},{112... | collective-permute-start | bytes 786440 | tf_op jit(solution)/shard_map/ppermute | solution.py:279
  100.1 4.6 %collective-permute-start.9 = (bf16[128,1024]{1,0:T(8,128)(2,1)}, bf16[128,1024]{1,0:T(8,128)(2,1)S(1)}, u32[]{:S(2)}, u32[]{:S(2)}) collective-permute-start(bf16[128,1024]{1,0:T(8,128)(2,1)} %get-tuple-element.16), channel_id=1, source_target_pairs={{0,385},{16,401},{32,417},{48,433},{64,449},{80,465},{96,481},{112... | collective-permute-start | bytes 786440 | tf_op jit(solution)/shard_map/ppermute | solution.py:279
  104.7 5.4 %collective-permute-done.10.refs_8_ = bf16[128,1024]{1,0:T(8,128)(2,1)S(1)} collective-permute-done((bf16[128,1024]{1,0:T(8,128)(2,1)S(1)}, bf16[128,1024]{1,0:T(8,128)(2,1)S(1)}, u32[]{:S(2)}, u32[]{:S(2)}) %collective-permute-start.10) | collective-permute-done | bytes 262176 | tf_op jit(solution)/shard_map/ppermute | solution.py:279
  110.1 5.7 %collective-permute-done.11.refs_9_ = bf16[128,1024]{1,0:T(8,128)(2,1)S(1)} collective-permute-done((bf16[128,1024]{1,0:T(8,128)(2,1)}, bf16[128,1024]{1,0:T(8,128)(2,1)S(1)}, u32[]{:S(2)}, u32[]{:S(2)}) %collective-permute-start.11) | collective-permute-done | bytes 262176 | tf_op jit(solution)/shard_map/ppermute | solution.py:279
  115.8 2.3 %collective-permute-done.9.refs_7_ = bf16[128,1024]{1,0:T(8,128)(2,1)S(1)} collective-permute-done((bf16[128,1024]{1,0:T(8,128)(2,1)}, bf16[128,1024]{1,0:T(8,128)(2,1)S(1)}, u32[]{:S(2)}, u32[]{:S(2)}) %collective-permute-start.9) | collective-permute-done | bytes 262176 | tf_op jit(solution)/shard_map/ppermute | solution.py:279
  118.1 0.7 copy-done.13
  118.8 3.3 %shard_map.55 = (f32[16,1024]{1,0:T(8,128)}, f32[16,1024]{1,0:T(8,128)}) custom-call(bf16[8,32,1024]{2,1,0:T(8,128)(2,1)S(1)} %all-to-all-done.1.refs_0_, f32[16,1024]{1,0:T(8,128)S(1)} %bitcast.19, bf16[128,1024]{1,0:T(8,128)(2,1)} %copy-done.2, bf16[128,1024]{1,0:T(8,128)(2,1)} %copy-done.3, bf16[128,1024]{1,0:T(8,128)(2,1)} %copy-done.4, ...), custom_call_target="tpu_custom_call" | custom-call | tf_op jit(solution)/shard_map/pallas_call | solution.py:94
  (34 shorter events, 0.1 us)
Async XLA Ops:
  0.6 46.2 %copy-start = (bf16[1024,1024]{1,0:T(8,128)(2,1)S(1)}, bf16[1024,1024]{1,0:T(8,128)(2,1)}, u32[]{:S(2)}) copy-start(bf16[1024,1024]{1,0:T(8,128)(2,1)} %param.4) | copy-start | bytes 6291460
  0.6 46.2 %copy-start.1 = (bf16[1024,1024]{1,0:T(8,128)(2,1)S(1)}, bf16[1024,1024]{1,0:T(8,128)(2,1)}, u32[]{:S(2)}) copy-start(bf16[1024,1024]{1,0:T(8,128)(2,1)} %x_ref.7) | copy-start | bytes 6291460
  0.7 1.0 copy-start.6
  37.6 51.0 %copy-start.2 = (bf16[128,1024]{1,0:T(8,128)(2,1)}, bf16[128,1024]{1,0:T(8,128)(2,1)S(1)}, u32[]{:S(2)}) copy-start(bf16[128,1024]{1,0:T(8,128)(2,1)S(1)} %shard_map.51.rows_ref.refs_2_) | copy-start | bytes 786436
  37.6 18.1 %collective-permute-start = (bf16[128,1024]{1,0:T(8,128)(2,1)S(1)}, bf16[128,1024]{1,0:T(8,128)(2,1)S(1)}, u32[]{:S(2)}, u32[]{:S(2)}) collective-permute-start(bf16[128,1024]{1,0:T(8,128)(2,1)S(1)} %shard_map.51.rows_ref.refs_2_), channel_id=1, source_target_pairs={{0,128},{16,144},{32,160},{48,176},{64,192},{80,208},{96,224},{112... | collective-permute-start | bytes 786440 | tf_op jit(solution)/shard_map/ppermute | solution.py:279
  40.8 20.1 %collective-permute-start.2 = (bf16[128,1024]{1,0:T(8,128)(2,1)S(1)}, bf16[128,1024]{1,0:T(8,128)(2,1)S(1)}, u32[]{:S(2)}, u32[]{:S(2)}) collective-permute-start(bf16[128,1024]{1,0:T(8,128)(2,1)S(1)} %shard_map.51.rows_ref.refs_2_), channel_id=1, source_target_pairs={{0,16},{16,0},{32,48},{48,32},{64,80},{80,64},{96,112},{112,96},{1... | collective-permute-start | bytes 786440 | tf_op jit(solution)/shard_map/ppermute | solution.py:279
  42.7 22.6 %collective-permute-start.4 = (bf16[128,1024]{1,0:T(8,128)(2,1)S(1)}, bf16[128,1024]{1,0:T(8,128)(2,1)S(1)}, u32[]{:S(2)}, u32[]{:S(2)}) collective-permute-start(bf16[128,1024]{1,0:T(8,128)(2,1)S(1)} %shard_map.51.rows_ref.refs_2_), channel_id=1, source_target_pairs={{0,144},{16,128},{32,176},{48,160},{64,208},{80,192},{96,240},{112... | collective-permute-start | bytes 786440 | tf_op jit(solution)/shard_map/ppermute | solution.py:279
  50.6 17.8 %collective-permute-start.6 = (bf16[8,16,1024]{2,1,0:T(8,128)(2,1)}, bf16[8,16,1024]{2,1,0:T(8,128)(2,1)S(1)}, u32[]{:S(2)}, u32[]{:S(2)}) collective-permute-start(bf16[8,16,1024]{2,1,0:T(8,128)(2,1)} %get-tuple-element.12), channel_id=1, source_target_pairs={{0,128},{16,144},{32,160},{48,176},{64,192},{80,208},{96,224},{112... | collective-permute-start | bytes 786440 | tf_op jit(solution)/shard_map/ppermute | solution.py:279
  53.8 19.8 %collective-permute-start.7 = (bf16[8,16,1024]{2,1,0:T(8,128)(2,1)}, bf16[8,16,1024]{2,1,0:T(8,128)(2,1)S(1)}, u32[]{:S(2)}, u32[]{:S(2)}) collective-permute-start(bf16[8,16,1024]{2,1,0:T(8,128)(2,1)} %get-tuple-element.13), channel_id=1, source_target_pairs={{0,16},{16,0},{32,48},{48,32},{64,80},{80,64},{96,112},{112,96},{1... | collective-permute-start | bytes 786440 | tf_op jit(solution)/shard_map/ppermute | solution.py:279
  55.7 9.6 %copy-start.3 = (bf16[128,1024]{1,0:T(8,128)(2,1)}, bf16[128,1024]{1,0:T(8,128)(2,1)S(1)}, u32[]{:S(2)}) copy-start(bf16[128,1024]{1,0:T(8,128)(2,1)S(1)} %collective-permute-done.rows_ref.refs_3_) | copy-start | bytes 786436
  55.7 17.9 %collective-permute-start.8 = (bf16[8,16,1024]{2,1,0:T(8,128)(2,1)}, bf16[8,16,1024]{2,1,0:T(8,128)(2,1)S(1)}, u32[]{:S(2)}, u32[]{:S(2)}) collective-permute-start(bf16[8,16,1024]{2,1,0:T(8,128)(2,1)} %get-tuple-element.14), channel_id=1, source_target_pairs={{0,144},{16,128},{32,176},{48,160},{64,208},{80,192},{96,240},{112... | collective-permute-start | bytes 786440 | tf_op jit(solution)/shard_map/ppermute | solution.py:279
  60.9 7.4 %copy-start.4 = (bf16[128,1024]{1,0:T(8,128)(2,1)}, bf16[128,1024]{1,0:T(8,128)(2,1)S(1)}, u32[]{:S(2)}) copy-start(bf16[128,1024]{1,0:T(8,128)(2,1)S(1)} %collective-permute-done.2.rows_ref.refs_4_) | copy-start | bytes 786436
  60.9 12.9 %collective-permute-start.1 = (bf16[128,1024]{1,0:T(8,128)(2,1)S(1)}, bf16[128,1024]{1,0:T(8,128)(2,1)S(1)}, u32[]{:S(2)}, u32[]{:S(2)}) collective-permute-start(bf16[128,1024]{1,0:T(8,128)(2,1)S(1)} %moment.5), channel_id=1, source_target_pairs={{0,128},{16,144},{32,160},{48,176},{64,192},{80,208},{96,224},{112... | collective-permute-start | bytes 786440 | tf_op jit(solution)/shard_map/ppermute | solution.py:279
  65.3 8.3 %copy-start.5 = (bf16[128,1024]{1,0:T(8,128)(2,1)}, bf16[128,1024]{1,0:T(8,128)(2,1)S(1)}, u32[]{:S(2)}) copy-start(bf16[128,1024]{1,0:T(8,128)(2,1)S(1)} %collective-permute-done.4.rows_ref.refs_5_) | copy-start | bytes 786436
  65.3 10.0 %collective-permute-start.3 = (bf16[128,1024]{1,0:T(8,128)(2,1)S(1)}, bf16[128,1024]{1,0:T(8,128)(2,1)S(1)}, u32[]{:S(2)}, u32[]{:S(2)}) collective-permute-start(bf16[128,1024]{1,0:T(8,128)(2,1)S(1)} %moment.6), channel_id=1, source_target_pairs={{0,16},{16,0},{32,48},{48,32},{64,80},{80,64},{96,112},{112,96},{1... | collective-permute-start | bytes 786440 | tf_op jit(solution)/shard_map/ppermute | solution.py:279
  68.4 10.0 %copy-start.8 = (bf16[8,16,1024]{2,1,0:T(8,128)(2,1)}, bf16[8,16,1024]{2,1,0:T(8,128)(2,1)S(1)}, u32[]{:S(2)}) copy-start(bf16[8,16,1024]{2,1,0:T(8,128)(2,1)S(1)} %collective-permute-done.6.refs_5_) | copy-start | bytes 786436
  68.4 10.0 %collective-permute-start.5 = (bf16[128,1024]{1,0:T(8,128)(2,1)S(1)}, bf16[128,1024]{1,0:T(8,128)(2,1)S(1)}, u32[]{:S(2)}, u32[]{:S(2)}) collective-permute-start(bf16[128,1024]{1,0:T(8,128)(2,1)S(1)} %moment.7), channel_id=1, source_target_pairs={{0,144},{16,128},{32,176},{48,160},{64,208},{80,192},{96,240},{112... | collective-permute-start | bytes 786440 | tf_op jit(solution)/shard_map/ppermute | solution.py:279
  73.6 4.8 %copy-start.9 = (bf16[8,16,1024]{2,1,0:T(8,128)(2,1)}, bf16[8,16,1024]{2,1,0:T(8,128)(2,1)S(1)}, u32[]{:S(2)}) copy-start(bf16[8,16,1024]{2,1,0:T(8,128)(2,1)S(1)} %collective-permute-done.7.refs_6_) | copy-start | bytes 786436
  73.6 4.8 %copy-start.10 = (bf16[8,16,1024]{2,1,0:T(8,128)(2,1)}, bf16[8,16,1024]{2,1,0:T(8,128)(2,1)S(1)}, u32[]{:S(2)}) copy-start(bf16[8,16,1024]{2,1,0:T(8,128)(2,1)S(1)} %collective-permute-done.8.refs_7_) | copy-start | bytes 786436
  78.4 40.4 %copy-start.7 = (f32[1024,16]{0,1:T(8,128)S(1)}, f32[1024,16]{0,1:T(8,128)}, u32[]{:S(2)}) copy-start(f32[1024,16]{0,1:T(8,128)} %param.5) | copy-start | bytes 196612
  80.6 37.5 %all-to-all-start.1 = ((bf16[8,32,1024]{2,1,0:T(8,128)(2,1)}), bf16[8,32,1024]{2,1,0:T(8,128)(2,1)S(1)}, u32[]{:S(2)}, u32[]{:S(2)}) async-start(bf16[8,32,1024]{2,1,0:T(8,128)(2,1)} %shard_map.53), calls=%async_computation.1 | async-start | bytes 1048576 | tf_op jit(solution)/shard_map/all_to_all | solution.py:67
  88.6 21.5 %collective-permute-start.10 = (bf16[128,1024]{1,0:T(8,128)(2,1)S(1)}, bf16[128,1024]{1,0:T(8,128)(2,1)S(1)}, u32[]{:S(2)}, u32[]{:S(2)}) collective-permute-start(bf16[128,1024]{1,0:T(8,128)(2,1)S(1)} %shard_map.51.rows_ref.refs_2_), channel_id=1, source_target_pairs={{0,112},{16,32},{32,16},{48,64},{64,48},{80,96},{96,80},{112,0},{1... | collective-permute-start | bytes 786440 | tf_op jit(solution)/shard_map/ppermute | solution.py:279
  98.1 17.6 %collective-permute-start.11 = (bf16[128,1024]{1,0:T(8,128)(2,1)}, bf16[128,1024]{1,0:T(8,128)(2,1)S(1)}, u32[]{:S(2)}, u32[]{:S(2)}) collective-permute-start(bf16[128,1024]{1,0:T(8,128)(2,1)} %get-tuple-element.17), channel_id=1, source_target_pairs={{0,497},{16,417},{32,401},{48,449},{64,433},{80,481},{96,465},{112... | collective-permute-start | bytes 786440 | tf_op jit(solution)/shard_map/ppermute | solution.py:279
  100.1 18.0 %collective-permute-start.9 = (bf16[128,1024]{1,0:T(8,128)(2,1)}, bf16[128,1024]{1,0:T(8,128)(2,1)S(1)}, u32[]{:S(2)}, u32[]{:S(2)}) collective-permute-start(bf16[128,1024]{1,0:T(8,128)(2,1)} %get-tuple-element.16), channel_id=1, source_target_pairs={{0,385},{16,401},{32,417},{48,433},{64,449},{80,465},{96,481},{112... | collective-permute-start | bytes 786440 | tf_op jit(solution)/shard_map/ppermute | solution.py:279
  110.1 5.7 %copy-start.11 = (bf16[128,1024]{1,0:T(8,128)(2,1)}, bf16[128,1024]{1,0:T(8,128)(2,1)S(1)}, u32[]{:S(2)}) copy-start(bf16[128,1024]{1,0:T(8,128)(2,1)S(1)} %collective-permute-done.10.refs_8_) | copy-start | bytes 786436
  115.8 2.4 %copy-start.12 = (bf16[128,1024]{1,0:T(8,128)(2,1)}, bf16[128,1024]{1,0:T(8,128)(2,1)S(1)}, u32[]{:S(2)}) copy-start(bf16[128,1024]{1,0:T(8,128)(2,1)S(1)} %collective-permute-done.11.refs_9_) | copy-start | bytes 786436
  118.1 0.7 copy-start.13

commit v5 on v4

v5 whole, which is shorter than its diff:
```python
import functools

import jax
import jax.numpy as jnp
from jax import lax
from jax.experimental import pallas as pl
from jax.experimental.pallas import tpu as pltpu
from jax.sharding import Mesh
from jax.sharding import PartitionSpec as P


SEQ = ("seq_0", "seq_1")
SEQ_GRP = ("seq_0", "seq_1", "grp")
PLANES = ("seq_0", "seq_1", "blk", "grp")


damping = 0.25
step_size = 0.4

f32, bf16 = jnp.float32, jnp.bfloat16
VMEM_LIMIT = 16 * 1024 * 1024
ROWS_ROWS = (((1,), (1,)), ((), ()))
TOKENS_FIRST = (((0,), (0,)), ((), ()))

BLOCKS = 8


def device(z, y, blk):
    core = blk % 2
    z, y = (z - core) % 8, (y - core) % 8
    return ((z % 4 * 8 + y) * BLOCKS + blk) * 2 + z // 4


FAR_GROUPS = [
    [
        device(4 * (h ^ (yh & 1)) + 2 * zh + b, 2 * yh + a, blk)
        for yh in range(4)
        for zh in range(2)
    ]
    for blk in range(BLOCKS)
    for h in range(2)
    for a in range(2)
    for b in range(2)
]


def moves(step_z, step_y):
    return [
        (device(z, y, blk), device(step_z(z), step_y(y), blk))
        for z in range(8)
        for y in range(8)
        for blk in range(BLOCKS)
    ]


def stay(at):
    return at


def inner(at):
    return at ^ 1


def outer(at):
    return (at - 1) % 8 if at % 2 == 0 else (at + 1) % 8


INNER = {1: moves(inner, stay), 2: moves(stay, inner), 3: moves(inner, inner)}
ACROSS = moves(stay, outer)


def exchange(blocks, groups):
    return lax.all_to_all(
        blocks, PLANES, split_axis=0, concat_axis=0, tiled=True, axis_index_groups=groups
    )


def vmem():
    return pl.BlockSpec(memory_space=pltpu.VMEM)


def hbm():
    return pl.BlockSpec(memory_space=pltpu.HBM)


def run_copies(pairs, sems):
    copies = [pltpu.make_async_copy(*pair, sems.at[k]) for k, pair in enumerate(pairs)]
    for copy in copies:
        copy.start()
    return copies


def position():
    core = lax.axis_index("blk") & 1
    z = (lax.axis_index("grp") * 4 + lax.axis_index("seq_0") + core) & 7
    y = (lax.axis_index("seq_1") + core) & 7
    yh, zh, half = y >> 1, (z & 3) >> 1, z >> 2
    return core, y & 1, z & 1, yh, zh, half ^ (yh & 1)


def call(kernel, out_shape, in_specs, out_specs, *args, **more):
    return pl.pallas_call(
        kernel,
        out_shape=out_shape,
        in_specs=in_specs,
        out_specs=out_specs,
        compiler_params=pltpu.CompilerParams(vmem_limit_bytes=VMEM_LIMIT),
        **more,
    )(*args)


def spread_kernel(own_ref, out_ref, low, sems):
    low[...] = own_ref[...].astype(bf16)
    for copy in run_copies([(low, out_ref.at[k]) for k in range(out_ref.shape[0])], sems):
        copy.wait()


def spread(own, count):
    shape = pltpu.HBM((count,) + own.shape, bf16)
    scratch = [pltpu.VMEM(own.shape, bf16), pltpu.SemaphoreType.DMA((count,))]
    return call(spread_kernel, shape, [vmem()], hbm(), own, scratch_shapes=scratch)


def pick_kernel(rows_ref, *refs):
    out_refs, sems = refs[:4], refs[4]
    core, a, b, _, _, h = position()
    pairs = []
    for d, out_ref in enumerate(out_refs):
        for f in range(8):
            row, column = f >> 1, f & 1
            z = 4 * (h ^ (row & 1)) + 2 * column + (b ^ (d & 1))
            y = 2 * row + (a ^ (d >> 1))
            z, y = (z + 8 - core) & 7, (y + 8 - core) & 7
            there = ((z & 3) * 8 + y) * 2 + (z >> 2)
            pairs.append((rows_ref.at[there], out_ref.at[f]))
    for copy in run_copies(pairs, sems):
        copy.wait()


def pick(rows):
    shape = pltpu.HBM((8,) + rows.shape[1:], rows.dtype)
    scratch = [pltpu.SemaphoreType.DMA((32,))]
    return call(pick_kernel, [shape] * 4, [vmem()], [hbm()] * 4, rows, scratch_shapes=scratch)


def moment_kernel(rows_ref, x_ref, out_ref):
    x = x_ref[...]
    whitened = lax.dot_general(rows_ref[...], x, ROWS_ROWS, preferred_element_type=f32)
    out_ref[...] = jnp.dot(whitened.astype(bf16), x, preferred_element_type=f32).astype(bf16)


def moment_of(rows, x):
    return pl.pallas_call(
        moment_kernel,
        out_shape=jax.ShapeDtypeStruct(rows.shape, bf16),
        in_specs=[vmem()] * 2,
        out_specs=vmem(),
        compiler_params=pltpu.CompilerParams(vmem_limit_bytes=VMEM_LIMIT),
        cost_estimate=pl.CostEstimate(
            flops=4 * rows.size * x.shape[0], bytes_accessed=2 * x.size, transcendentals=0
        ),
        name="moment",
    )(rows, x)


def join_kernel(*refs):
    moments, gradients, out_ref, staged, sems = refs[:4], refs[4:8], refs[8], refs[9], refs[10]
    leaving = []
    for f in range(8):
        for first, parts in ((0, moments), (16, gradients)):
            total = parts[0][f].astype(f32)
            for part in parts[1:]:
                total = total + part[f].astype(f32)
            staged[f, first : first + 16] = total.astype(bf16)
        copy = pltpu.make_async_copy(staged.at[f], out_ref.at[f], sems.at[f])
        copy.start()
        leaving.append(copy)
    for copy in leaving:
        copy.wait()


def join(moments, gradients):
    width = gradients[0].shape[2]
    moments = [m.reshape(8, 16, width) for m in moments]
    shape = pltpu.HBM((8, 32, width), bf16)
    scratch = [pltpu.VMEM(shape.shape, bf16), pltpu.SemaphoreType.DMA((8,))]
    return call(
        join_kernel, shape, [vmem()] * 8, hbm(), *moments, *gradients, scratch_shapes=scratch
    )


def finish_kernel(tokens, *refs):
    sums_ref, own_ref, blocks = refs[0], refs[1], refs[2:4]
    new_ref, direction_ref, rows, sems = refs[4:]
    pairs = [(block, rows.at[pl.ds(k * 512, 512)]) for k, block in enumerate(blocks)]
    copies = run_copies(pairs, sems)
    _, _, _, yh, zh, _ = position()
    at = (2 * yh + zh) * 16
    own = own_ref[...]
    total = sums_ref[0].astype(f32)
    for k in range(1, 8):
        total = total + sums_ref[k].astype(f32)
    inner_rows = total[:16] / tokens + damping * own.astype(bf16).astype(f32)
    high = inner_rows.astype(bf16)
    low = (inner_rows - high.astype(f32)).astype(bf16)
    left = jnp.concatenate([high, low, total[16:].astype(bf16)], axis=0)
    for copy in copies:
        copy.wait()
    product = lax.dot_general(left, rows[...], ROWS_ROWS, preferred_element_type=f32)
    curve = product[:16] + product[16:32]
    column = lax.broadcasted_iota(jnp.int32, curve.shape, 1)
    row = lax.broadcasted_iota(jnp.int32, curve.shape, 0)
    curve = curve - (column == row + at).astype(f32)
    right = jnp.concatenate([curve.astype(bf16), product[32:].astype(bf16)], axis=0)
    result = jnp.dot(right, rows[...], preferred_element_type=f32)
    new_ref[...] = own - 0.5 * step_size * result[:16]
    direction_ref[...] = result[16:]


def finish(tokens, sums, own, blocks):
    blocks = [pltpu.with_memory_space_constraint(block, pltpu.HBM) for block in blocks]
    scratch = [
        pltpu.VMEM((2 * 512, own.shape[1]), bf16),
        pltpu.SemaphoreType.DMA((2,)),
    ]
    return call(
        functools.partial(finish_kernel, tokens),
        [jax.ShapeDtypeStruct(own.shape, f32)] * 2,
        [vmem()] * 2 + [hbm()] * 2,
        [vmem()] * 2,
        sums,
        own,
        *blocks,
        scratch_shapes=scratch,
    )


def on_device(activations, cotangent, factor):
    seq_count = lax.axis_size(SEQ)
    owned = factor.shape[1]
    width = factor.shape[0]
    total_tokens = activations.shape[0] * seq_count

    def turn(block, pairs):
        return lax.ppermute(block, PLANES, pairs)

    own = factor.T
    mine = exchange(spread(own, 8), FAR_GROUPS).reshape(8 * owned, width)

    gradient_part = lax.dot_general(
        cotangent, activations, TOKENS_FIRST, preferred_element_type=f32
    ).astype(bf16)
    parts = pick(gradient_part.reshape(2 * seq_count, owned, width))
    gradients = [parts[0]]
    for d in (1, 2, 3):
        gradients.append(turn(parts[d], INNER[d]))

    near = [mine]
    for d in (1, 2, 3):
        near.append(turn(mine, INNER[d]))
    moments = [moment_of(mine, activations)]
    for d in (1, 2, 3):
        moment = moment_of(near[d], activations)
        moments.append(turn(moment, INNER[d]))
    near = jnp.concatenate(near, axis=0)
    far = turn(near, ACROSS)
    joined = join(moments, gradients)
    sums = exchange(joined, FAR_GROUPS)

    new_factor, direction = finish(total_tokens, sums, own, [near, far])
    return (new_factor.T, direction.T)


def solution(mesh):
    torus = Mesh(
        mesh.devices.reshape(4, 8, mesh.shape["blk"], mesh.shape["grp"]),
        ("seq_0", "seq_1", "blk", "grp"),
    )
    return jax.shard_map(
        on_device,
        mesh=torus,
        in_specs=(P(SEQ, "blk"), P(SEQ, None), P("blk", SEQ_GRP)),
        out_specs=(P("blk", SEQ_GRP), P("blk", SEQ_GRP)),
        check_vma=False,
    )
```

time: 124 us -> 106 us (0.85)
  starting transfers between devices: 50.7 us -> 38.4 us
  blocking collectives: 34.9 us -> 27.9 us
  Pallas kernels: 13.2 us -> 10.8 us
  waiting for transfers between devices: 18.2 us -> 20.4 us
  matrix products: 2.41 us -> 3.98 us
    all_to_all x1, waiting for transfers between devices: 0.01 us -> 12.9 us  [exchange(): lax.all_to_all(blocks, PLANES, split_axis=0, concat_axis=0, tiled=True, a...]
    ppermute x12 -> x10, starting transfers between devices: 42.7 us -> 30.8 us  [turn(): return lax.ppermute(block, PLANES, pairs)]
    ppermute x12 -> x10, waiting for transfers between devices: 18.2 us -> 7.42 us  [turn(): return lax.ppermute(block, PLANES, pairs)]
    all_to_all x1, blocking collectives: 34.9 us -> 27.9 us  [exchange(): lax.all_to_all(blocks, PLANES, split_axis=0, concat_axis=0, tiled=True, a...]
    pallas_call x6 -> x4, Pallas kernels: 8.72 us -> 6.36 us  [call(): pl.pallas_call(kernel, out_shape=out_shape, in_specs=in_specs, out_specs=...]
    dot_general x1, matrix products: 2.41 us -> 3.98 us  [on_device(): lax.dot_general(cotangent, activations, TOKENS_FIRST, preferred_element_t...]
  transfers between devices with their start and end apart: 13 -> 11, of which waited for: 6 -> 2; matrix products, arithmetic and copies ran while one was open for 2% -> 5% of each run, Pallas kernels for 5% -> 6%
where the time goes in v5:
time: 106 us; the launch traced here: 104 us
  starting transfers between devices  38.4 us (36%)
  blocking collectives  27.9 us (26%)
  waiting for transfers between devices  20.4 us (19%)
  Pallas kernels  10.8 us (10%)
  matrix products  3.98 us (4%)
    ppermute x10, starting transfers between devices, turn(): return lax.ppermute(block, PLANES, pairs)  30.8 us
    all_to_all x1, blocking collectives, exchange(): lax.all_to_all(blocks, PLANES, split_axis=0, concat_axis=0, tiled=True, a...  27.9 us
    all_to_all x1, waiting for transfers between devices, exchange(): lax.all_to_all(blocks, PLANES, split_axis=0, concat_axis=0, tiled=True, a...  12.9 us
    all_to_all x1, starting transfers between devices, exchange(): lax.all_to_all(blocks, PLANES, split_axis=0, concat_axis=0, tiled=True, a...  7.58 us
    ppermute x10, waiting for transfers between devices, turn(): return lax.ppermute(block, PLANES, pairs)  7.42 us
    pallas_call x4, Pallas kernels, call(): pl.pallas_call(kernel, out_shape=out_shape, in_specs=in_specs, out_specs=...  6.36 us
    pallas_call x4, Pallas kernels, moment_of(): pl.pallas_call(moment_kernel, out_shape=jax.ShapeDtypeStruct(rows.shape,...  4.46 us
    dot_general x1, matrix products, on_device(): lax.dot_general(cotangent, activations, TOKENS_FIRST, preferred_element_t...  3.98 us
  transfers between devices with their start and end apart: 11, of which 2 were waited for; matrix products, arithmetic and copies ran while one was open for 5% of the time, Pallas kernels for 6%

profile of v5, /device:TPU:6, one launch (start us, length us, event | category | flops | bytes accessed | tf_op | source)
XLA Modules:
  0.0 104.5 jit_solution(14497891788508395454)
XLA Ops:
  0.6 0.0 copy-start
  0.6 0.0 copy-start.3
  0.7 1.0 copy-done.3
  1.6 0.8 shard_map.50
  2.4 27.9 %all_to_all.10 = bf16[8,16,1024]{2,1,0:T(8,128)(2,1)S(1)} all-to-all(bf16[8,16,1024]{2,1,0:T(8,128)(2,1)} %shard_map.50), channel_id=1, replica_groups={{0,256,33,289,64,320,97,353},{128,384,161,417,192,448,225,481},{16,272,..., dimensions={0} | all-to-all | bytes 524288 | tf_op jit(solution)/shard_map/all_to_all | solution.py:73
  30.4 2.9 %collective-permute-start = (bf16[128,1024]{1,0:T(8,128)(2,1)S(1)}, bf16[128,1024]{1,0:T(8,128)(2,1)S(1)}, u32[]{:S(2)}, u32[]{:S(2)}) collective-permute-start(bf16[128,1024]{1,0:T(8,128)(2,1)S(1)} %bitcast.11), channel_id=1, source_target_pairs={{0,128},{499,114},{4,132},{503,118},{8,136},{507,122},{12,140},{51... | collective-permute-start | bytes 786440 | tf_op jit(solution)/shard_map/ppermute | solution.py:245
  33.3 2.4 %collective-permute-start.2 = (bf16[128,1024]{1,0:T(8,128)(2,1)S(1)}, bf16[128,1024]{1,0:T(8,128)(2,1)S(1)}, u32[]{:S(2)}, u32[]{:S(2)}) collective-permute-start(bf16[128,1024]{1,0:T(8,128)(2,1)S(1)} %bitcast.12), channel_id=1, source_target_pairs={{0,16},{499,387},{4,20},{503,391},{8,24},{507,395},{12,28},{511,39... | collective-permute-start | bytes 786440 | tf_op jit(solution)/shard_map/ppermute | solution.py:245
  35.7 3.9 %collective-permute-start.4 = (bf16[128,1024]{1,0:T(8,128)(2,1)S(1)}, bf16[128,1024]{1,0:T(8,128)(2,1)S(1)}, u32[]{:S(2)}, u32[]{:S(2)}) collective-permute-start(bf16[128,1024]{1,0:T(8,128)(2,1)S(1)} %bitcast.13), channel_id=1, source_target_pairs={{0,144},{499,2},{4,148},{503,6},{8,152},{507,10},{12,156},{511,14}... | collective-permute-start | bytes 786440 | tf_op jit(solution)/shard_map/ppermute | solution.py:245
  39.6 4.0 %convolution_convert_fusion = bf16[1024,1024]{1,0:T(8,128)(2,1)S(1)} fusion(bf16[1024,1024]{1,0:T(8,128)(2,1)S(1)} %copy-done, bf16[1024,1024]{1,0:T(8,128)(2,1)} %x_ref.7), kind=kOutput, calls=%fused_computation | convolution fusion | flops 2148532224 | bytes 6291456 | tf_op jit(solution)/shard_map/dot_general | solution.py:250
  43.6 0.0 copy-start.1
  43.6 1.3 %shard_map.51 = (bf16[8,16,1024]{2,1,0:T(8,128)(2,1)}, bf16[8,16,1024]{2,1,0:T(8,128)(2,1)}, bf16[8,16,1024]{2,1,0:T(8,128)(2,1)}, bf16[8,16,1024]{2,1,0:T(8,128)(2,1)}) custom-call(bf16[64,16,1024]{2,1,0:T(8,128)(2,1)S(1)} %bitcast.16), custom_call_target="tpu_custom_call" | custom-call | tf_op jit(solution)/shard_map/pallas_call | solution.py:102
  44.9 2.9 %collective-permute-start.6 = (bf16[8,16,1024]{2,1,0:T(8,128)(2,1)}, bf16[8,16,1024]{2,1,0:T(8,128)(2,1)S(1)}, u32[]{:S(2)}, u32[]{:S(2)}) collective-permute-start(bf16[8,16,1024]{2,1,0:T(8,128)(2,1)} %get-tuple-element.9), channel_id=1, source_target_pairs={{0,128},{499,114},{4,132},{503,118},{8,136},{507,122},{12,140},{51... | collective-permute-start | bytes 786440 | tf_op jit(solution)/shard_map/ppermute | solution.py:245
  47.8 2.4 %collective-permute-start.7 = (bf16[8,16,1024]{2,1,0:T(8,128)(2,1)}, bf16[8,16,1024]{2,1,0:T(8,128)(2,1)S(1)}, u32[]{:S(2)}, u32[]{:S(2)}) collective-permute-start(bf16[8,16,1024]{2,1,0:T(8,128)(2,1)} %get-tuple-element.10), channel_id=1, source_target_pairs={{0,16},{499,387},{4,20},{503,391},{8,24},{507,395},{12,28},{511,39... | collective-permute-start | bytes 786440 | tf_op jit(solution)/shard_map/ppermute | solution.py:245
  50.3 0.0 collective-permute-done.rows_ref
  50.3 3.9 %collective-permute-start.8 = (bf16[8,16,1024]{2,1,0:T(8,128)(2,1)}, bf16[8,16,1024]{2,1,0:T(8,128)(2,1)S(1)}, u32[]{:S(2)}, u32[]{:S(2)}) collective-permute-start(bf16[8,16,1024]{2,1,0:T(8,128)(2,1)} %get-tuple-element.11), channel_id=1, source_target_pairs={{0,144},{499,2},{4,148},{503,6},{8,152},{507,10},{12,156},{511,14}... | collective-permute-start | bytes 786440 | tf_op jit(solution)/shard_map/ppermute | solution.py:245
  54.2 1.1 %moment.5 = bf16[128,1024]{1,0:T(8,128)(2,1)S(1)} custom-call(bf16[128,1024]{1,0:T(8,128)(2,1)S(1)} %collective-permute-done.rows_ref, bf16[1024,1024]{1,0:T(8,128)(2,1)S(1)} %copy-done.1), custom_call_target="tpu_custom_call" | custom-call | flops 536870912 | bytes 2097152 | tf_op jit(solution)/shard_map/moment/pallas_call | solution.py:153
  55.3 0.0 collective-permute-done.2.rows_ref
  55.3 2.9 %collective-permute-start.1 = (bf16[128,1024]{1,0:T(8,128)(2,1)S(1)}, bf16[128,1024]{1,0:T(8,128)(2,1)S(1)}, u32[]{:S(2)}, u32[]{:S(2)}) collective-permute-start(bf16[128,1024]{1,0:T(8,128)(2,1)S(1)} %moment.5), channel_id=1, source_target_pairs={{0,128},{499,114},{4,132},{503,118},{8,136},{507,122},{12,140},{51... | collective-permute-start | bytes 786440 | tf_op jit(solution)/shard_map/ppermute | solution.py:245
  58.2 1.1 %moment.6 = bf16[128,1024]{1,0:T(8,128)(2,1)S(1)} custom-call(bf16[128,1024]{1,0:T(8,128)(2,1)S(1)} %collective-permute-done.2.rows_ref, bf16[1024,1024]{1,0:T(8,128)(2,1)S(1)} %copy-done.1), custom_call_target="tpu_custom_call" | custom-call | flops 536870912 | bytes 2097152 | tf_op jit(solution)/shard_map/moment/pallas_call | solution.py:153
  59.4 2.4 %collective-permute-start.3 = (bf16[128,1024]{1,0:T(8,128)(2,1)S(1)}, bf16[128,1024]{1,0:T(8,128)(2,1)S(1)}, u32[]{:S(2)}, u32[]{:S(2)}) collective-permute-start(bf16[128,1024]{1,0:T(8,128)(2,1)S(1)} %moment.6), channel_id=1, source_target_pairs={{0,16},{499,387},{4,20},{503,391},{8,24},{507,395},{12,28},{511,39... | collective-permute-start | bytes 786440 | tf_op jit(solution)/shard_map/ppermute | solution.py:245
  61.8 1.1 %moment.7 = bf16[128,1024]{1,0:T(8,128)(2,1)S(1)} custom-call(bf16[128,1024]{1,0:T(8,128)(2,1)S(1)} %collective-permute-done.4.rows_ref, bf16[1024,1024]{1,0:T(8,128)(2,1)S(1)} %copy-done.1), custom_call_target="tpu_custom_call" | custom-call | flops 536870912 | bytes 2097152 | tf_op jit(solution)/shard_map/moment/pallas_call | solution.py:153
  63.0 4.0 %collective-permute-start.5 = (bf16[128,1024]{1,0:T(8,128)(2,1)S(1)}, bf16[128,1024]{1,0:T(8,128)(2,1)S(1)}, u32[]{:S(2)}, u32[]{:S(2)}) collective-permute-start(bf16[128,1024]{1,0:T(8,128)(2,1)S(1)} %moment.7), channel_id=1, source_target_pairs={{0,144},{499,2},{4,148},{503,6},{8,152},{507,10},{12,156},{511,14}... | collective-permute-start | bytes 786440 | tf_op jit(solution)/shard_map/ppermute | solution.py:245
  67.0 1.1 %pad_maximum_fusion.refs_2_ = bf16[512,1024]{1,0:T(8,128)(2,1)} fusion(bf16[128,1024]{1,0:T(8,128)(2,1)S(1)} %collective-permute-done.4.rows_ref, bf16[128,1024]{1,0:T(8,128)(2,1)S(1)} %collective-permute-done.2.rows_ref, bf16[128,1024]{1,0:T(8,128)(2,1)S(1)} %collective-permute-done.rows_ref, bf16[128,1024]{1,0:T(8,128)(2,1)S(1)} %bitcast.14), kind=kLoop, calls=%fused_computation.1 | loop fusion | flops 4194304 | bytes 2097152 | tf_op jit(solution)/shard_map/concatenate | solution.py:265
  68.0 3.1 %collective-permute-start.9 = (bf16[512,1024]{1,0:T(8,128)(2,1)}, bf16[512,1024]{1,0:T(8,128)(2,1)}, u32[]{:S(2)}, u32[]{:S(2)}) collective-permute-start(bf16[512,1024]{1,0:T(8,128)(2,1)} %pad_maximum_fusion.refs_2_), channel_id=1, source_target_pairs={{0,112},{499,483},{4,116},{503,487},{8,120},{507,491},{12,124},{51... | collective-permute-start | bytes 3145736 | tf_op jit(solution)/shard_map/ppermute | solution.py:245
  71.1 1.1 %moment.4 = bf16[128,1024]{1,0:T(8,128)(2,1)S(1)} custom-call(bf16[128,1024]{1,0:T(8,128)(2,1)S(1)} %bitcast.15, bf16[1024,1024]{1,0:T(8,128)(2,1)S(1)} %copy-done.1), custom_call_target="tpu_custom_call" | custom-call | flops 536870912 | bytes 2097152 | tf_op jit(solution)/shard_map/moment/pallas_call | solution.py:153
  72.2 0.0 copy-start.4
  72.2 0.0 collective-permute-done.8.refs_7_
  72.3 1.0 shard_map.52
  73.3 7.6 %all-to-all-start.1 = ((bf16[8,32,1024]{2,1,0:T(8,128)(2,1)}), bf16[8,32,1024]{2,1,0:T(8,128)(2,1)S(1)}, u32[]{:S(2)}, u32[]{:S(2)}) async-start(bf16[8,32,1024]{2,1,0:T(8,128)(2,1)} %shard_map.52), calls=%async_computation.1 | async-start | bytes 1048576 | tf_op jit(solution)/shard_map/all_to_all | solution.py:73
  80.8 7.4 %collective-permute-done.9.refs_3_ = bf16[512,1024]{1,0:T(8,128)(2,1)} collective-permute-done((bf16[512,1024]{1,0:T(8,128)(2,1)}, bf16[512,1024]{1,0:T(8,128)(2,1)}, u32[]{:S(2)}, u32[]{:S(2)}) %collective-permute-start.9) | collective-permute-done | bytes 1048608 | tf_op jit(solution)/shard_map/ppermute | solution.py:245
  88.2 12.9 %all-to-all-done.1.refs_0_ = bf16[8,32,1024]{2,1,0:T(8,128)(2,1)S(1)} async-done(((bf16[8,32,1024]{2,1,0:T(8,128)(2,1)}), bf16[8,32,1024]{2,1,0:T(8,128)(2,1)S(1)}, u32[]{:S(2)}, u32[]{:S(2)}) %all-to-all-start.1) | async-done | bytes 524320 | tf_op jit(solution)/shard_map/all_to_all | solution.py:73
  101.2 3.3 %shard_map.53 = (f32[16,1024]{1,0:T(8,128)}, f32[16,1024]{1,0:T(8,128)}) custom-call(bf16[8,32,1024]{2,1,0:T(8,128)(2,1)S(1)} %all-to-all-done.1.refs_0_, f32[16,1024]{1,0:T(8,128)S(1)} %bitcast.22, bf16[512,1024]{1,0:T(8,128)(2,1)} %pad_maximum_fusion.refs_2_, bf16[512,1024]{1,0:T(8,128)(2,1)} %collective-permute-done.9.refs_3_), custom_call_target="tpu_custom_call" | custom-call | tf_op jit(solution)/shard_map/pallas_call | solution.py:102
  (11 shorter events, 0.0 us)
Async XLA Ops:
  0.6 39.0 %copy-start = (bf16[1024,1024]{1,0:T(8,128)(2,1)S(1)}, bf16[1024,1024]{1,0:T(8,128)(2,1)}, u32[]{:S(2)}) copy-start(bf16[1024,1024]{1,0:T(8,128)(2,1)} %param.4) | copy-start | bytes 6291460
  0.6 1.0 copy-start.3
  30.4 19.9 %collective-permute-start = (bf16[128,1024]{1,0:T(8,128)(2,1)S(1)}, bf16[128,1024]{1,0:T(8,128)(2,1)S(1)}, u32[]{:S(2)}, u32[]{:S(2)}) collective-permute-start(bf16[128,1024]{1,0:T(8,128)(2,1)S(1)} %bitcast.11), channel_id=1, source_target_pairs={{0,128},{499,114},{4,132},{503,118},{8,136},{507,122},{12,140},{51... | collective-permute-start | bytes 786440 | tf_op jit(solution)/shard_map/ppermute | solution.py:245
  33.3 22.0 %collective-permute-start.2 = (bf16[128,1024]{1,0:T(8,128)(2,1)S(1)}, bf16[128,1024]{1,0:T(8,128)(2,1)S(1)}, u32[]{:S(2)}, u32[]{:S(2)}) collective-permute-start(bf16[128,1024]{1,0:T(8,128)(2,1)S(1)} %bitcast.12), channel_id=1, source_target_pairs={{0,16},{499,387},{4,20},{503,391},{8,24},{507,395},{12,28},{511,39... | collective-permute-start | bytes 786440 | tf_op jit(solution)/shard_map/ppermute | solution.py:245
  35.7 23.7 %collective-permute-start.4 = (bf16[128,1024]{1,0:T(8,128)(2,1)S(1)}, bf16[128,1024]{1,0:T(8,128)(2,1)S(1)}, u32[]{:S(2)}, u32[]{:S(2)}) collective-permute-start(bf16[128,1024]{1,0:T(8,128)(2,1)S(1)} %bitcast.13), channel_id=1, source_target_pairs={{0,144},{499,2},{4,148},{503,6},{8,152},{507,10},{12,156},{511,14}... | collective-permute-start | bytes 786440 | tf_op jit(solution)/shard_map/ppermute | solution.py:245
  43.6 10.6 %copy-start.1 = (bf16[1024,1024]{1,0:T(8,128)(2,1)S(1)}, bf16[1024,1024]{1,0:T(8,128)(2,1)}, u32[]{:S(2)}) copy-start(bf16[1024,1024]{1,0:T(8,128)(2,1)} %x_ref.7) | copy-start | bytes 6291460
  44.9 18.0 %collective-permute-start.6 = (bf16[8,16,1024]{2,1,0:T(8,128)(2,1)}, bf16[8,16,1024]{2,1,0:T(8,128)(2,1)S(1)}, u32[]{:S(2)}, u32[]{:S(2)}) collective-permute-start(bf16[8,16,1024]{2,1,0:T(8,128)(2,1)} %get-tuple-element.9), channel_id=1, source_target_pairs={{0,128},{499,114},{4,132},{503,118},{8,136},{507,122},{12,140},{51... | collective-permute-start | bytes 786440 | tf_op jit(solution)/shard_map/ppermute | solution.py:245
  47.8 20.2 %collective-permute-start.7 = (bf16[8,16,1024]{2,1,0:T(8,128)(2,1)}, bf16[8,16,1024]{2,1,0:T(8,128)(2,1)S(1)}, u32[]{:S(2)}, u32[]{:S(2)}) collective-permute-start(bf16[8,16,1024]{2,1,0:T(8,128)(2,1)} %get-tuple-element.10), channel_id=1, source_target_pairs={{0,16},{499,387},{4,20},{503,391},{8,24},{507,395},{12,28},{511,39... | collective-permute-start | bytes 786440 | tf_op jit(solution)/shard_map/ppermute | solution.py:245
  50.3 21.9 %collective-permute-start.8 = (bf16[8,16,1024]{2,1,0:T(8,128)(2,1)}, bf16[8,16,1024]{2,1,0:T(8,128)(2,1)S(1)}, u32[]{:S(2)}, u32[]{:S(2)}) collective-permute-start(bf16[8,16,1024]{2,1,0:T(8,128)(2,1)} %get-tuple-element.11), channel_id=1, source_target_pairs={{0,144},{499,2},{4,148},{503,6},{8,152},{507,10},{12,156},{511,14}... | collective-permute-start | bytes 786440 | tf_op jit(solution)/shard_map/ppermute | solution.py:245
  55.3 16.9 %collective-permute-start.1 = (bf16[128,1024]{1,0:T(8,128)(2,1)S(1)}, bf16[128,1024]{1,0:T(8,128)(2,1)S(1)}, u32[]{:S(2)}, u32[]{:S(2)}) collective-permute-start(bf16[128,1024]{1,0:T(8,128)(2,1)S(1)} %moment.5), channel_id=1, source_target_pairs={{0,128},{499,114},{4,132},{503,118},{8,136},{507,122},{12,140},{51... | collective-permute-start | bytes 786440 | tf_op jit(solution)/shard_map/ppermute | solution.py:245
  59.4 12.9 %collective-permute-start.3 = (bf16[128,1024]{1,0:T(8,128)(2,1)S(1)}, bf16[128,1024]{1,0:T(8,128)(2,1)S(1)}, u32[]{:S(2)}, u32[]{:S(2)}) collective-permute-start(bf16[128,1024]{1,0:T(8,128)(2,1)S(1)} %moment.6), channel_id=1, source_target_pairs={{0,16},{499,387},{4,20},{503,391},{8,24},{507,395},{12,28},{511,39... | collective-permute-start | bytes 786440 | tf_op jit(solution)/shard_map/ppermute | solution.py:245
  62.9 9.3 %copy-start.2 = (bf16[8,16,1024]{2,1,0:T(8,128)(2,1)S(1)}, bf16[8,16,1024]{2,1,0:T(8,128)(2,1)}, u32[]{:S(2)}) copy-start(bf16[8,16,1024]{2,1,0:T(8,128)(2,1)} %get-tuple-element.8.refs_4_) | copy-start | bytes 786436
  63.0 9.3 %collective-permute-start.5 = (bf16[128,1024]{1,0:T(8,128)(2,1)S(1)}, bf16[128,1024]{1,0:T(8,128)(2,1)S(1)}, u32[]{:S(2)}, u32[]{:S(2)}) collective-permute-start(bf16[128,1024]{1,0:T(8,128)(2,1)S(1)} %moment.7), channel_id=1, source_target_pairs={{0,144},{499,2},{4,148},{503,6},{8,152},{507,10},{12,156},{511,14}... | collective-permute-start | bytes 786440 | tf_op jit(solution)/shard_map/ppermute | solution.py:245
  68.0 20.2 %collective-permute-start.9 = (bf16[512,1024]{1,0:T(8,128)(2,1)}, bf16[512,1024]{1,0:T(8,128)(2,1)}, u32[]{:S(2)}, u32[]{:S(2)}) collective-permute-start(bf16[512,1024]{1,0:T(8,128)(2,1)} %pad_maximum_fusion.refs_2_), channel_id=1, source_target_pairs={{0,112},{499,483},{4,116},{503,487},{8,120},{507,491},{12,124},{51... | collective-permute-start | bytes 3145736 | tf_op jit(solution)/shard_map/ppermute | solution.py:245
  72.2 29.0 %copy-start.4 = (f32[1024,16]{0,1:T(8,128)S(1)}, f32[1024,16]{0,1:T(8,128)}, u32[]{:S(2)}) copy-start(f32[1024,16]{0,1:T(8,128)} %param.5) | copy-start | bytes 196612
  73.3 27.9 %all-to-all-start.1 = ((bf16[8,32,1024]{2,1,0:T(8,128)(2,1)}), bf16[8,32,1024]{2,1,0:T(8,128)(2,1)S(1)}, u32[]{:S(2)}, u32[]{:S(2)}) async-start(bf16[8,32,1024]{2,1,0:T(8,128)(2,1)} %shard_map.52), calls=%async_computation.1 | async-start | bytes 1048576 | tf_op jit(solution)/shard_map/all_to_all | solution.py:73

commit v6 on v5

--- a/solution.py
+++ b/solution.py
@@ -41,6 +41,19 @@
     for h in range(2)
     for a in range(2)
     for b in range(2)
+]
+
+
+SQUARES = [
+    [
+        device(4 * (h ^ (yh & 1)) + 2 * zh + b, 2 * yh + a, blk)
+        for a in range(2)
+        for b in range(2)
+    ]
+    for blk in range(BLOCKS)
+    for h in range(2)
+    for yh in range(4)
+    for zh in range(2)
 ]
 
 
@@ -143,59 +156,82 @@
     return call(pick_kernel, [shape] * 4, [vmem()], [hbm()] * 4, rows, scratch_shapes=scratch)
 
 
-def moment_kernel(rows_ref, x_ref, out_ref):
+def moment_kernel(rows_ref, x_ref, out_ref, staged, sems):
     x = x_ref[...]
     whitened = lax.dot_general(rows_ref[...], x, ROWS_ROWS, preferred_element_type=f32)
-    out_ref[...] = jnp.dot(whitened.astype(bf16), x, preferred_element_type=f32).astype(bf16)
-
-
-def moment_of(rows, x):
-    return pl.pallas_call(
-        moment_kernel,
-        out_shape=jax.ShapeDtypeStruct(rows.shape, bf16),
-        in_specs=[vmem()] * 2,
-        out_specs=vmem(),
-        compiler_params=pltpu.CompilerParams(vmem_limit_bytes=VMEM_LIMIT),
-        cost_estimate=pl.CostEstimate(
-            flops=4 * rows.size * x.shape[0], bytes_accessed=2 * x.size, transcendentals=0
-        ),
-        name="moment",
-    )(rows, x)
-
-
-def join_kernel(*refs):
-    moments, gradients, out_ref, staged, sems = refs[:4], refs[4:8], refs[8], refs[9], refs[10]
+    whitened = whitened.astype(bf16)
     leaving = []
-    for f in range(8):
-        for first, parts in ((0, moments), (16, gradients)):
-            total = parts[0][f].astype(f32)
-            for part in parts[1:]:
-                total = total + part[f].astype(f32)
-            staged[f, first : first + 16] = total.astype(bf16)
-        copy = pltpu.make_async_copy(staged.at[f], out_ref.at[f], sems.at[f])
+    for k in range(2):
+        part = pl.ds(k * 256, 256)
+        moment = jnp.dot(whitened[k * 256 : k * 256 + 256], x, preferred_element_type=f32)
+        staged[part] = moment.astype(bf16)
+        copy = pltpu.make_async_copy(staged.at[part], out_ref.at[part], sems.at[k])
         copy.start()
         leaving.append(copy)
     for copy in leaving:
         copy.wait()
 
 
-def join(moments, gradients):
-    width = gradients[0].shape[2]
-    moments = [m.reshape(8, 16, width) for m in moments]
-    shape = pltpu.HBM((8, 32, width), bf16)
-    scratch = [pltpu.VMEM(shape.shape, bf16), pltpu.SemaphoreType.DMA((8,))]
-    return call(
-        join_kernel, shape, [vmem()] * 8, hbm(), *moments, *gradients, scratch_shapes=scratch
-    )
+def moment_of(rows, x):
+    scratch = [pltpu.VMEM(rows.shape, bf16), pltpu.SemaphoreType.DMA((2,))]
+    shape = pltpu.HBM(rows.shape, bf16)
+    return call(moment_kernel, shape, [vmem()] * 2, hbm(), rows, x, scratch_shapes=scratch)
+
+
+def presum_kernel(*refs):
+    parts, out_ref, staged, sem = refs[:4], refs[4], refs[5], refs[6]
+    for f in range(8):
+        total = parts[0][f].astype(f32)
+        for part in parts[1:]:
+            total = total + part[f].astype(f32)
+        staged[f] = total.astype(bf16)
+    copy = pltpu.make_async_copy(staged, out_ref, sem)
+    copy.start()
+    copy.wait()
+
+
+def presum(parts):
+    shape = pltpu.HBM(parts[0].shape, bf16)
+    scratch = [pltpu.VMEM(shape.shape, bf16), pltpu.SemaphoreType.DMA]
+    return call(presum_kernel, shape, [vmem()] * 4, hbm(), *parts, scratch_shapes=scratch)
+
+
+def join_kernel(moments_ref, gradient_ref, out_ref, staged, sem, sems):
+    arriving = pltpu.make_async_copy(gradient_ref, staged.at[:, pl.ds(16, 16)], sem)
+    arriving.start()
+    for f in range(8):
+        total = moments_ref[0, f].astype(f32)
+        for k in range(1, 4):
+            total = total + moments_ref[k, f].astype(f32)
+        staged[f, :16] = total.astype(bf16)
+    arriving.wait()
+    leaving = run_copies([(staged.at[f], out_ref.at[f]) for f in range(8)], sems)
+    for copy in leaving:
+        copy.wait()
+
+
+def join(moments, gradient):
+    gradient = pltpu.with_memory_space_constraint(gradient, pltpu.HBM)
+    shape = pltpu.HBM((8, 32, gradient.shape[2]), bf16)
+    scratch = [
+        pltpu.VMEM(shape.shape, bf16),
+        pltpu.SemaphoreType.DMA,
+        pltpu.SemaphoreType.DMA((8,)),
+    ]
+    specs = [vmem(), hbm()]
+    return call(join_kernel, shape, specs, hbm(), moments, gradient, scratch_shapes=scratch)
 
 
 def finish_kernel(tokens, *refs):
     sums_ref, own_ref, blocks = refs[0], refs[1], refs[2:4]
     new_ref, direction_ref, rows, sems = refs[4:]
-    pairs = [(block, rows.at[pl.ds(k * 512, 512)]) for k, block in enumerate(blocks)]
+    pairs = []
+    for k in range(4):
+        piece = blocks[k // 2].at[pl.ds(k % 2 * 256, 256)]
+        pairs.append((piece, rows.at[pl.ds(k * 256, 256)]))
     copies = run_copies(pairs, sems)
-    _, _, _, yh, zh, _ = position()
-    at = (2 * yh + zh) * 16
+    _, a, b, yh, zh, _ = position()
+    at = (2 * a + b) * 128 + (2 * yh + zh) * 16
     own = own_ref[...]
     total = sums_ref[0].astype(f32)
     for k in range(1, 8):
@@ -204,15 +240,18 @@
     high = inner_rows.astype(bf16)
     low = (inner_rows - high.astype(f32)).astype(bf16)
     left = jnp.concatenate([high, low, total[16:].astype(bf16)], axis=0)
-    for copy in copies:
-        copy.wait()
-    product = lax.dot_general(left, rows[...], ROWS_ROWS, preferred_element_type=f32)
-    curve = product[:16] + product[16:32]
-    column = lax.broadcasted_iota(jnp.int32, curve.shape, 1)
-    row = lax.broadcasted_iota(jnp.int32, curve.shape, 0)
-    curve = curve - (column == row + at).astype(f32)
-    right = jnp.concatenate([curve.astype(bf16), product[32:].astype(bf16)], axis=0)
-    result = jnp.dot(right, rows[...], preferred_element_type=f32)
+    result = jnp.zeros((32, own.shape[1]), f32)
+    for k, copy in enumerate(copies):
+        copy.wait()
+        part = rows[pl.ds(k * 256, 256)]
+        product = lax.dot_general(left, part, ROWS_ROWS, preferred_element_type=f32)
+        curve = product[:16] + product[16:32]
+        if k < 2:
+            column = lax.broadcasted_iota(jnp.int32, curve.shape, 1) + k * 256
+            row = lax.broadcasted_iota(jnp.int32, curve.shape, 0)
+            curve = curve - (column == row + at).astype(f32)
+        right = jnp.concatenate([curve.astype(bf16), product[32:].astype(bf16)], axis=0)
+        result = result + jnp.dot(right, part, preferred_element_type=f32)
     new_ref[...] = own - 0.5 * step_size * result[:16]
     direction_ref[...] = result[16:]
 
@@ -221,7 +260,7 @@
     blocks = [pltpu.with_memory_space_constraint(block, pltpu.HBM) for block in blocks]
     scratch = [
         pltpu.VMEM((2 * 512, own.shape[1]), bf16),
-        pltpu.SemaphoreType.DMA((2,)),
+        pltpu.SemaphoreType.DMA((4,)),
     ]
     return call(
         functools.partial(finish_kernel, tokens),
@@ -255,16 +294,13 @@
     for d in (1, 2, 3):
         gradients.append(turn(parts[d], INNER[d]))
 
-    near = [mine]
-    for d in (1, 2, 3):
-        near.append(turn(mine, INNER[d]))
-    moments = [moment_of(mine, activations)]
-    for d in (1, 2, 3):
-        moment = moment_of(near[d], activations)
-        moments.append(turn(moment, INNER[d]))
-    near = jnp.concatenate(near, axis=0)
+    square = jnp.broadcast_to(mine[None], (4, 8 * owned, width))
+    near = exchange(square, SQUARES).reshape(32 * owned, width)
+    moments = moment_of(near, activations).reshape(4, 8 * owned, width)
+    moments = exchange(moments, SQUARES).reshape(4, 8, owned, width)
     far = turn(near, ACROSS)
-    joined = join(moments, gradients)
+    gradient = presum(gradients)
+    joined = join(moments, gradient)
     sums = exchange(joined, FAR_GROUPS)
 
     new_factor, direction = finish(total_tokens, sums, own, [near, far])

time: 106 us -> 111 us (1.047)
  starting transfers between devices: 38.4 us -> 23.2 us
  blocking collectives: 27.9 us -> 40.5 us
  waiting for transfers between devices: 20.4 us -> 24.7 us
  Pallas kernels: 10.8 us -> 13.9 us
    ppermute x10 -> x4, starting transfers between devices: 30.8 us -> 13.2 us  [turn(): return lax.ppermute(block, PLANES, pairs)]
    all_to_all x1 -> x2, blocking collectives: 27.9 us -> 40.5 us  [exchange(): lax.all_to_all(blocks, PLANES, split_axis=0, concat_axis=0, tiled=True, a...]
    pallas_call x4 -> x6, Pallas kernels: 6.36 us -> 13.9 us  [call(): pl.pallas_call(kernel, out_shape=out_shape, in_specs=in_specs, out_specs=...]
    all_to_all x1 -> x2, waiting for transfers between devices: 12.9 us -> 19.1 us  [exchange(): lax.all_to_all(blocks, PLANES, split_axis=0, concat_axis=0, tiled=True, a...]
    pallas_call x4 -> x0, Pallas kernels: 4.46 us -> none  [moment_of(): pl.pallas_call(moment_kernel, out_shape=jax.ShapeDtypeStruct(rows.shape,...]
    all_to_all x1 -> x2, starting transfers between devices: 7.58 us -> 10 us  [exchange(): lax.all_to_all(blocks, PLANES, split_axis=0, concat_axis=0, tiled=True, a...]
    ppermute x10 -> x4, waiting for transfers between devices: 7.42 us -> 5.58 us  [turn(): return lax.ppermute(block, PLANES, pairs)]
  transfers between devices with their start and end apart: 11 -> 6, of which waited for: 2 -> 3; matrix products, arithmetic and copies ran while one was open for 5% -> 4% of each run, Pallas kernels for 6% -> 5%
where the time goes in v6:
time: 111 us; the launch traced here: 109 us
  blocking collectives  40.5 us (36%)
  waiting for transfers between devices  24.7 us (22%)
  starting transfers between devices  23.2 us (21%)
  Pallas kernels  13.9 us (13%)
  matrix products  3.98 us (4%)
  local copies, waits for them, and re-layouts  2.07 us (2%)
    all_to_all x2, blocking collectives, exchange(): lax.all_to_all(blocks, PLANES, split_axis=0, concat_axis=0, tiled=True, a...  40.5 us
    all_to_all x2, waiting for transfers between devices, exchange(): lax.all_to_all(blocks, PLANES, split_axis=0, concat_axis=0, tiled=True, a...  19.1 us
    pallas_call x6, Pallas kernels, call(): pl.pallas_call(kernel, out_shape=out_shape, in_specs=in_specs, out_specs=...  13.9 us
    ppermute x4, starting transfers between devices, turn(): return lax.ppermute(block, PLANES, pairs)  13.2 us
    all_to_all x2, starting transfers between devices, exchange(): lax.all_to_all(blocks, PLANES, split_axis=0, concat_axis=0, tiled=True, a...  10 us
    ppermute x4, waiting for transfers between devices, turn(): return lax.ppermute(block, PLANES, pairs)  5.58 us
    dot_general x1, matrix products, on_device(): lax.dot_general(cotangent, activations, TOKENS_FIRST, preferred_element_t...  3.98 us
  transfers between devices with their start and end apart: 6, of which 3 were waited for; matrix products, arithmetic and copies ran while one was open for 4% of the time, Pallas kernels for 5%

profile of v6, /device:TPU:6, one launch (start us, length us, event | category | flops | bytes accessed | tf_op | source)
XLA Modules:
  0.0 109.1 jit_solution(13958150032328435755)
XLA Ops:
  0.6 0.0 copy-start
  0.6 0.0 copy-start.4
  0.7 1.0 copy-done.4
  1.6 0.0 copy-start.2
  1.6 0.8 shard_map.50
  2.4 27.9 %all_to_all.20 = bf16[8,16,1024]{2,1,0:T(8,128)(2,1)S(1)} all-to-all(bf16[8,16,1024]{2,1,0:T(8,128)(2,1)} %shard_map.50), channel_id=1, replica_groups={{0,256,33,289,64,320,97,353},{128,384,161,417,192,448,225,481},{16,272,..., dimensions={0} | all-to-all | bytes 524288 | tf_op jit(solution)/shard_map/all_to_all | solution.py:86
  30.4 0.1 broadcast_in_dim.8
  30.5 12.5 %all_to_all.21 = bf16[4,128,1024]{2,1,0:T(8,128)(2,1)S(1)} all-to-all(bf16[4,128,1024]{2,1,0:T(8,128)(2,1)S(1)} %broadcast_in_dim.8), channel_id=1, replica_groups={{0,128,16,144},{256,384,272,400},{33,161,49,177},{289,417,305,433},{64,..., dimensions={0} | all-to-all | bytes 2097152 | tf_op jit(solution)/shard_map/all_to_all | solution.py:86
  43.0 0.0 copy-start.1
  43.0 0.0 copy-done.2
  43.0 3.2 %shard_map.51 = bf16[512,1024]{1,0:T(8,128)(2,1)} custom-call(bf16[512,1024]{1,0:T(8,128)(2,1)S(1)} %bitcast.10, bf16[1024,1024]{1,0:T(8,128)(2,1)S(1)} %copy-done.2), custom_call_target="tpu_custom_call" | custom-call | tf_op jit(solution)/shard_map/pallas_call | solution.py:115
  46.2 4.3 %all-to-all-start.2 = ((bf16[4,128,1024]{2,1,0:T(8,128)(2,1)}), bf16[4,128,1024]{2,1,0:T(8,128)(2,1)}, u32[]{:S(2)}, u32[]{:S(2)}) async-start(bf16[4,128,1024]{2,1,0:T(8,128)(2,1)} %bitcast.16), calls=%async_computation.2 | async-start | bytes 2097152 | tf_op jit(solution)/shard_map/all_to_all | solution.py:86
  50.5 0.0 copy-done
  50.5 4.0 %convolution_convert_fusion = bf16[1024,1024]{1,0:T(8,128)(2,1)S(1)} fusion(bf16[1024,1024]{1,0:T(8,128)(2,1)S(1)} %copy-done, bf16[1024,1024]{1,0:T(8,128)(2,1)} %x_ref.1), kind=kOutput, calls=%fused_computation | convolution fusion | flops 2148532224 | bytes 6291456 | tf_op jit(solution)/shard_map/dot_general | solution.py:289
  54.5 1.3 %shard_map.52 = (bf16[8,16,1024]{2,1,0:T(8,128)(2,1)}, bf16[8,16,1024]{2,1,0:T(8,128)(2,1)}, bf16[8,16,1024]{2,1,0:T(8,128)(2,1)}, bf16[8,16,1024]{2,1,0:T(8,128)(2,1)}) custom-call(bf16[64,16,1024]{2,1,0:T(8,128)(2,1)S(1)} %bitcast.13), custom_call_target="tpu_custom_call" | custom-call | tf_op jit(solution)/shard_map/pallas_call | solution.py:115
  55.8 3.9 %collective-permute-start = (bf16[8,16,1024]{2,1,0:T(8,128)(2,1)}, bf16[8,16,1024]{2,1,0:T(8,128)(2,1)S(1)}, u32[]{:S(2)}, u32[]{:S(2)}) collective-permute-start(bf16[8,16,1024]{2,1,0:T(8,128)(2,1)} %get-tuple-element.9), channel_id=1, source_target_pairs={{0,128},{499,114},{4,132},{503,118},{8,136},{507,122},{12,140},{51... | collective-permute-start | bytes 786440 | tf_op jit(solution)/shard_map/ppermute | solution.py:284
  59.7 3.4 %collective-permute-start.1 = (bf16[8,16,1024]{2,1,0:T(8,128)(2,1)}, bf16[8,16,1024]{2,1,0:T(8,128)(2,1)S(1)}, u32[]{:S(2)}, u32[]{:S(2)}) collective-permute-start(bf16[8,16,1024]{2,1,0:T(8,128)(2,1)} %get-tuple-element.10), channel_id=1, source_target_pairs={{0,16},{499,387},{4,20},{503,391},{8,24},{507,395},{12,28},{511,39... | collective-permute-start | bytes 786440 | tf_op jit(solution)/shard_map/ppermute | solution.py:284
  63.0 2.0 %collective-permute-start.2 = (bf16[8,16,1024]{2,1,0:T(8,128)(2,1)}, bf16[8,16,1024]{2,1,0:T(8,128)(2,1)S(1)}, u32[]{:S(2)}, u32[]{:S(2)}) collective-permute-start(bf16[8,16,1024]{2,1,0:T(8,128)(2,1)} %get-tuple-element.11), channel_id=1, source_target_pairs={{0,144},{499,2},{4,148},{503,6},{8,152},{507,10},{12,156},{511,14}... | collective-permute-start | bytes 786440 | tf_op jit(solution)/shard_map/ppermute | solution.py:284
  65.0 0.0 copy-done.1
  65.0 4.0 %collective-permute-start.3 = (bf16[512,1024]{1,0:T(8,128)(2,1)S(1)}, bf16[512,1024]{1,0:T(8,128)(2,1)}, u32[]{:S(2)}, u32[]{:S(2)}) collective-permute-start(bf16[512,1024]{1,0:T(8,128)(2,1)S(1)} %bitcast.11), channel_id=1, source_target_pairs={{0,112},{499,483},{4,116},{503,487},{8,120},{507,491},{12,124},{51... | collective-permute-start | bytes 3145736 | tf_op jit(solution)/shard_map/ppermute | solution.py:284
  69.0 0.0 collective-permute-done.refs_1_
  69.0 0.0 collective-permute-done.1.refs_2_
  69.0 5.4 %collective-permute-done.2.refs_3_ = bf16[8,16,1024]{2,1,0:T(8,128)(2,1)S(1)} collective-permute-done((bf16[8,16,1024]{2,1,0:T(8,128)(2,1)}, bf16[8,16,1024]{2,1,0:T(8,128)(2,1)S(1)}, u32[]{:S(2)}, u32[]{:S(2)}) %collective-permute-start.2) | collective-permute-done | bytes 262176 | tf_op jit(solution)/shard_map/ppermute | solution.py:284
  74.4 0.9 copy-done.3
  75.4 0.8 shard_map.53.gradient_ref
  76.2 0.0 all-to-all-done.2
  76.2 3.1 %shard_map.54 = bf16[8,32,1024]{2,1,0:T(8,128)(2,1)} custom-call(bf16[4,8,16,1024]{3,2,1,0:T(8,128)(2,1)} %bitcast.4.moments_ref, bf16[8,16,1024]{2,1,0:T(8,128)(2,1)} %shard_map.53.gradient_ref), custom_call_target="tpu_custom_call" | custom-call | tf_op jit(solution)/shard_map/pallas_call | solution.py:115
  79.3 5.8 %all-to-all-start.3 = ((bf16[8,32,1024]{2,1,0:T(8,128)(2,1)}), bf16[8,32,1024]{2,1,0:T(8,128)(2,1)}, u32[]{:S(2)}, u32[]{:S(2)}) async-start(bf16[8,32,1024]{2,1,0:T(8,128)(2,1)} %shard_map.54), calls=%async_computation.3 | async-start | bytes 1048576 | tf_op jit(solution)/shard_map/all_to_all | solution.py:86
  85.1 0.2 collective-permute-done.3.refs_3_
  85.2 19.1 %all-to-all-done.3.refs_0_ = bf16[8,32,1024]{2,1,0:T(8,128)(2,1)} async-done(((bf16[8,32,1024]{2,1,0:T(8,128)(2,1)}), bf16[8,32,1024]{2,1,0:T(8,128)(2,1)}, u32[]{:S(2)}, u32[]{:S(2)}) %all-to-all-start.3) | async-done | bytes 524320 | tf_op jit(solution)/shard_map/all_to_all | solution.py:86
  104.4 0.0 copy-done.5
  104.4 4.8 %shard_map.55 = (f32[16,1024]{1,0:T(8,128)}, f32[16,1024]{1,0:T(8,128)}) custom-call(bf16[8,32,1024]{2,1,0:T(8,128)(2,1)} %all-to-all-done.3.refs_0_, f32[16,1024]{1,0:T(8,128)S(1)} %bitcast.15, bf16[512,1024]{1,0:T(8,128)(2,1)} %bitcast.12, bf16[512,1024]{1,0:T(8,128)(2,1)} %collective-permute-done.3.refs_3_), custom_call_target="tpu_custom_call" | custom-call | tf_op jit(solution)/shard_map/pallas_call | solution.py:115
  (2 shorter events, 0.0 us)
Async XLA Ops:
  0.6 49.9 %copy-start = (bf16[1024,1024]{1,0:T(8,128)(2,1)S(1)}, bf16[1024,1024]{1,0:T(8,128)(2,1)}, u32[]{:S(2)}) copy-start(bf16[1024,1024]{1,0:T(8,128)(2,1)} %param.4) | copy-start | bytes 6291460
  0.6 1.0 copy-start.4
  1.6 41.4 %copy-start.2 = (bf16[1024,1024]{1,0:T(8,128)(2,1)S(1)}, bf16[1024,1024]{1,0:T(8,128)(2,1)}, u32[]{:S(2)}) copy-start(bf16[1024,1024]{1,0:T(8,128)(2,1)} %x_ref.1) | copy-start | bytes 6291460
  43.0 22.0 %copy-start.1 = (bf16[4,128,1024]{2,1,0:T(8,128)(2,1)}, bf16[4,128,1024]{2,1,0:T(8,128)(2,1)S(1)}, u32[]{:S(2)}) copy-start(bf16[4,128,1024]{2,1,0:T(8,128)(2,1)S(1)} %all_to_all.21) | copy-start | bytes 3145732
  46.2 30.0 %all-to-all-start.2 = ((bf16[4,128,1024]{2,1,0:T(8,128)(2,1)}), bf16[4,128,1024]{2,1,0:T(8,128)(2,1)}, u32[]{:S(2)}, u32[]{:S(2)}) async-start(bf16[4,128,1024]{2,1,0:T(8,128)(2,1)} %bitcast.16), calls=%async_computation.2 | async-start | bytes 2097152 | tf_op jit(solution)/shard_map/all_to_all | solution.py:86
  55.8 13.2 %collective-permute-start = (bf16[8,16,1024]{2,1,0:T(8,128)(2,1)}, bf16[8,16,1024]{2,1,0:T(8,128)(2,1)S(1)}, u32[]{:S(2)}, u32[]{:S(2)}) collective-permute-start(bf16[8,16,1024]{2,1,0:T(8,128)(2,1)} %get-tuple-element.9), channel_id=1, source_target_pairs={{0,128},{499,114},{4,132},{503,118},{8,136},{507,122},{12,140},{51... | collective-permute-start | bytes 786440 | tf_op jit(solution)/shard_map/ppermute | solution.py:284
  59.7 9.4 %collective-permute-start.1 = (bf16[8,16,1024]{2,1,0:T(8,128)(2,1)}, bf16[8,16,1024]{2,1,0:T(8,128)(2,1)S(1)}, u32[]{:S(2)}, u32[]{:S(2)}) collective-permute-start(bf16[8,16,1024]{2,1,0:T(8,128)(2,1)} %get-tuple-element.10), channel_id=1, source_target_pairs={{0,16},{499,387},{4,20},{503,391},{8,24},{507,395},{12,28},{511,39... | collective-permute-start | bytes 786440 | tf_op jit(solution)/shard_map/ppermute | solution.py:284
  63.0 11.4 %collective-permute-start.2 = (bf16[8,16,1024]{2,1,0:T(8,128)(2,1)}, bf16[8,16,1024]{2,1,0:T(8,128)(2,1)S(1)}, u32[]{:S(2)}, u32[]{:S(2)}) collective-permute-start(bf16[8,16,1024]{2,1,0:T(8,128)(2,1)} %get-tuple-element.11), channel_id=1, source_target_pairs={{0,144},{499,2},{4,148},{503,6},{8,152},{507,10},{12,156},{511,14}... | collective-permute-start | bytes 786440 | tf_op jit(solution)/shard_map/ppermute | solution.py:284
  65.0 20.2 %collective-permute-start.3 = (bf16[512,1024]{1,0:T(8,128)(2,1)S(1)}, bf16[512,1024]{1,0:T(8,128)(2,1)}, u32[]{:S(2)}, u32[]{:S(2)}) collective-permute-start(bf16[512,1024]{1,0:T(8,128)(2,1)S(1)} %bitcast.11), channel_id=1, source_target_pairs={{0,112},{499,483},{4,116},{503,487},{8,120},{507,491},{12,124},{51... | collective-permute-start | bytes 3145736 | tf_op jit(solution)/shard_map/ppermute | solution.py:284
  74.4 1.0 copy-start.3
  75.4 29.0 %copy-start.5 = (f32[1024,16]{0,1:T(8,128)S(1)}, f32[1024,16]{0,1:T(8,128)}, u32[]{:S(2)}) copy-start(f32[1024,16]{0,1:T(8,128)} %param.5) | copy-start | bytes 196612
  79.3 25.1 %all-to-all-start.3 = ((bf16[8,32,1024]{2,1,0:T(8,128)(2,1)}), bf16[8,32,1024]{2,1,0:T(8,128)(2,1)}, u32[]{:S(2)}, u32[]{:S(2)}) async-start(bf16[8,32,1024]{2,1,0:T(8,128)(2,1)} %shard_map.54), calls=%async_computation.3 | async-start | bytes 1048576 | tf_op jit(solution)/shard_map/all_to_all | solution.py:86

commit v7 on v5

--- a/solution.py
+++ b/solution.py
@@ -44,6 +44,11 @@
 ]
 
 
+COSETS = [
+    FAR_GROUPS[8 * blk + k] + FAR_GROUPS[8 * blk + 4 + k] for blk in range(BLOCKS) for k in range(4)
+]
+
+
 def moves(step_z, step_y):
     return [
         (device(z, y, blk), device(step_z(z), step_y(y), blk))
@@ -61,12 +66,7 @@
     return at ^ 1
 
 
-def outer(at):
-    return (at - 1) % 8 if at % 2 == 0 else (at + 1) % 8
-
-
 INNER = {1: moves(inner, stay), 2: moves(stay, inner), 3: moves(inner, inner)}
-ACROSS = moves(stay, outer)
 
 
 def exchange(blocks, groups):
@@ -145,57 +145,38 @@
 
 def moment_kernel(rows_ref, x_ref, out_ref):
     x = x_ref[...]
-    whitened = lax.dot_general(rows_ref[...], x, ROWS_ROWS, preferred_element_type=f32)
+    rows = rows_ref[position()[5]]
+    whitened = lax.dot_general(rows, x, ROWS_ROWS, preferred_element_type=f32)
     out_ref[...] = jnp.dot(whitened.astype(bf16), x, preferred_element_type=f32).astype(bf16)
 
 
 def moment_of(rows, x):
-    return pl.pallas_call(
-        moment_kernel,
-        out_shape=jax.ShapeDtypeStruct(rows.shape, bf16),
-        in_specs=[vmem()] * 2,
-        out_specs=vmem(),
-        compiler_params=pltpu.CompilerParams(vmem_limit_bytes=VMEM_LIMIT),
-        cost_estimate=pl.CostEstimate(
-            flops=4 * rows.size * x.shape[0], bytes_accessed=2 * x.size, transcendentals=0
-        ),
-        name="moment",
-    )(rows, x)
+    shape = jax.ShapeDtypeStruct(rows.shape[1:], bf16)
+    return call(moment_kernel, shape, [vmem()] * 2, vmem(), rows, x)
 
 
 def join_kernel(*refs):
-    moments, gradients, out_ref, staged, sems = refs[:4], refs[4:8], refs[8], refs[9], refs[10]
-    leaving = []
+    moments, gradients, out_ref = refs[:4], refs[4:8], refs[8]
     for f in range(8):
         for first, parts in ((0, moments), (16, gradients)):
             total = parts[0][f].astype(f32)
             for part in parts[1:]:
                 total = total + part[f].astype(f32)
-            staged[f, first : first + 16] = total.astype(bf16)
-        copy = pltpu.make_async_copy(staged.at[f], out_ref.at[f], sems.at[f])
-        copy.start()
-        leaving.append(copy)
-    for copy in leaving:
-        copy.wait()
+            out_ref[f, first : first + 16] = total.astype(bf16)
 
 
 def join(moments, gradients):
     width = gradients[0].shape[2]
     moments = [m.reshape(8, 16, width) for m in moments]
-    shape = pltpu.HBM((8, 32, width), bf16)
-    scratch = [pltpu.VMEM(shape.shape, bf16), pltpu.SemaphoreType.DMA((8,))]
-    return call(
-        join_kernel, shape, [vmem()] * 8, hbm(), *moments, *gradients, scratch_shapes=scratch
-    )
+    shape = jax.ShapeDtypeStruct((8, 32, width), bf16)
+    return call(join_kernel, shape, [vmem()] * 8, vmem(), *moments, *gradients)
 
 
 def finish_kernel(tokens, *refs):
-    sums_ref, own_ref, blocks = refs[0], refs[1], refs[2:4]
-    new_ref, direction_ref, rows, sems = refs[4:]
-    pairs = [(block, rows.at[pl.ds(k * 512, 512)]) for k, block in enumerate(blocks)]
-    copies = run_copies(pairs, sems)
-    _, _, _, yh, zh, _ = position()
-    at = (2 * yh + zh) * 16
+    sums_ref, own_ref, blocks = refs[0], refs[1], refs[2:6]
+    new_ref, direction_ref = refs[6:]
+    _, _, _, yh, zh, h = position()
+    at = h * 128 + (2 * yh + zh) * 16
     own = own_ref[...]
     total = sums_ref[0].astype(f32)
     for k in range(1, 8):
@@ -204,34 +185,30 @@
     high = inner_rows.astype(bf16)
     low = (inner_rows - high.astype(f32)).astype(bf16)
     left = jnp.concatenate([high, low, total[16:].astype(bf16)], axis=0)
-    for copy in copies:
-        copy.wait()
-    product = lax.dot_general(left, rows[...], ROWS_ROWS, preferred_element_type=f32)
-    curve = product[:16] + product[16:32]
-    column = lax.broadcasted_iota(jnp.int32, curve.shape, 1)
-    row = lax.broadcasted_iota(jnp.int32, curve.shape, 0)
-    curve = curve - (column == row + at).astype(f32)
-    right = jnp.concatenate([curve.astype(bf16), product[32:].astype(bf16)], axis=0)
-    result = jnp.dot(right, rows[...], preferred_element_type=f32)
+    result = jnp.zeros((32, own.shape[1]), f32)
+    for k, block in enumerate(blocks):
+        part = block[...]
+        product = lax.dot_general(left, part, ROWS_ROWS, preferred_element_type=f32)
+        curve = product[:16] + product[16:32]
+        if k == 0:
+            column = lax.broadcasted_iota(jnp.int32, curve.shape, 1)
+            row = lax.broadcasted_iota(jnp.int32, curve.shape, 0)
+            curve = curve - (column == row + at).astype(f32)
+        right = jnp.concatenate([curve.astype(bf16), product[32:].astype(bf16)], axis=0)
+        result = result + jnp.dot(right, part, preferred_element_type=f32)
     new_ref[...] = own - 0.5 * step_size * result[:16]
     direction_ref[...] = result[16:]
 
 
 def finish(tokens, sums, own, blocks):
-    blocks = [pltpu.with_memory_space_constraint(block, pltpu.HBM) for block in blocks]
-    scratch = [
-        pltpu.VMEM((2 * 512, own.shape[1]), bf16),
-        pltpu.SemaphoreType.DMA((2,)),
-    ]
     return call(
         functools.partial(finish_kernel, tokens),
         [jax.ShapeDtypeStruct(own.shape, f32)] * 2,
-        [vmem()] * 2 + [hbm()] * 2,
+        [vmem()] * 6,
         [vmem()] * 2,
         sums,
         own,
-        *blocks,
-        scratch_shapes=scratch,
+        *[block.reshape(256, own.shape[1]) for block in blocks],
     )
 
 
@@ -245,7 +222,7 @@
         return lax.ppermute(block, PLANES, pairs)
 
     own = factor.T
-    mine = exchange(spread(own, 8), FAR_GROUPS).reshape(8 * owned, width)
+    mine = exchange(spread(own, 16), COSETS).reshape(2, 8 * owned, width)
 
     gradient_part = lax.dot_general(
         cotangent, activations, TOKENS_FIRST, preferred_element_type=f32
@@ -262,12 +239,10 @@
     for d in (1, 2, 3):
         moment = moment_of(near[d], activations)
         moments.append(turn(moment, INNER[d]))
-    near = jnp.concatenate(near, axis=0)
-    far = turn(near, ACROSS)
     joined = join(moments, gradients)
     sums = exchange(joined, FAR_GROUPS)
 
-    new_factor, direction = finish(total_tokens, sums, own, [near, far])
+    new_factor, direction = finish(total_tokens, sums, own, near)
     return (new_factor.T, direction.T)
 
 

time: 106 us -> 110 us (1.038)
  blocking collectives: 27.9 us -> 60.4 us
  waiting for transfers between devices: 20.4 us -> 4.65 us
  starting transfers between devices: 38.4 us -> 27.8 us
  Pallas kernels: 10.8 us -> 9.16 us
    all_to_all x1 -> x2, blocking collectives: 27.9 us -> 60.4 us  [exchange(): lax.all_to_all(blocks, PLANES, split_axis=0, concat_axis=0, tiled=True, a...]
    all_to_all x1 -> x0, waiting for transfers between devices: 12.9 us -> none  [exchange(): lax.all_to_all(blocks, PLANES, split_axis=0, concat_axis=0, tiled=True, a...]
    all_to_all x1 -> x0, starting transfers between devices: 7.58 us -> none  [exchange(): lax.all_to_all(blocks, PLANES, split_axis=0, concat_axis=0, tiled=True, a...]
    pallas_call x4 -> x0, Pallas kernels: 4.46 us -> none  [moment_of(): pl.pallas_call(moment_kernel, out_shape=jax.ShapeDtypeStruct(rows.shape,...]
    ppermute x10 -> x9, starting transfers between devices: 30.8 us -> 27.8 us  [turn(): return lax.ppermute(block, PLANES, pairs)]
    pallas_call x4 -> x8, Pallas kernels: 6.36 us -> 9.16 us  [call(): pl.pallas_call(kernel, out_shape=out_shape, in_specs=in_specs, out_specs=...]
    ppermute x10 -> x9, waiting for transfers between devices: 7.42 us -> 4.65 us  [turn(): return lax.ppermute(block, PLANES, pairs)]
  transfers between devices with their start and end apart: 11 -> 9, of which waited for: 2 -> 1; matrix products, arithmetic and copies ran while one was open for 5% -> 4% of each run, Pallas kernels for 6% -> 5%
where the time goes in v7:
time: 110 us; the launch traced here: 108 us
  blocking collectives  60.4 us (55%)
  starting transfers between devices  27.8 us (25%)
  Pallas kernels  9.16 us (8%)
  waiting for transfers between devices  4.65 us (4%)
  matrix products  3.98 us (4%)
    all_to_all x2, blocking collectives, exchange(): lax.all_to_all(blocks, PLANES, split_axis=0, concat_axis=0, tiled=True, a...  60.4 us
    ppermute x9, starting transfers between devices, turn(): return lax.ppermute(block, PLANES, pairs)  27.8 us
    pallas_call x8, Pallas kernels, call(): pl.pallas_call(kernel, out_shape=out_shape, in_specs=in_specs, out_specs=...  9.16 us
    ppermute x9, waiting for transfers between devices, turn(): return lax.ppermute(block, PLANES, pairs)  4.65 us
    dot_general x1, matrix products, on_device(): lax.dot_general(cotangent, activations, TOKENS_FIRST, preferred_element_t...  3.98 us
  transfers between devices with their start and end apart: 9, of which 1 were waited for; matrix products, arithmetic and copies ran while one was open for 4% of the time, Pallas kernels for 5%

profile of v7, /device:TPU:6, one launch (start us, length us, event | category | flops | bytes accessed | tf_op | source)
XLA Modules:
  0.0 107.8 jit_solution(4291564707514603219)
XLA Ops:
  0.6 0.0 copy-start
  0.6 0.0 copy-start.3
  0.7 1.0 copy-done.3
  1.6 0.9 shard_map.50
  2.6 33.8 %all_to_all.10 = bf16[16,16,1024]{2,1,0:T(8,128)(2,1)S(1)} all-to-all(bf16[16,16,1024]{2,1,0:T(8,128)(2,1)} %shard_map.50), channel_id=1, replica_groups={{0,256,33,289,64,320,97,353,1,257,32,288,65,321,96,352},{128,384,161,41..., dimensions={0} | all-to-all | bytes 1048576 | tf_op jit(solution)/shard_map/all_to_all | solution.py:73
  36.3 1.9 %collective-permute-start.4 = (bf16[2,128,1024]{2,1,0:T(8,128)(2,1)S(1)}, bf16[2,128,1024]{2,1,0:T(8,128)(2,1)S(1)}, u32[]{:S(2)}, u32[]{:S(2)}) collective-permute-start(bf16[2,128,1024]{2,1,0:T(8,128)(2,1)S(1)} %bitcast.15), channel_id=1, source_target_pairs={{0,144},{499,2},{4,148},{503,6},{8,152},{507,10},{12,156},{511,14}... | collective-permute-start | bytes 1572872 | tf_op jit(solution)/shard_map/ppermute | solution.py:222
  38.3 4.8 %collective-permute-start.2 = (bf16[2,128,1024]{2,1,0:T(8,128)(2,1)S(1)}, bf16[2,128,1024]{2,1,0:T(8,128)(2,1)S(1)}, u32[]{:S(2)}, u32[]{:S(2)}) collective-permute-start(bf16[2,128,1024]{2,1,0:T(8,128)(2,1)S(1)} %bitcast.16), channel_id=1, source_target_pairs={{0,16},{499,387},{4,20},{503,391},{8,24},{507,395},{12,28},{511,39... | collective-permute-start | bytes 1572872 | tf_op jit(solution)/shard_map/ppermute | solution.py:222
  43.1 2.5 %collective-permute-start = (bf16[2,128,1024]{2,1,0:T(8,128)(2,1)S(1)}, bf16[2,128,1024]{2,1,0:T(8,128)(2,1)S(1)}, u32[]{:S(2)}, u32[]{:S(2)}) collective-permute-start(bf16[2,128,1024]{2,1,0:T(8,128)(2,1)S(1)} %bitcast.17), channel_id=1, source_target_pairs={{0,128},{499,114},{4,132},{503,118},{8,136},{507,122},{12,140},{51... | collective-permute-start | bytes 1572872 | tf_op jit(solution)/shard_map/ppermute | solution.py:222
  45.6 4.0 %convolution_convert_fusion = bf16[1024,1024]{1,0:T(8,128)(2,1)S(1)} fusion(bf16[1024,1024]{1,0:T(8,128)(2,1)S(1)} %copy-done, bf16[1024,1024]{1,0:T(8,128)(2,1)} %x_ref.7), kind=kOutput, calls=%fused_computation | convolution fusion | flops 2148532224 | bytes 6291456 | tf_op jit(solution)/shard_map/dot_general | solution.py:227
  49.6 0.0 copy-start.1
  49.6 1.3 %shard_map.55 = (bf16[8,16,1024]{2,1,0:T(8,128)(2,1)}, bf16[8,16,1024]{2,1,0:T(8,128)(2,1)}, bf16[8,16,1024]{2,1,0:T(8,128)(2,1)}, bf16[8,16,1024]{2,1,0:T(8,128)(2,1)}) custom-call(bf16[64,16,1024]{2,1,0:T(8,128)(2,1)S(1)} %bitcast.20), custom_call_target="tpu_custom_call" | custom-call | tf_op jit(solution)/shard_map/pallas_call | solution.py:102
  50.9 3.4 %collective-permute-start.6 = (bf16[8,16,1024]{2,1,0:T(8,128)(2,1)}, bf16[8,16,1024]{2,1,0:T(8,128)(2,1)S(1)}, u32[]{:S(2)}, u32[]{:S(2)}) collective-permute-start(bf16[8,16,1024]{2,1,0:T(8,128)(2,1)} %get-tuple-element.9), channel_id=1, source_target_pairs={{0,128},{499,114},{4,132},{503,118},{8,136},{507,122},{12,140},{51... | collective-permute-start | bytes 786440 | tf_op jit(solution)/shard_map/ppermute | solution.py:222
  54.3 1.9 %collective-permute-start.7 = (bf16[8,16,1024]{2,1,0:T(8,128)(2,1)}, bf16[8,16,1024]{2,1,0:T(8,128)(2,1)S(1)}, u32[]{:S(2)}, u32[]{:S(2)}) collective-permute-start(bf16[8,16,1024]{2,1,0:T(8,128)(2,1)} %get-tuple-element.10), channel_id=1, source_target_pairs={{0,16},{499,387},{4,20},{503,391},{8,24},{507,395},{12,28},{511,39... | collective-permute-start | bytes 786440 | tf_op jit(solution)/shard_map/ppermute | solution.py:222
  56.2 0.0 collective-permute-done.4.rows_ref
  56.2 3.9 %collective-permute-start.8 = (bf16[8,16,1024]{2,1,0:T(8,128)(2,1)}, bf16[8,16,1024]{2,1,0:T(8,128)(2,1)S(1)}, u32[]{:S(2)}, u32[]{:S(2)}) collective-permute-start(bf16[8,16,1024]{2,1,0:T(8,128)(2,1)} %get-tuple-element.11), channel_id=1, source_target_pairs={{0,144},{499,2},{4,148},{503,6},{8,152},{507,10},{12,156},{511,14}... | collective-permute-start | bytes 786440 | tf_op jit(solution)/shard_map/ppermute | solution.py:222
  60.1 1.1 %shard_map.54 = bf16[128,1024]{1,0:T(8,128)(2,1)S(1)} custom-call(bf16[2,128,1024]{2,1,0:T(8,128)(2,1)S(1)} %collective-permute-done.4.rows_ref, bf16[1024,1024]{1,0:T(8,128)(2,1)S(1)} %copy-done.1), custom_call_target="tpu_custom_call" | custom-call | tf_op jit(solution)/shard_map/pallas_call | solution.py:102
  61.3 2.8 %collective-permute-start.5 = (bf16[128,1024]{1,0:T(8,128)(2,1)S(1)}, bf16[128,1024]{1,0:T(8,128)(2,1)S(1)}, u32[]{:S(2)}, u32[]{:S(2)}) collective-permute-start(bf16[128,1024]{1,0:T(8,128)(2,1)S(1)} %shard_map.54), channel_id=1, source_target_pairs={{0,144},{499,2},{4,148},{503,6},{8,152},{507,10},{12,156},{511,14}... | collective-permute-start | bytes 786440 | tf_op jit(solution)/shard_map/ppermute | solution.py:222
  64.1 1.1 %shard_map.53 = bf16[128,1024]{1,0:T(8,128)(2,1)S(1)} custom-call(bf16[2,128,1024]{2,1,0:T(8,128)(2,1)S(1)} %collective-permute-done.2.rows_ref, bf16[1024,1024]{1,0:T(8,128)(2,1)S(1)} %copy-done.1), custom_call_target="tpu_custom_call" | custom-call | tf_op jit(solution)/shard_map/pallas_call | solution.py:102
  65.2 0.0 collective-permute-done.rows_ref
  65.2 3.9 %collective-permute-start.3 = (bf16[128,1024]{1,0:T(8,128)(2,1)S(1)}, bf16[128,1024]{1,0:T(8,128)(2,1)S(1)}, u32[]{:S(2)}, u32[]{:S(2)}) collective-permute-start(bf16[128,1024]{1,0:T(8,128)(2,1)S(1)} %shard_map.53), channel_id=1, source_target_pairs={{0,16},{499,387},{4,20},{503,391},{8,24},{507,395},{12,28},{511,39... | collective-permute-start | bytes 786440 | tf_op jit(solution)/shard_map/ppermute | solution.py:222
  69.2 1.1 %shard_map.52 = bf16[128,1024]{1,0:T(8,128)(2,1)S(1)} custom-call(bf16[2,128,1024]{2,1,0:T(8,128)(2,1)S(1)} %collective-permute-done.rows_ref, bf16[1024,1024]{1,0:T(8,128)(2,1)S(1)} %copy-done.1), custom_call_target="tpu_custom_call" | custom-call | tf_op jit(solution)/shard_map/pallas_call | solution.py:102
  70.3 0.0 collective-permute-done.6.refs_5_
  70.3 2.6 %collective-permute-start.1 = (bf16[128,1024]{1,0:T(8,128)(2,1)S(1)}, bf16[128,1024]{1,0:T(8,128)(2,1)S(1)}, u32[]{:S(2)}, u32[]{:S(2)}) collective-permute-start(bf16[128,1024]{1,0:T(8,128)(2,1)S(1)} %shard_map.52), channel_id=1, source_target_pairs={{0,128},{499,114},{4,132},{503,118},{8,136},{507,122},{12,140},{51... | collective-permute-start | bytes 786440 | tf_op jit(solution)/shard_map/ppermute | solution.py:222
  72.9 1.1 %shard_map.51 = bf16[128,1024]{1,0:T(8,128)(2,1)S(1)} custom-call(bf16[2,128,1024]{2,1,0:T(8,128)(2,1)S(1)} %bitcast.18, bf16[1024,1024]{1,0:T(8,128)(2,1)S(1)} %copy-done.1), custom_call_target="tpu_custom_call" | custom-call | tf_op jit(solution)/shard_map/pallas_call | solution.py:102
  74.0 0.0 copy-start.4
  74.0 0.0 collective-permute-done.7.refs_6_
  74.0 0.0 collective-permute-done.5
  74.1 0.0 collective-permute-done.3
  74.1 4.6 %collective-permute-done.1 = bf16[128,1024]{1,0:T(8,128)(2,1)S(1)} collective-permute-done((bf16[128,1024]{1,0:T(8,128)(2,1)S(1)}, bf16[128,1024]{1,0:T(8,128)(2,1)S(1)}, u32[]{:S(2)}, u32[]{:S(2)}) %collective-permute-start.1) | collective-permute-done | bytes 262176 | tf_op jit(solution)/shard_map/ppermute | solution.py:222
  78.7 0.3 shard_map.56
  79.0 26.6 %all_to_all.11.refs_0_ = bf16[8,32,1024]{2,1,0:T(8,128)(2,1)S(1)} all-to-all(bf16[8,32,1024]{2,1,0:T(8,128)(2,1)S(1)} %shard_map.56), channel_id=1, replica_groups={{0,256,33,289,64,320,97,353},{128,384,161,417,192,448,225,481},{16,272,..., dimensions={0} | all-to-all | bytes 1048576 | tf_op jit(solution)/shard_map/all_to_all | solution.py:73
  105.6 2.2 %shard_map.57 = (f32[16,1024]{1,0:T(8,128)}, f32[16,1024]{1,0:T(8,128)}) custom-call(bf16[8,32,1024]{2,1,0:T(8,128)(2,1)S(1)} %all_to_all.11.refs_0_, f32[16,1024]{1,0:T(8,128)S(1)} %bitcast.29, bf16[256,1024]{1,0:T(8,128)(2,1)S(1)} %bitcast.19, bf16[256,1024]{1,0:T(8,128)(2,1)S(1)} %bitcast.23, bf16[256,1024]{1,0:T(8,128)(2,1)S(1)} %bitcast.22, ...), custom_call_target="tpu_custom_call" | custom-call | tf_op jit(solution)/shard_map/pallas_call | solution.py:102
  (7 shorter events, 0.0 us)
Async XLA Ops:
  0.6 44.9 %copy-start = (bf16[1024,1024]{1,0:T(8,128)(2,1)S(1)}, bf16[1024,1024]{1,0:T(8,128)(2,1)}, u32[]{:S(2)}) copy-start(bf16[1024,1024]{1,0:T(8,128)(2,1)} %param.4) | copy-start | bytes 6291460
  0.6 1.0 copy-start.3
  36.3 19.9 %collective-permute-start.4 = (bf16[2,128,1024]{2,1,0:T(8,128)(2,1)S(1)}, bf16[2,128,1024]{2,1,0:T(8,128)(2,1)S(1)}, u32[]{:S(2)}, u32[]{:S(2)}) collective-permute-start(bf16[2,128,1024]{2,1,0:T(8,128)(2,1)S(1)} %bitcast.15), channel_id=1, source_target_pairs={{0,144},{499,2},{4,148},{503,6},{8,152},{507,10},{12,156},{511,14}... | collective-permute-start | bytes 1572872 | tf_op jit(solution)/shard_map/ppermute | solution.py:222
  38.3 23.0 %collective-permute-start.2 = (bf16[2,128,1024]{2,1,0:T(8,128)(2,1)S(1)}, bf16[2,128,1024]{2,1,0:T(8,128)(2,1)S(1)}, u32[]{:S(2)}, u32[]{:S(2)}) collective-permute-start(bf16[2,128,1024]{2,1,0:T(8,128)(2,1)S(1)} %bitcast.16), channel_id=1, source_target_pairs={{0,16},{499,387},{4,20},{503,391},{8,24},{507,395},{12,28},{511,39... | collective-permute-start | bytes 1572872 | tf_op jit(solution)/shard_map/ppermute | solution.py:222
  43.1 22.1 %collective-permute-start = (bf16[2,128,1024]{2,1,0:T(8,128)(2,1)S(1)}, bf16[2,128,1024]{2,1,0:T(8,128)(2,1)S(1)}, u32[]{:S(2)}, u32[]{:S(2)}) collective-permute-start(bf16[2,128,1024]{2,1,0:T(8,128)(2,1)S(1)} %bitcast.17), channel_id=1, source_target_pairs={{0,128},{499,114},{4,132},{503,118},{8,136},{507,122},{12,140},{51... | collective-permute-start | bytes 1572872 | tf_op jit(solution)/shard_map/ppermute | solution.py:222
  49.6 10.6 %copy-start.1 = (bf16[1024,1024]{1,0:T(8,128)(2,1)S(1)}, bf16[1024,1024]{1,0:T(8,128)(2,1)}, u32[]{:S(2)}) copy-start(bf16[1024,1024]{1,0:T(8,128)(2,1)} %x_ref.7) | copy-start | bytes 6291460
  50.9 19.4 %collective-permute-start.6 = (bf16[8,16,1024]{2,1,0:T(8,128)(2,1)}, bf16[8,16,1024]{2,1,0:T(8,128)(2,1)S(1)}, u32[]{:S(2)}, u32[]{:S(2)}) collective-permute-start(bf16[8,16,1024]{2,1,0:T(8,128)(2,1)} %get-tuple-element.9), channel_id=1, source_target_pairs={{0,128},{499,114},{4,132},{503,118},{8,136},{507,122},{12,140},{51... | collective-permute-start | bytes 786440 | tf_op jit(solution)/shard_map/ppermute | solution.py:222
  54.3 19.8 %collective-permute-start.7 = (bf16[8,16,1024]{2,1,0:T(8,128)(2,1)}, bf16[8,16,1024]{2,1,0:T(8,128)(2,1)S(1)}, u32[]{:S(2)}, u32[]{:S(2)}) collective-permute-start(bf16[8,16,1024]{2,1,0:T(8,128)(2,1)} %get-tuple-element.10), channel_id=1, source_target_pairs={{0,16},{499,387},{4,20},{503,391},{8,24},{507,395},{12,28},{511,39... | collective-permute-start | bytes 786440 | tf_op jit(solution)/shard_map/ppermute | solution.py:222
  56.2 17.8 %collective-permute-start.8 = (bf16[8,16,1024]{2,1,0:T(8,128)(2,1)}, bf16[8,16,1024]{2,1,0:T(8,128)(2,1)S(1)}, u32[]{:S(2)}, u32[]{:S(2)}) collective-permute-start(bf16[8,16,1024]{2,1,0:T(8,128)(2,1)} %get-tuple-element.11), channel_id=1, source_target_pairs={{0,144},{499,2},{4,148},{503,6},{8,152},{507,10},{12,156},{511,14}... | collective-permute-start | bytes 786440 | tf_op jit(solution)/shard_map/ppermute | solution.py:222
  61.3 12.8 %collective-permute-start.5 = (bf16[128,1024]{1,0:T(8,128)(2,1)S(1)}, bf16[128,1024]{1,0:T(8,128)(2,1)S(1)}, u32[]{:S(2)}, u32[]{:S(2)}) collective-permute-start(bf16[128,1024]{1,0:T(8,128)(2,1)S(1)} %shard_map.54), channel_id=1, source_target_pairs={{0,144},{499,2},{4,148},{503,6},{8,152},{507,10},{12,156},{511,14}... | collective-permute-start | bytes 786440 | tf_op jit(solution)/shard_map/ppermute | solution.py:222
  65.2 8.8 %collective-permute-start.3 = (bf16[128,1024]{1,0:T(8,128)(2,1)S(1)}, bf16[128,1024]{1,0:T(8,128)(2,1)S(1)}, u32[]{:S(2)}, u32[]{:S(2)}) collective-permute-start(bf16[128,1024]{1,0:T(8,128)(2,1)S(1)} %shard_map.53), channel_id=1, source_target_pairs={{0,16},{499,387},{4,20},{503,391},{8,24},{507,395},{12,28},{511,39... | collective-permute-start | bytes 786440 | tf_op jit(solution)/shard_map/ppermute | solution.py:222
  70.3 8.4 %copy-start.2 = (bf16[8,16,1024]{2,1,0:T(8,128)(2,1)S(1)}, bf16[8,16,1024]{2,1,0:T(8,128)(2,1)}, u32[]{:S(2)}) copy-start(bf16[8,16,1024]{2,1,0:T(8,128)(2,1)} %get-tuple-element.8.refs_4_) | copy-start | bytes 786436
  70.3 8.4 %collective-permute-start.1 = (bf16[128,1024]{1,0:T(8,128)(2,1)S(1)}, bf16[128,1024]{1,0:T(8,128)(2,1)S(1)}, u32[]{:S(2)}, u32[]{:S(2)}) collective-permute-start(bf16[128,1024]{1,0:T(8,128)(2,1)S(1)} %shard_map.52), channel_id=1, source_target_pairs={{0,128},{499,114},{4,132},{503,118},{8,136},{507,122},{12,140},{51... | collective-permute-start | bytes 786440 | tf_op jit(solution)/shard_map/ppermute | solution.py:222
  74.0 31.6 %copy-start.4 = (f32[1024,16]{0,1:T(8,128)S(1)}, f32[1024,16]{0,1:T(8,128)}, u32[]{:S(2)}) copy-start(f32[1024,16]{0,1:T(8,128)} %param.5) | copy-start | bytes 196612

commit v8 on v7

--- a/solution.py
+++ b/solution.py
@@ -32,11 +32,7 @@
 
 
 FAR_GROUPS = [
-    [
-        device(4 * (h ^ (yh & 1)) + 2 * zh + b, 2 * yh + a, blk)
-        for yh in range(4)
-        for zh in range(2)
-    ]
+    [device(4 * h + 2 * zh + b, 2 * yh + a, blk) for yh in range(4) for zh in range(2)]
     for blk in range(BLOCKS)
     for h in range(2)
     for a in range(2)
@@ -46,6 +42,15 @@
 
 COSETS = [
     FAR_GROUPS[8 * blk + k] + FAR_GROUPS[8 * blk + 4 + k] for blk in range(BLOCKS) for k in range(4)
+]
+
+
+SQUARES = [
+    [device(4 * h + 2 * zh + b, 2 * yh + a, blk) for a in range(2) for b in range(2)]
+    for blk in range(BLOCKS)
+    for h in range(2)
+    for yh in range(4)
+    for zh in range(2)
 ]
 
 
@@ -94,8 +99,7 @@
     core = lax.axis_index("blk") & 1
     z = (lax.axis_index("grp") * 4 + lax.axis_index("seq_0") + core) & 7
     y = (lax.axis_index("seq_1") + core) & 7
-    yh, zh, half = y >> 1, (z & 3) >> 1, z >> 2
-    return core, y & 1, z & 1, yh, zh, half ^ (yh & 1)
+    return core, y & 1, z & 1, y >> 1, (z & 3) >> 1, z >> 2
 
 
 def call(kernel, out_shape, in_specs, out_specs, *args, **more):
@@ -128,7 +132,7 @@
     for d, out_ref in enumerate(out_refs):
         for f in range(8):
             row, column = f >> 1, f & 1
-            z = 4 * (h ^ (row & 1)) + 2 * column + (b ^ (d & 1))
+            z = 4 * h + 2 * column + (b ^ (d & 1))
             y = 2 * row + (a ^ (d >> 1))
             z, y = (z + 8 - core) & 7, (y + 8 - core) & 7
             there = ((z & 3) * 8 + y) * 2 + (z >> 2)
@@ -143,33 +147,68 @@
     return call(pick_kernel, [shape] * 4, [vmem()], [hbm()] * 4, rows, scratch_shapes=scratch)
 
 
-def moment_kernel(rows_ref, x_ref, out_ref):
+def own_moment_kernel(rows_ref, far_x_ref, x_ref, out_ref, sems):
+    pieces = [pl.ds(k * 256, 256) for k in range(4)]
+    arriving = run_copies([(far_x_ref.at[piece], x_ref.at[piece]) for piece in pieces], sems)
+    rows = rows_ref[position()[5]]
+    total = jnp.zeros(out_ref.shape, f32)
+    for piece, copy in zip(pieces, arriving):
+        copy.wait()
+        x = x_ref[piece]
+        whitened = lax.dot_general(rows, x, ROWS_ROWS, preferred_element_type=f32)
+        total = total + jnp.dot(whitened.astype(bf16), x, preferred_element_type=f32)
+    out_ref[...] = total.astype(bf16)
+
+
+def own_moment(rows, x):
+    shapes = [
+        jax.ShapeDtypeStruct(x.shape, bf16),
+        jax.ShapeDtypeStruct(rows.shape[1:], bf16),
+    ]
+    x = pltpu.with_memory_space_constraint(x, pltpu.HBM)
+    scratch = [pltpu.SemaphoreType.DMA((4,))]
+    specs = [vmem(), hbm()]
+    return call(own_moment_kernel, shapes, specs, [vmem()] * 2, rows, x, scratch_shapes=scratch)
+
+
+def moments_kernel(x_ref, own_ref, *refs):
+    blocks, out_ref, rows = refs[:3], refs[3], refs[4]
+    _, a, b, _, _, h = position()
+    me = 2 * a + b
+    out_ref[me] = own_ref[...]
+    for k, block in enumerate(blocks):
+        rows[pl.ds(k * 128, 128)] = block[h]
     x = x_ref[...]
-    rows = rows_ref[position()[5]]
-    whitened = lax.dot_general(rows, x, ROWS_ROWS, preferred_element_type=f32)
-    out_ref[...] = jnp.dot(whitened.astype(bf16), x, preferred_element_type=f32).astype(bf16)
-
-
-def moment_of(rows, x):
-    shape = jax.ShapeDtypeStruct(rows.shape[1:], bf16)
-    return call(moment_kernel, shape, [vmem()] * 2, vmem(), rows, x)
-
-
-def join_kernel(*refs):
-    moments, gradients, out_ref = refs[:4], refs[4:8], refs[8]
+    whitened = lax.dot_general(rows[...], x, ROWS_ROWS, preferred_element_type=f32)
+    total = jnp.dot(whitened.astype(bf16), x, preferred_element_type=f32).astype(bf16)
+    for k in range(3):
+        out_ref[me ^ (k + 1)] = total[k * 128 : k * 128 + 128]
+
+
+def moments_of(x, own, blocks):
+    shape = jax.ShapeDtypeStruct((4,) + own.shape, bf16)
+    scratch = [pltpu.VMEM((3 * 128, x.shape[1]), bf16)]
+    return call(
+        moments_kernel, shape, [vmem()] * 5, vmem(), x, own, *blocks, scratch_shapes=scratch
+    )
+
+
+def join_kernel(moments_ref, *refs):
+    gradients, out_ref = refs[:4], refs[4]
     for f in range(8):
-        for first, parts in ((0, moments), (16, gradients)):
-            total = parts[0][f].astype(f32)
-            for part in parts[1:]:
-                total = total + part[f].astype(f32)
-            out_ref[f, first : first + 16] = total.astype(bf16)
+        total = moments_ref[0, f].astype(f32)
+        for k in range(1, 4):
+            total = total + moments_ref[k, f].astype(f32)
+        out_ref[f, :16] = total.astype(bf16)
+        total = gradients[0][f].astype(f32)
+        for part in gradients[1:]:
+            total = total + part[f].astype(f32)
+        out_ref[f, 16:] = total.astype(bf16)
 
 
 def join(moments, gradients):
-    width = gradients[0].shape[2]
-    moments = [m.reshape(8, 16, width) for m in moments]
-    shape = jax.ShapeDtypeStruct((8, 32, width), bf16)
-    return call(join_kernel, shape, [vmem()] * 8, vmem(), *moments, *gradients)
+    shape = jax.ShapeDtypeStruct((8, 32, moments.shape[3]), bf16)
+    return call(join_kernel, shape, [vmem()] * 5, vmem(), moments, *gradients)
 
 
 def finish_kernel(tokens, *refs):
@@ -235,10 +274,10 @@
     near = [mine]
     for d in (1, 2, 3):
         near.append(turn(mine, INNER[d]))
-    moments = [moment_of(mine, activations)]
-    for d in (1, 2, 3):
-        moment = moment_of(near[d], activations)
-        moments.append(turn(moment, INNER[d]))
+    x, moment = own_moment(mine, activations)
+    moments = moments_of(x, moment, near[1:])
+    moments, *gradients = lax.optimization_barrier((moments, *gradients))
+    moments = exchange(moments, SQUARES).reshape(4, 8, owned, width)
     joined = join(moments, gradients)
     sums = exchange(joined, FAR_GROUPS)
 

time: 110 us -> 106 us (0.964)
  blocking collectives: 60.4 us -> 70.6 us
  starting transfers between devices: 27.8 us -> 18.4 us
  waiting for transfers between devices: 4.65 us -> 0.39 us
    all_to_all x2 -> x3, blocking collectives: 60.4 us -> 70.6 us  [exchange(): lax.all_to_all(blocks, PLANES, split_axis=0, concat_axis=0, tiled=True, a...]
    ppermute x9 -> x6, starting transfers between devices: 27.8 us -> 18.4 us  [turn(): return lax.ppermute(block, PLANES, pairs)]
    ppermute x9 -> x6, waiting for transfers between devices: 4.65 us -> 0.39 us  [turn(): return lax.ppermute(block, PLANES, pairs)]
    pallas_call x8 -> x6, Pallas kernels: 9.16 us -> 9.71 us  [call(): pl.pallas_call(kernel, out_shape=out_shape, in_specs=in_specs, out_specs=...]
  transfers between devices with their start and end apart: 9 -> 6, of which waited for: 1 -> 1; matrix products, arithmetic and copies ran while one was open for 4% -> 4% of each run, Pallas kernels for 5% -> 6%
where the time goes in v8:
time: 106 us; the launch traced here: 105 us
  blocking collectives  70.6 us (67%)
  starting transfers between devices  18.4 us (17%)
  Pallas kernels  9.71 us (9%)
  matrix products  3.98 us (4%)
    all_to_all x3, blocking collectives, exchange(): lax.all_to_all(blocks, PLANES, split_axis=0, concat_axis=0, tiled=True, a...  70.6 us
    ppermute x6, starting transfers between devices, turn(): return lax.ppermute(block, PLANES, pairs)  18.4 us
    pallas_call x6, Pallas kernels, call(): pl.pallas_call(kernel, out_shape=out_shape, in_specs=in_specs, out_specs=...  9.71 us
    dot_general x1, matrix products, on_device(): lax.dot_general(cotangent, activations, TOKENS_FIRST, preferred_element_t...  3.98 us
  transfers between devices with their start and end apart: 6, of which 1 were waited for; matrix products, arithmetic and copies ran while one was open for 4% of the time, Pallas kernels for 6%

profile of v8, /device:TPU:6, one launch (start us, length us, event | category | flops | bytes accessed | tf_op | source)
XLA Modules:
  0.0 104.9 jit_solution(3779395114761595577)
XLA Ops:
  0.6 0.0 copy-start
  0.6 0.0 copy-start.2
  0.7 1.0 copy-done.2
  1.6 1.0 shard_map.50
  2.6 34.1 %all_to_all.15 = bf16[16,16,1024]{2,1,0:T(8,128)(2,1)S(1)} all-to-all(bf16[16,16,1024]{2,1,0:T(8,128)(2,1)} %shard_map.50), channel_id=1, replica_groups={{0,256,32,288,64,320,96,352,1,257,33,289,65,321,97,353},{128,384,160,41..., dimensions={0} | all-to-all | bytes 1048576 | tf_op jit(solution)/shard_map/all_to_all | solution.py:78
  36.7 3.0 %collective-permute-start = (bf16[2,128,1024]{2,1,0:T(8,128)(2,1)S(1)}, bf16[2,128,1024]{2,1,0:T(8,128)(2,1)S(1)}, u32[]{:S(2)}, u32[]{:S(2)}) collective-permute-start(bf16[2,128,1024]{2,1,0:T(8,128)(2,1)S(1)} %bitcast.12), channel_id=1, source_target_pairs={{0,128},{499,114},{4,132},{503,118},{8,136},{507,122},{12,140},{51... | collective-permute-start | bytes 1572872 | tf_op jit(solution)/shard_map/ppermute | solution.py:261
  39.7 1.9 %collective-permute-start.1 = (bf16[2,128,1024]{2,1,0:T(8,128)(2,1)S(1)}, bf16[2,128,1024]{2,1,0:T(8,128)(2,1)S(1)}, u32[]{:S(2)}, u32[]{:S(2)}) collective-permute-start(bf16[2,128,1024]{2,1,0:T(8,128)(2,1)S(1)} %bitcast.13), channel_id=1, source_target_pairs={{0,16},{499,387},{4,20},{503,391},{8,24},{507,395},{12,28},{511,39... | collective-permute-start | bytes 1572872 | tf_op jit(solution)/shard_map/ppermute | solution.py:261
  41.7 4.3 %collective-permute-start.2 = (bf16[2,128,1024]{2,1,0:T(8,128)(2,1)S(1)}, bf16[2,128,1024]{2,1,0:T(8,128)(2,1)S(1)}, u32[]{:S(2)}, u32[]{:S(2)}) collective-permute-start(bf16[2,128,1024]{2,1,0:T(8,128)(2,1)S(1)} %bitcast.14), channel_id=1, source_target_pairs={{0,144},{499,2},{4,148},{503,6},{8,152},{507,10},{12,156},{511,14}... | collective-permute-start | bytes 1572872 | tf_op jit(solution)/shard_map/ppermute | solution.py:261
  45.9 0.0 copy-done
  45.9 4.0 %convolution_convert_fusion = bf16[1024,1024]{1,0:T(8,128)(2,1)S(1)} fusion(bf16[1024,1024]{1,0:T(8,128)(2,1)S(1)} %copy-done, bf16[1024,1024]{1,0:T(8,128)(2,1)} %far_x_ref.1), kind=kOutput, calls=%fused_computation | convolution fusion | flops 2148532224 | bytes 6291456 | tf_op jit(solution)/shard_map/dot_general | solution.py:266
  49.9 1.3 %shard_map.53 = (bf16[8,16,1024]{2,1,0:T(8,128)(2,1)}, bf16[8,16,1024]{2,1,0:T(8,128)(2,1)}, bf16[8,16,1024]{2,1,0:T(8,128)(2,1)}, bf16[8,16,1024]{2,1,0:T(8,128)(2,1)}) custom-call(bf16[64,16,1024]{2,1,0:T(8,128)(2,1)S(1)} %bitcast.18), custom_call_target="tpu_custom_call" | custom-call | tf_op jit(solution)/shard_map/pallas_call | solution.py:106
  51.2 3.0 %collective-permute-start.3 = (bf16[8,16,1024]{2,1,0:T(8,128)(2,1)}, bf16[8,16,1024]{2,1,0:T(8,128)(2,1)S(1)}, u32[]{:S(2)}, u32[]{:S(2)}) collective-permute-start(bf16[8,16,1024]{2,1,0:T(8,128)(2,1)} %get-tuple-element.18), channel_id=1, source_target_pairs={{0,128},{499,114},{4,132},{503,118},{8,136},{507,122},{12,140},{51... | collective-permute-start | bytes 786440 | tf_op jit(solution)/shard_map/ppermute | solution.py:261
  54.3 1.9 %collective-permute-start.4 = (bf16[8,16,1024]{2,1,0:T(8,128)(2,1)}, bf16[8,16,1024]{2,1,0:T(8,128)(2,1)S(1)}, u32[]{:S(2)}, u32[]{:S(2)}) collective-permute-start(bf16[8,16,1024]{2,1,0:T(8,128)(2,1)} %get-tuple-element.19), channel_id=1, source_target_pairs={{0,16},{499,387},{4,20},{503,391},{8,24},{507,395},{12,28},{511,39... | collective-permute-start | bytes 786440 | tf_op jit(solution)/shard_map/ppermute | solution.py:261
  56.2 0.0 collective-permute-done.refs_0_
  56.2 4.3 %collective-permute-start.5 = (bf16[8,16,1024]{2,1,0:T(8,128)(2,1)}, bf16[8,16,1024]{2,1,0:T(8,128)(2,1)S(1)}, u32[]{:S(2)}, u32[]{:S(2)}) collective-permute-start(bf16[8,16,1024]{2,1,0:T(8,128)(2,1)} %get-tuple-element.20), channel_id=1, source_target_pairs={{0,144},{499,2},{4,148},{503,6},{8,152},{507,10},{12,156},{511,14}... | collective-permute-start | bytes 786440 | tf_op jit(solution)/shard_map/ppermute | solution.py:261
  60.5 3.1 %shard_map.51 = (bf16[1024,1024]{1,0:T(8,128)(2,1)S(1)}, bf16[128,1024]{1,0:T(8,128)(2,1)S(1)}) custom-call(bf16[2,128,1024]{2,1,0:T(8,128)(2,1)S(1)} %bitcast.15, bf16[1024,1024]{1,0:T(8,128)(2,1)} %far_x_ref.1), custom_call_target="tpu_custom_call" | custom-call | tf_op jit(solution)/shard_map/pallas_call | solution.py:106
  63.6 0.0 collective-permute-done.1.refs_1_
  63.6 0.0 collective-permute-done.2.refs_2_
  63.6 1.8 %shard_map.52 = bf16[4,128,1024]{2,1,0:T(8,128)(2,1)S(1)} custom-call(bf16[1024,1024]{1,0:T(8,128)(2,1)S(1)} %get-tuple-element.15.x_ref, bf16[128,1024]{1,0:T(8,128)(2,1)S(1)} %get-tuple-element.16.own_ref, bf16[2,128,1024]{2,1,0:T(8,128)(2,1)S(1)} %collective-permute-done.refs_0_, bf16[2,128,1024]{2,1,0:T(8,128)(2,1)S(1)} %collective-permute-done.1.refs_1_, ...), custom_call_target="tpu_custom_call" | custom-call | tf_op jit(solution)/shard_map/pallas_call | solution.py:106
  65.5 0.0 copy-start.1
  65.5 0.0 collective-permute-done.3.refs_1_
  65.5 0.0 collective-permute-done.4.refs_2_
  65.5 0.4 collective-permute-done.5.refs_3_
  65.9 13.0 %all_to_all.16 = bf16[4,128,1024]{2,1,0:T(8,128)(2,1)S(1)} all-to-all(bf16[4,128,1024]{2,1,0:T(8,128)(2,1)S(1)} %shard_map.52), channel_id=1, replica_groups={{0,128,16,144},{256,384,272,400},{32,160,48,176},{288,416,304,432},{64,..., dimensions={0} | all-to-all | bytes 2097152 | tf_op jit(solution)/shard_map/all_to_all | solution.py:78
  78.9 0.0 copy-start.3
  78.9 0.0 copy-done.1
  78.9 0.3 shard_map.54
  79.2 23.5 %all_to_all.17.refs_0_ = bf16[8,32,1024]{2,1,0:T(8,128)(2,1)S(1)} all-to-all(bf16[8,32,1024]{2,1,0:T(8,128)(2,1)S(1)} %shard_map.54), channel_id=1, replica_groups={{0,256,32,288,64,320,96,352},{128,384,160,416,192,448,224,480},{16,272,..., dimensions={0} | all-to-all | bytes 1048576 | tf_op jit(solution)/shard_map/all_to_all | solution.py:78
  102.6 0.0 copy-done.3
  102.6 2.2 %shard_map.55 = (f32[16,1024]{1,0:T(8,128)}, f32[16,1024]{1,0:T(8,128)}) custom-call(bf16[8,32,1024]{2,1,0:T(8,128)(2,1)S(1)} %all_to_all.17.refs_0_, f32[16,1024]{1,0:T(8,128)S(1)} %bitcast.23, bf16[256,1024]{1,0:T(8,128)(2,1)S(1)} %bitcast.16, bf16[256,1024]{1,0:T(8,128)(2,1)S(1)} %bitcast.19, bf16[256,1024]{1,0:T(8,128)(2,1)S(1)} %bitcast.20, ...), custom_call_target="tpu_custom_call" | custom-call | tf_op jit(solution)/shard_map/pallas_call | solution.py:106
Async XLA Ops:
  0.6 45.3 %copy-start = (bf16[1024,1024]{1,0:T(8,128)(2,1)S(1)}, bf16[1024,1024]{1,0:T(8,128)(2,1)}, u32[]{:S(2)}) copy-start(bf16[1024,1024]{1,0:T(8,128)(2,1)} %param.4) | copy-start | bytes 6291460
  0.6 1.0 copy-start.2
  36.7 19.5 %collective-permute-start = (bf16[2,128,1024]{2,1,0:T(8,128)(2,1)S(1)}, bf16[2,128,1024]{2,1,0:T(8,128)(2,1)S(1)}, u32[]{:S(2)}, u32[]{:S(2)}) collective-permute-start(bf16[2,128,1024]{2,1,0:T(8,128)(2,1)S(1)} %bitcast.12), channel_id=1, source_target_pairs={{0,128},{499,114},{4,132},{503,118},{8,136},{507,122},{12,140},{51... | collective-permute-start | bytes 1572872 | tf_op jit(solution)/shard_map/ppermute | solution.py:261
  39.7 23.9 %collective-permute-start.1 = (bf16[2,128,1024]{2,1,0:T(8,128)(2,1)S(1)}, bf16[2,128,1024]{2,1,0:T(8,128)(2,1)S(1)}, u32[]{:S(2)}, u32[]{:S(2)}) collective-permute-start(bf16[2,128,1024]{2,1,0:T(8,128)(2,1)S(1)} %bitcast.13), channel_id=1, source_target_pairs={{0,16},{499,387},{4,20},{503,391},{8,24},{507,395},{12,28},{511,39... | collective-permute-start | bytes 1572872 | tf_op jit(solution)/shard_map/ppermute | solution.py:261
  41.7 22.0 %collective-permute-start.2 = (bf16[2,128,1024]{2,1,0:T(8,128)(2,1)S(1)}, bf16[2,128,1024]{2,1,0:T(8,128)(2,1)S(1)}, u32[]{:S(2)}, u32[]{:S(2)}) collective-permute-start(bf16[2,128,1024]{2,1,0:T(8,128)(2,1)S(1)} %bitcast.14), channel_id=1, source_target_pairs={{0,144},{499,2},{4,148},{503,6},{8,152},{507,10},{12,156},{511,14}... | collective-permute-start | bytes 1572872 | tf_op jit(solution)/shard_map/ppermute | solution.py:261
  51.2 14.3 %collective-permute-start.3 = (bf16[8,16,1024]{2,1,0:T(8,128)(2,1)}, bf16[8,16,1024]{2,1,0:T(8,128)(2,1)S(1)}, u32[]{:S(2)}, u32[]{:S(2)}) collective-permute-start(bf16[8,16,1024]{2,1,0:T(8,128)(2,1)} %get-tuple-element.18), channel_id=1, source_target_pairs={{0,128},{499,114},{4,132},{503,118},{8,136},{507,122},{12,140},{51... | collective-permute-start | bytes 786440 | tf_op jit(solution)/shard_map/ppermute | solution.py:261
  54.3 11.2 %collective-permute-start.4 = (bf16[8,16,1024]{2,1,0:T(8,128)(2,1)}, bf16[8,16,1024]{2,1,0:T(8,128)(2,1)S(1)}, u32[]{:S(2)}, u32[]{:S(2)}) collective-permute-start(bf16[8,16,1024]{2,1,0:T(8,128)(2,1)} %get-tuple-element.19), channel_id=1, source_target_pairs={{0,16},{499,387},{4,20},{503,391},{8,24},{507,395},{12,28},{511,39... | collective-permute-start | bytes 786440 | tf_op jit(solution)/shard_map/ppermute | solution.py:261
  56.2 9.7 %collective-permute-start.5 = (bf16[8,16,1024]{2,1,0:T(8,128)(2,1)}, bf16[8,16,1024]{2,1,0:T(8,128)(2,1)S(1)}, u32[]{:S(2)}, u32[]{:S(2)}) collective-permute-start(bf16[8,16,1024]{2,1,0:T(8,128)(2,1)} %get-tuple-element.20), channel_id=1, source_target_pairs={{0,144},{499,2},{4,148},{503,6},{8,152},{507,10},{12,156},{511,14}... | collective-permute-start | bytes 786440 | tf_op jit(solution)/shard_map/ppermute | solution.py:261
  65.5 13.4 %copy-start.1 = (bf16[8,16,1024]{2,1,0:T(8,128)(2,1)S(1)}, bf16[8,16,1024]{2,1,0:T(8,128)(2,1)}, u32[]{:S(2)}) copy-start(bf16[8,16,1024]{2,1,0:T(8,128)(2,1)} %get-tuple-element.22.refs_0_) | copy-start | bytes 786436
  78.9 23.7 %copy-start.3 = (f32[1024,16]{0,1:T(8,128)S(1)}, f32[1024,16]{0,1:T(8,128)}, u32[]{:S(2)}) copy-start(f32[1024,16]{0,1:T(8,128)} %param.5) | copy-start | bytes 196612

commit v9 on v7

--- a/solution.py
+++ b/solution.py
@@ -32,11 +32,7 @@
 
 
 FAR_GROUPS = [
-    [
-        device(4 * (h ^ (yh & 1)) + 2 * zh + b, 2 * yh + a, blk)
-        for yh in range(4)
-        for zh in range(2)
-    ]
+    [device(4 * h + 2 * zh + b, 2 * yh + a, blk) for yh in range(4) for zh in range(2)]
     for blk in range(BLOCKS)
     for h in range(2)
     for a in range(2)
@@ -94,8 +90,7 @@
     core = lax.axis_index("blk") & 1
     z = (lax.axis_index("grp") * 4 + lax.axis_index("seq_0") + core) & 7
     y = (lax.axis_index("seq_1") + core) & 7
-    yh, zh, half = y >> 1, (z & 3) >> 1, z >> 2
-    return core, y & 1, z & 1, yh, zh, half ^ (yh & 1)
+    return core, y & 1, z & 1, y >> 1, (z & 3) >> 1, z >> 2
 
 
 def call(kernel, out_shape, in_specs, out_specs, *args, **more):
@@ -109,16 +104,25 @@
     )(*args)
 
 
-def spread_kernel(own_ref, out_ref, low, sems):
-    low[...] = own_ref[...].astype(bf16)
+def spread_kernel(far_own_ref, out_ref, own, low, sem, sems):
+    arriving = pltpu.make_async_copy(far_own_ref, own, sem)
+    arriving.start()
+    arriving.wait()
+    low[...] = own[...].astype(bf16)
     for copy in run_copies([(low, out_ref.at[k]) for k in range(out_ref.shape[0])], sems):
         copy.wait()
 
 
 def spread(own, count):
+    own = pltpu.with_memory_space_constraint(own, pltpu.HBM)
     shape = pltpu.HBM((count,) + own.shape, bf16)
-    scratch = [pltpu.VMEM(own.shape, bf16), pltpu.SemaphoreType.DMA((count,))]
-    return call(spread_kernel, shape, [vmem()], hbm(), own, scratch_shapes=scratch)
+    scratch = [
+        pltpu.VMEM(own.shape, f32),
+        pltpu.VMEM(own.shape, bf16),
+        pltpu.SemaphoreType.DMA,
+        pltpu.SemaphoreType.DMA((count,)),
+    ]
+    return call(spread_kernel, shape, [hbm()], hbm(), own, scratch_shapes=scratch)
 
 
 def pick_kernel(rows_ref, *refs):
@@ -128,7 +132,7 @@
     for d, out_ref in enumerate(out_refs):
         for f in range(8):
             row, column = f >> 1, f & 1
-            z = 4 * (h ^ (row & 1)) + 2 * column + (b ^ (d & 1))
+            z = 4 * h + 2 * column + (b ^ (d & 1))
             y = 2 * row + (a ^ (d >> 1))
             z, y = (z + 8 - core) & 7, (y + 8 - core) & 7
             there = ((z & 3) * 8 + y) * 2 + (z >> 2)

time: 110 us -> 105 us (0.955)
  the two profiles are of different devices: /device:TPU:6 before, /device:TPU:65 now
where the time goes in v9:
time: 105 us; the launch traced here: 104 us
  blocking collectives  54.9 us (52%)
  starting transfers between devices  29.9 us (28%)
  Pallas kernels  10.2 us (10%)
  waiting for transfers between devices  4.33 us (4%)
  matrix products  3.98 us (4%)
    all_to_all x2, blocking collectives, exchange(): lax.all_to_all(blocks, PLANES, split_axis=0, concat_axis=0, tiled=True, a...  54.9 us
    ppermute x9, starting transfers between devices, turn(): return lax.ppermute(block, PLANES, pairs)  29.9 us
    pallas_call x8, Pallas kernels, call(): pl.pallas_call(kernel, out_shape=out_shape, in_specs=in_specs, out_specs=...  10.2 us
    ppermute x9, waiting for transfers between devices, turn(): return lax.ppermute(block, PLANES, pairs)  4.33 us
    dot_general x1, matrix products, on_device(): lax.dot_general(cotangent, activations, TOKENS_FIRST, preferred_element_t...  3.98 us
  transfers between devices with their start and end apart: 9, of which 1 were waited for; matrix products, arithmetic and copies ran while one was open for 4% of the time, Pallas kernels for 6%

profile of v9, /device:TPU:65, one launch (start us, length us, event | category | flops | bytes accessed | tf_op | source)
XLA Modules:
  0.0 104.3 jit_solution(12362736313991177302)
XLA Ops:
  0.6 0.0 copy-start
  0.6 1.9 %shard_map.50 = bf16[16,16,1024]{2,1,0:T(8,128)(2,1)} custom-call(f32[16,1024]{1,0:T(8,128)} %bitcast.28), custom_call_target="tpu_custom_call" | custom-call | tf_op jit(solution)/shard_map/pallas_call | solution.py:97
  2.6 30.0 %all_to_all.10 = bf16[16,16,1024]{2,1,0:T(8,128)(2,1)S(1)} all-to-all(bf16[16,16,1024]{2,1,0:T(8,128)(2,1)} %shard_map.50), channel_id=1, replica_groups={{0,256,32,288,64,320,96,352,1,257,33,289,65,321,97,353},{128,384,160,41..., dimensions={0} | all-to-all | bytes 1048576 | tf_op jit(solution)/shard_map/all_to_all | solution.py:69
  32.6 3.4 %collective-permute-start.4 = (bf16[2,128,1024]{2,1,0:T(8,128)(2,1)S(1)}, bf16[2,128,1024]{2,1,0:T(8,128)(2,1)S(1)}, u32[]{:S(2)}, u32[]{:S(2)}) collective-permute-start(bf16[2,128,1024]{2,1,0:T(8,128)(2,1)S(1)} %bitcast.15), channel_id=1, source_target_pairs={{0,144},{499,2},{4,148},{503,6},{8,152},{507,10},{12,156},{511,14}... | collective-permute-start | bytes 1572872 | tf_op jit(solution)/shard_map/ppermute | solution.py:226
  36.0 5.3 %collective-permute-start.2 = (bf16[2,128,1024]{2,1,0:T(8,128)(2,1)S(1)}, bf16[2,128,1024]{2,1,0:T(8,128)(2,1)S(1)}, u32[]{:S(2)}, u32[]{:S(2)}) collective-permute-start(bf16[2,128,1024]{2,1,0:T(8,128)(2,1)S(1)} %bitcast.16), channel_id=1, source_target_pairs={{0,16},{499,387},{4,20},{503,391},{8,24},{507,395},{12,28},{511,39... | collective-permute-start | bytes 1572872 | tf_op jit(solution)/shard_map/ppermute | solution.py:226
  41.4 1.9 %collective-permute-start = (bf16[2,128,1024]{2,1,0:T(8,128)(2,1)S(1)}, bf16[2,128,1024]{2,1,0:T(8,128)(2,1)S(1)}, u32[]{:S(2)}, u32[]{:S(2)}) collective-permute-start(bf16[2,128,1024]{2,1,0:T(8,128)(2,1)S(1)} %bitcast.17), channel_id=1, source_target_pairs={{0,128},{499,114},{4,132},{503,118},{8,136},{507,122},{12,140},{51... | collective-permute-start | bytes 1572872 | tf_op jit(solution)/shard_map/ppermute | solution.py:226
  43.3 4.0 %convolution_convert_fusion = bf16[1024,1024]{1,0:T(8,128)(2,1)S(1)} fusion(bf16[1024,1024]{1,0:T(8,128)(2,1)S(1)} %copy-done, bf16[1024,1024]{1,0:T(8,128)(2,1)} %x_ref.7), kind=kOutput, calls=%fused_computation | convolution fusion | flops 2148532224 | bytes 6291456 | tf_op jit(solution)/shard_map/dot_general | solution.py:231
  47.3 0.0 copy-start.1
  47.3 1.3 %shard_map.55 = (bf16[8,16,1024]{2,1,0:T(8,128)(2,1)}, bf16[8,16,1024]{2,1,0:T(8,128)(2,1)}, bf16[8,16,1024]{2,1,0:T(8,128)(2,1)}, bf16[8,16,1024]{2,1,0:T(8,128)(2,1)}) custom-call(bf16[64,16,1024]{2,1,0:T(8,128)(2,1)S(1)} %bitcast.20), custom_call_target="tpu_custom_call" | custom-call | tf_op jit(solution)/shard_map/pallas_call | solution.py:97
  48.6 3.4 %collective-permute-start.6 = (bf16[8,16,1024]{2,1,0:T(8,128)(2,1)}, bf16[8,16,1024]{2,1,0:T(8,128)(2,1)S(1)}, u32[]{:S(2)}, u32[]{:S(2)}) collective-permute-start(bf16[8,16,1024]{2,1,0:T(8,128)(2,1)} %get-tuple-element.9), channel_id=1, source_target_pairs={{0,128},{499,114},{4,132},{503,118},{8,136},{507,122},{12,140},{51... | collective-permute-start | bytes 786440 | tf_op jit(solution)/shard_map/ppermute | solution.py:226
  52.0 1.9 %collective-permute-start.7 = (bf16[8,16,1024]{2,1,0:T(8,128)(2,1)}, bf16[8,16,1024]{2,1,0:T(8,128)(2,1)S(1)}, u32[]{:S(2)}, u32[]{:S(2)}) collective-permute-start(bf16[8,16,1024]{2,1,0:T(8,128)(2,1)} %get-tuple-element.10), channel_id=1, source_target_pairs={{0,16},{499,387},{4,20},{503,391},{8,24},{507,395},{12,28},{511,39... | collective-permute-start | bytes 786440 | tf_op jit(solution)/shard_map/ppermute | solution.py:226
  53.9 0.0 collective-permute-done.4.rows_ref
  53.9 4.3 %collective-permute-start.8 = (bf16[8,16,1024]{2,1,0:T(8,128)(2,1)}, bf16[8,16,1024]{2,1,0:T(8,128)(2,1)S(1)}, u32[]{:S(2)}, u32[]{:S(2)}) collective-permute-start(bf16[8,16,1024]{2,1,0:T(8,128)(2,1)} %get-tuple-element.11), channel_id=1, source_target_pairs={{0,144},{499,2},{4,148},{503,6},{8,152},{507,10},{12,156},{511,14}... | collective-permute-start | bytes 786440 | tf_op jit(solution)/shard_map/ppermute | solution.py:226
  58.2 1.1 %shard_map.54 = bf16[128,1024]{1,0:T(8,128)(2,1)S(1)} custom-call(bf16[2,128,1024]{2,1,0:T(8,128)(2,1)S(1)} %collective-permute-done.4.rows_ref, bf16[1024,1024]{1,0:T(8,128)(2,1)S(1)} %copy-done.1), custom_call_target="tpu_custom_call" | custom-call | tf_op jit(solution)/shard_map/pallas_call | solution.py:97
  59.3 0.0 collective-permute-done.2.rows_ref
  59.4 3.1 %collective-permute-start.5 = (bf16[128,1024]{1,0:T(8,128)(2,1)S(1)}, bf16[128,1024]{1,0:T(8,128)(2,1)S(1)}, u32[]{:S(2)}, u32[]{:S(2)}) collective-permute-start(bf16[128,1024]{1,0:T(8,128)(2,1)S(1)} %shard_map.54), channel_id=1, source_target_pairs={{0,144},{499,2},{4,148},{503,6},{8,152},{507,10},{12,156},{511,14}... | collective-permute-start | bytes 786440 | tf_op jit(solution)/shard_map/ppermute | solution.py:226
  62.5 1.1 %shard_map.53 = bf16[128,1024]{1,0:T(8,128)(2,1)S(1)} custom-call(bf16[2,128,1024]{2,1,0:T(8,128)(2,1)S(1)} %collective-permute-done.2.rows_ref, bf16[1024,1024]{1,0:T(8,128)(2,1)S(1)} %copy-done.1), custom_call_target="tpu_custom_call" | custom-call | tf_op jit(solution)/shard_map/pallas_call | solution.py:97
  63.6 0.0 collective-permute-done.rows_ref
  63.6 4.6 %collective-permute-start.3 = (bf16[128,1024]{1,0:T(8,128)(2,1)S(1)}, bf16[128,1024]{1,0:T(8,128)(2,1)S(1)}, u32[]{:S(2)}, u32[]{:S(2)}) collective-permute-start(bf16[128,1024]{1,0:T(8,128)(2,1)S(1)} %shard_map.53), channel_id=1, source_target_pairs={{0,16},{499,387},{4,20},{503,391},{8,24},{507,395},{12,28},{511,39... | collective-permute-start | bytes 786440 | tf_op jit(solution)/shard_map/ppermute | solution.py:226
  68.2 1.1 %shard_map.52 = bf16[128,1024]{1,0:T(8,128)(2,1)S(1)} custom-call(bf16[2,128,1024]{2,1,0:T(8,128)(2,1)S(1)} %collective-permute-done.rows_ref, bf16[1024,1024]{1,0:T(8,128)(2,1)S(1)} %copy-done.1), custom_call_target="tpu_custom_call" | custom-call | tf_op jit(solution)/shard_map/pallas_call | solution.py:97
  69.3 0.0 collective-permute-done.6.refs_5_
  69.3 2.1 %collective-permute-start.1 = (bf16[128,1024]{1,0:T(8,128)(2,1)S(1)}, bf16[128,1024]{1,0:T(8,128)(2,1)S(1)}, u32[]{:S(2)}, u32[]{:S(2)}) collective-permute-start(bf16[128,1024]{1,0:T(8,128)(2,1)S(1)} %shard_map.52), channel_id=1, source_target_pairs={{0,128},{499,114},{4,132},{503,118},{8,136},{507,122},{12,140},{51... | collective-permute-start | bytes 786440 | tf_op jit(solution)/shard_map/ppermute | solution.py:226
  71.4 1.1 %shard_map.51 = bf16[128,1024]{1,0:T(8,128)(2,1)S(1)} custom-call(bf16[2,128,1024]{2,1,0:T(8,128)(2,1)S(1)} %bitcast.18, bf16[1024,1024]{1,0:T(8,128)(2,1)S(1)} %copy-done.1), custom_call_target="tpu_custom_call" | custom-call | tf_op jit(solution)/shard_map/pallas_call | solution.py:97
  72.5 0.0 copy-start.3
  72.5 0.0 collective-permute-done.7.refs_6_
  72.5 0.0 collective-permute-done.8.refs_7_
  72.5 0.0 collective-permute-done.5
  72.5 0.0 collective-permute-done.3
  72.5 4.3 %collective-permute-done.1 = bf16[128,1024]{1,0:T(8,128)(2,1)S(1)} collective-permute-done((bf16[128,1024]{1,0:T(8,128)(2,1)S(1)}, bf16[128,1024]{1,0:T(8,128)(2,1)S(1)}, u32[]{:S(2)}, u32[]{:S(2)}) %collective-permute-start.1) | collective-permute-done | bytes 262176 | tf_op jit(solution)/shard_map/ppermute | solution.py:226
  76.9 0.3 shard_map.56
  77.1 24.9 %all_to_all.11.refs_0_ = bf16[8,32,1024]{2,1,0:T(8,128)(2,1)S(1)} all-to-all(bf16[8,32,1024]{2,1,0:T(8,128)(2,1)S(1)} %shard_map.56), channel_id=1, replica_groups={{0,256,32,288,64,320,96,352},{128,384,160,416,192,448,224,480},{16,272,..., dimensions={0} | all-to-all | bytes 1048576 | tf_op jit(solution)/shard_map/all_to_all | solution.py:69
  102.0 2.2 %shard_map.57 = (f32[16,1024]{1,0:T(8,128)}, f32[16,1024]{1,0:T(8,128)}) custom-call(bf16[8,32,1024]{2,1,0:T(8,128)(2,1)S(1)} %all_to_all.11.refs_0_, f32[16,1024]{1,0:T(8,128)S(1)} %bitcast.29, bf16[256,1024]{1,0:T(8,128)(2,1)S(1)} %bitcast.19, bf16[256,1024]{1,0:T(8,128)(2,1)S(1)} %bitcast.23, bf16[256,1024]{1,0:T(8,128)(2,1)S(1)} %bitcast.22, ...), custom_call_target="tpu_custom_call" | custom-call | tf_op jit(solution)/shard_map/pallas_call | solution.py:97
  (5 shorter events, 0.0 us)
Async XLA Ops:
  0.6 42.7 %copy-start = (bf16[1024,1024]{1,0:T(8,128)(2,1)S(1)}, bf16[1024,1024]{1,0:T(8,128)(2,1)}, u32[]{:S(2)}) copy-start(bf16[1024,1024]{1,0:T(8,128)(2,1)} %param.4) | copy-start | bytes 6291460
  32.6 21.3 %collective-permute-start.4 = (bf16[2,128,1024]{2,1,0:T(8,128)(2,1)S(1)}, bf16[2,128,1024]{2,1,0:T(8,128)(2,1)S(1)}, u32[]{:S(2)}, u32[]{:S(2)}) collective-permute-start(bf16[2,128,1024]{2,1,0:T(8,128)(2,1)S(1)} %bitcast.15), channel_id=1, source_target_pairs={{0,144},{499,2},{4,148},{503,6},{8,152},{507,10},{12,156},{511,14}... | collective-permute-start | bytes 1572872 | tf_op jit(solution)/shard_map/ppermute | solution.py:226
  36.0 23.3 %collective-permute-start.2 = (bf16[2,128,1024]{2,1,0:T(8,128)(2,1)S(1)}, bf16[2,128,1024]{2,1,0:T(8,128)(2,1)S(1)}, u32[]{:S(2)}, u32[]{:S(2)}) collective-permute-start(bf16[2,128,1024]{2,1,0:T(8,128)(2,1)S(1)} %bitcast.16), channel_id=1, source_target_pairs={{0,16},{499,387},{4,20},{503,391},{8,24},{507,395},{12,28},{511,39... | collective-permute-start | bytes 1572872 | tf_op jit(solution)/shard_map/ppermute | solution.py:226
  41.4 22.2 %collective-permute-start = (bf16[2,128,1024]{2,1,0:T(8,128)(2,1)S(1)}, bf16[2,128,1024]{2,1,0:T(8,128)(2,1)S(1)}, u32[]{:S(2)}, u32[]{:S(2)}) collective-permute-start(bf16[2,128,1024]{2,1,0:T(8,128)(2,1)S(1)} %bitcast.17), channel_id=1, source_target_pairs={{0,128},{499,114},{4,132},{503,118},{8,136},{507,122},{12,140},{51... | collective-permute-start | bytes 1572872 | tf_op jit(solution)/shard_map/ppermute | solution.py:226
  47.3 10.9 %copy-start.1 = (bf16[1024,1024]{1,0:T(8,128)(2,1)S(1)}, bf16[1024,1024]{1,0:T(8,128)(2,1)}, u32[]{:S(2)}) copy-start(bf16[1024,1024]{1,0:T(8,128)(2,1)} %x_ref.7) | copy-start | bytes 6291460
  48.6 20.7 %collective-permute-start.6 = (bf16[8,16,1024]{2,1,0:T(8,128)(2,1)}, bf16[8,16,1024]{2,1,0:T(8,128)(2,1)S(1)}, u32[]{:S(2)}, u32[]{:S(2)}) collective-permute-start(bf16[8,16,1024]{2,1,0:T(8,128)(2,1)} %get-tuple-element.9), channel_id=1, source_target_pairs={{0,128},{499,114},{4,132},{503,118},{8,136},{507,122},{12,140},{51... | collective-permute-start | bytes 786440 | tf_op jit(solution)/shard_map/ppermute | solution.py:226
  52.0 20.5 %collective-permute-start.7 = (bf16[8,16,1024]{2,1,0:T(8,128)(2,1)}, bf16[8,16,1024]{2,1,0:T(8,128)(2,1)S(1)}, u32[]{:S(2)}, u32[]{:S(2)}) collective-permute-start(bf16[8,16,1024]{2,1,0:T(8,128)(2,1)} %get-tuple-element.10), channel_id=1, source_target_pairs={{0,16},{499,387},{4,20},{503,391},{8,24},{507,395},{12,28},{511,39... | collective-permute-start | bytes 786440 | tf_op jit(solution)/shard_map/ppermute | solution.py:226
  53.9 18.6 %collective-permute-start.8 = (bf16[8,16,1024]{2,1,0:T(8,128)(2,1)}, bf16[8,16,1024]{2,1,0:T(8,128)(2,1)S(1)}, u32[]{:S(2)}, u32[]{:S(2)}) collective-permute-start(bf16[8,16,1024]{2,1,0:T(8,128)(2,1)} %get-tuple-element.11), channel_id=1, source_target_pairs={{0,144},{499,2},{4,148},{503,6},{8,152},{507,10},{12,156},{511,14}... | collective-permute-start | bytes 786440 | tf_op jit(solution)/shard_map/ppermute | solution.py:226
  59.4 13.2 %collective-permute-start.5 = (bf16[128,1024]{1,0:T(8,128)(2,1)S(1)}, bf16[128,1024]{1,0:T(8,128)(2,1)S(1)}, u32[]{:S(2)}, u32[]{:S(2)}) collective-permute-start(bf16[128,1024]{1,0:T(8,128)(2,1)S(1)} %shard_map.54), channel_id=1, source_target_pairs={{0,144},{499,2},{4,148},{503,6},{8,152},{507,10},{12,156},{511,14}... | collective-permute-start | bytes 786440 | tf_op jit(solution)/shard_map/ppermute | solution.py:226
  63.6 9.0 %collective-permute-start.3 = (bf16[128,1024]{1,0:T(8,128)(2,1)S(1)}, bf16[128,1024]{1,0:T(8,128)(2,1)S(1)}, u32[]{:S(2)}, u32[]{:S(2)}) collective-permute-start(bf16[128,1024]{1,0:T(8,128)(2,1)S(1)} %shard_map.53), channel_id=1, source_target_pairs={{0,16},{499,387},{4,20},{503,391},{8,24},{507,395},{12,28},{511,39... | collective-permute-start | bytes 786440 | tf_op jit(solution)/shard_map/ppermute | solution.py:226
  69.3 7.6 %copy-start.2 = (bf16[8,16,1024]{2,1,0:T(8,128)(2,1)S(1)}, bf16[8,16,1024]{2,1,0:T(8,128)(2,1)}, u32[]{:S(2)}) copy-start(bf16[8,16,1024]{2,1,0:T(8,128)(2,1)} %get-tuple-element.8.refs_4_) | copy-start | bytes 786436
  69.3 7.5 %collective-permute-start.1 = (bf16[128,1024]{1,0:T(8,128)(2,1)S(1)}, bf16[128,1024]{1,0:T(8,128)(2,1)S(1)}, u32[]{:S(2)}, u32[]{:S(2)}) collective-permute-start(bf16[128,1024]{1,0:T(8,128)(2,1)S(1)} %shard_map.52), channel_id=1, source_target_pairs={{0,128},{499,114},{4,132},{503,118},{8,136},{507,122},{12,140},{51... | collective-permute-start | bytes 786440 | tf_op jit(solution)/shard_map/ppermute | solution.py:226
  72.5 29.5 %copy-start.3 = (f32[1024,16]{0,1:T(8,128)S(1)}, f32[1024,16]{0,1:T(8,128)}, u32[]{:S(2)}) copy-start(f32[1024,16]{0,1:T(8,128)} %param.5) | copy-start | bytes 196612

commit v10 on v9

--- a/solution.py
+++ b/solution.py
@@ -63,6 +63,7 @@
 
 
 INNER = {1: moves(inner, stay), 2: moves(stay, inner), 3: moves(inner, inner)}
+ORDER = (3, 1, 2)
 
 
 def exchange(blocks, groups):
@@ -236,17 +237,17 @@
     for d in (1, 2, 3):
         gradients.append(turn(parts[d], INNER[d]))
 
-    near = [mine]
-    for d in (1, 2, 3):
-        near.append(turn(mine, INNER[d]))
+    near = {0: mine}
+    for d in ORDER:
+        near[d] = turn(mine, INNER[d])
     moments = [moment_of(mine, activations)]
-    for d in (1, 2, 3):
+    for d in ORDER:
         moment = moment_of(near[d], activations)
         moments.append(turn(moment, INNER[d]))
     joined = join(moments, gradients)
     sums = exchange(joined, FAR_GROUPS)
 
-    new_factor, direction = finish(total_tokens, sums, own, near)
+    new_factor, direction = finish(total_tokens, sums, own, [near[d] for d in range(4)])
     return (new_factor.T, direction.T)
 
 

time: 105 us -> 106 us (level)
  the two profiles are of different devices: /device:TPU:65 before, /device:TPU:1 now
where the time goes in v10:
time: 106 us; the launch traced here: 105 us
  blocking collectives  53.9 us (51%)
  starting transfers between devices  32.5 us (31%)
  Pallas kernels  10.2 us (10%)
  matrix products  3.98 us (4%)
  waiting for transfers between devices  3.75 us (4%)
    all_to_all x2, blocking collectives, exchange(): lax.all_to_all(blocks, PLANES, split_axis=0, concat_axis=0, tiled=True, a...  53.9 us
    ppermute x9, starting transfers between devices, turn(): return lax.ppermute(block, PLANES, pairs)  32.5 us
    pallas_call x8, Pallas kernels, call(): pl.pallas_call(kernel, out_shape=out_shape, in_specs=in_specs, out_specs=...  10.2 us
    dot_general x1, matrix products, on_device(): lax.dot_general(cotangent, activations, TOKENS_FIRST, preferred_element_t...  3.98 us
    ppermute x9, waiting for transfers between devices, turn(): return lax.ppermute(block, PLANES, pairs)  3.75 us
  transfers between devices with their start and end apart: 9, of which 1 were waited for; matrix products, arithmetic and copies ran while one was open for 4% of the time, Pallas kernels for 5%

profile of v10, /device:TPU:1, one launch (start us, length us, event | category | flops | bytes accessed | tf_op | source)
XLA Modules:
  0.0 105.2 jit_solution(4273266091872712775)
XLA Ops:
  0.6 0.0 copy-start
  0.6 1.9 %shard_map.50 = bf16[16,16,1024]{2,1,0:T(8,128)(2,1)} custom-call(f32[16,1024]{1,0:T(8,128)} %bitcast.28), custom_call_target="tpu_custom_call" | custom-call | tf_op jit(solution)/shard_map/pallas_call | solution.py:98
  2.6 34.1 %all_to_all.10 = bf16[16,16,1024]{2,1,0:T(8,128)(2,1)S(1)} all-to-all(bf16[16,16,1024]{2,1,0:T(8,128)(2,1)} %shard_map.50), channel_id=1, replica_groups={{0,256,32,288,64,320,96,352,1,257,33,289,65,321,97,353},{128,384,160,41..., dimensions={0} | all-to-all | bytes 1048576 | tf_op jit(solution)/shard_map/all_to_all | solution.py:70
  36.7 2.3 %collective-permute-start.4 = (bf16[2,128,1024]{2,1,0:T(8,128)(2,1)S(1)}, bf16[2,128,1024]{2,1,0:T(8,128)(2,1)S(1)}, u32[]{:S(2)}, u32[]{:S(2)}) collective-permute-start(bf16[2,128,1024]{2,1,0:T(8,128)(2,1)S(1)} %bitcast.15), channel_id=1, source_target_pairs={{0,16},{499,387},{4,20},{503,391},{8,24},{507,395},{12,28},{511,39... | collective-permute-start | bytes 1572872 | tf_op jit(solution)/shard_map/ppermute | solution.py:227
  38.9 3.0 %collective-permute-start.2 = (bf16[2,128,1024]{2,1,0:T(8,128)(2,1)S(1)}, bf16[2,128,1024]{2,1,0:T(8,128)(2,1)S(1)}, u32[]{:S(2)}, u32[]{:S(2)}) collective-permute-start(bf16[2,128,1024]{2,1,0:T(8,128)(2,1)S(1)} %bitcast.16), channel_id=1, source_target_pairs={{0,128},{499,114},{4,132},{503,118},{8,136},{507,122},{12,140},{51... | collective-permute-start | bytes 1572872 | tf_op jit(solution)/shard_map/ppermute | solution.py:227
  41.9 5.5 %collective-permute-start = (bf16[2,128,1024]{2,1,0:T(8,128)(2,1)S(1)}, bf16[2,128,1024]{2,1,0:T(8,128)(2,1)S(1)}, u32[]{:S(2)}, u32[]{:S(2)}) collective-permute-start(bf16[2,128,1024]{2,1,0:T(8,128)(2,1)S(1)} %bitcast.17), channel_id=1, source_target_pairs={{0,144},{499,2},{4,148},{503,6},{8,152},{507,10},{12,156},{511,14}... | collective-permute-start | bytes 1572872 | tf_op jit(solution)/shard_map/ppermute | solution.py:227
  47.5 4.0 %convolution_convert_fusion = bf16[1024,1024]{1,0:T(8,128)(2,1)S(1)} fusion(bf16[1024,1024]{1,0:T(8,128)(2,1)S(1)} %copy-done, bf16[1024,1024]{1,0:T(8,128)(2,1)} %x_ref.7), kind=kOutput, calls=%fused_computation | convolution fusion | flops 2148532224 | bytes 6291456 | tf_op jit(solution)/shard_map/dot_general | solution.py:232
  51.5 0.0 copy-start.1
  51.5 1.3 %shard_map.55 = (bf16[8,16,1024]{2,1,0:T(8,128)(2,1)}, bf16[8,16,1024]{2,1,0:T(8,128)(2,1)}, bf16[8,16,1024]{2,1,0:T(8,128)(2,1)}, bf16[8,16,1024]{2,1,0:T(8,128)(2,1)}) custom-call(bf16[64,16,1024]{2,1,0:T(8,128)(2,1)S(1)} %bitcast.20), custom_call_target="tpu_custom_call" | custom-call | tf_op jit(solution)/shard_map/pallas_call | solution.py:98
  52.8 3.3 %collective-permute-start.6 = (bf16[8,16,1024]{2,1,0:T(8,128)(2,1)}, bf16[8,16,1024]{2,1,0:T(8,128)(2,1)S(1)}, u32[]{:S(2)}, u32[]{:S(2)}) collective-permute-start(bf16[8,16,1024]{2,1,0:T(8,128)(2,1)} %get-tuple-element.9), channel_id=1, source_target_pairs={{0,128},{499,114},{4,132},{503,118},{8,136},{507,122},{12,140},{51... | collective-permute-start | bytes 786440 | tf_op jit(solution)/shard_map/ppermute | solution.py:227
  56.1 1.9 %collective-permute-start.7 = (bf16[8,16,1024]{2,1,0:T(8,128)(2,1)}, bf16[8,16,1024]{2,1,0:T(8,128)(2,1)S(1)}, u32[]{:S(2)}, u32[]{:S(2)}) collective-permute-start(bf16[8,16,1024]{2,1,0:T(8,128)(2,1)} %get-tuple-element.10), channel_id=1, source_target_pairs={{0,16},{499,387},{4,20},{503,391},{8,24},{507,395},{12,28},{511,39... | collective-permute-start | bytes 786440 | tf_op jit(solution)/shard_map/ppermute | solution.py:227
  58.1 0.0 collective-permute-done.4.rows_ref
  58.1 5.5 %collective-permute-start.8 = (bf16[8,16,1024]{2,1,0:T(8,128)(2,1)}, bf16[8,16,1024]{2,1,0:T(8,128)(2,1)S(1)}, u32[]{:S(2)}, u32[]{:S(2)}) collective-permute-start(bf16[8,16,1024]{2,1,0:T(8,128)(2,1)} %get-tuple-element.11), channel_id=1, source_target_pairs={{0,144},{499,2},{4,148},{503,6},{8,152},{507,10},{12,156},{511,14}... | collective-permute-start | bytes 786440 | tf_op jit(solution)/shard_map/ppermute | solution.py:227
  63.6 1.1 %shard_map.54 = bf16[128,1024]{1,0:T(8,128)(2,1)S(1)} custom-call(bf16[2,128,1024]{2,1,0:T(8,128)(2,1)S(1)} %collective-permute-done.4.rows_ref, bf16[1024,1024]{1,0:T(8,128)(2,1)S(1)} %copy-done.1), custom_call_target="tpu_custom_call" | custom-call | tf_op jit(solution)/shard_map/pallas_call | solution.py:98
  64.7 0.0 collective-permute-done.2.rows_ref
  64.7 2.3 %collective-permute-start.5 = (bf16[128,1024]{1,0:T(8,128)(2,1)S(1)}, bf16[128,1024]{1,0:T(8,128)(2,1)S(1)}, u32[]{:S(2)}, u32[]{:S(2)}) collective-permute-start(bf16[128,1024]{1,0:T(8,128)(2,1)S(1)} %shard_map.54), channel_id=1, source_target_pairs={{0,16},{499,387},{4,20},{503,391},{8,24},{507,395},{12,28},{511,39... | collective-permute-start | bytes 786440 | tf_op jit(solution)/shard_map/ppermute | solution.py:227
  67.0 1.1 %shard_map.53 = bf16[128,1024]{1,0:T(8,128)(2,1)S(1)} custom-call(bf16[2,128,1024]{2,1,0:T(8,128)(2,1)S(1)} %collective-permute-done.2.rows_ref, bf16[1024,1024]{1,0:T(8,128)(2,1)S(1)} %copy-done.1), custom_call_target="tpu_custom_call" | custom-call | tf_op jit(solution)/shard_map/pallas_call | solution.py:98
  68.1 0.0 collective-permute-done.rows_ref
  68.1 3.0 %collective-permute-start.3 = (bf16[128,1024]{1,0:T(8,128)(2,1)S(1)}, bf16[128,1024]{1,0:T(8,128)(2,1)S(1)}, u32[]{:S(2)}, u32[]{:S(2)}) collective-permute-start(bf16[128,1024]{1,0:T(8,128)(2,1)S(1)} %shard_map.53), channel_id=1, source_target_pairs={{0,128},{499,114},{4,132},{503,118},{8,136},{507,122},{12,140},{51... | collective-permute-start | bytes 786440 | tf_op jit(solution)/shard_map/ppermute | solution.py:227
  71.2 1.1 %shard_map.52 = bf16[128,1024]{1,0:T(8,128)(2,1)S(1)} custom-call(bf16[2,128,1024]{2,1,0:T(8,128)(2,1)S(1)} %collective-permute-done.rows_ref, bf16[1024,1024]{1,0:T(8,128)(2,1)S(1)} %copy-done.1), custom_call_target="tpu_custom_call" | custom-call | tf_op jit(solution)/shard_map/pallas_call | solution.py:98
  72.3 0.0 collective-permute-done.6.refs_5_
  72.3 5.7 %collective-permute-start.1 = (bf16[128,1024]{1,0:T(8,128)(2,1)S(1)}, bf16[128,1024]{1,0:T(8,128)(2,1)S(1)}, u32[]{:S(2)}, u32[]{:S(2)}) collective-permute-start(bf16[128,1024]{1,0:T(8,128)(2,1)S(1)} %shard_map.52), channel_id=1, source_target_pairs={{0,144},{499,2},{4,148},{503,6},{8,152},{507,10},{12,156},{511,14}... | collective-permute-start | bytes 786440 | tf_op jit(solution)/shard_map/ppermute | solution.py:227
  78.0 1.1 %shard_map.51 = bf16[128,1024]{1,0:T(8,128)(2,1)S(1)} custom-call(bf16[2,128,1024]{2,1,0:T(8,128)(2,1)S(1)} %bitcast.18, bf16[1024,1024]{1,0:T(8,128)(2,1)S(1)} %copy-done.1), custom_call_target="tpu_custom_call" | custom-call | tf_op jit(solution)/shard_map/pallas_call | solution.py:98
  79.1 0.0 copy-start.3
  79.1 0.0 collective-permute-done.7.refs_6_
  79.1 0.0 collective-permute-done.8.refs_7_
  79.1 0.0 collective-permute-done.5
  79.1 0.0 collective-permute-done.3
  79.1 3.7 %collective-permute-done.1 = bf16[128,1024]{1,0:T(8,128)(2,1)S(1)} collective-permute-done((bf16[128,1024]{1,0:T(8,128)(2,1)S(1)}, bf16[128,1024]{1,0:T(8,128)(2,1)S(1)}, u32[]{:S(2)}, u32[]{:S(2)}) %collective-permute-start.1) | collective-permute-done | bytes 262176 | tf_op jit(solution)/shard_map/ppermute | solution.py:227
  82.9 0.3 shard_map.56
  83.1 19.8 %all_to_all.11.refs_0_ = bf16[8,32,1024]{2,1,0:T(8,128)(2,1)S(1)} all-to-all(bf16[8,32,1024]{2,1,0:T(8,128)(2,1)S(1)} %shard_map.56), channel_id=1, replica_groups={{0,256,32,288,64,320,96,352},{128,384,160,416,192,448,224,480},{16,272,..., dimensions={0} | all-to-all | bytes 1048576 | tf_op jit(solution)/shard_map/all_to_all | solution.py:70
  102.9 2.2 %shard_map.57 = (f32[16,1024]{1,0:T(8,128)}, f32[16,1024]{1,0:T(8,128)}) custom-call(bf16[8,32,1024]{2,1,0:T(8,128)(2,1)S(1)} %all_to_all.11.refs_0_, f32[16,1024]{1,0:T(8,128)S(1)} %bitcast.29, bf16[256,1024]{1,0:T(8,128)(2,1)S(1)} %bitcast.19, bf16[256,1024]{1,0:T(8,128)(2,1)S(1)} %bitcast.22, bf16[256,1024]{1,0:T(8,128)(2,1)S(1)} %bitcast.21, ...), custom_call_target="tpu_custom_call" | custom-call | tf_op jit(solution)/shard_map/pallas_call | solution.py:98
  (5 shorter events, 0.0 us)
Async XLA Ops:
  0.6 46.8 %copy-start = (bf16[1024,1024]{1,0:T(8,128)(2,1)S(1)}, bf16[1024,1024]{1,0:T(8,128)(2,1)}, u32[]{:S(2)}) copy-start(bf16[1024,1024]{1,0:T(8,128)(2,1)} %param.4) | copy-start | bytes 6291460
  36.7 21.4 %collective-permute-start.4 = (bf16[2,128,1024]{2,1,0:T(8,128)(2,1)S(1)}, bf16[2,128,1024]{2,1,0:T(8,128)(2,1)S(1)}, u32[]{:S(2)}, u32[]{:S(2)}) collective-permute-start(bf16[2,128,1024]{2,1,0:T(8,128)(2,1)S(1)} %bitcast.15), channel_id=1, source_target_pairs={{0,16},{499,387},{4,20},{503,391},{8,24},{507,395},{12,28},{511,39... | collective-permute-start | bytes 1572872 | tf_op jit(solution)/shard_map/ppermute | solution.py:227
  38.9 25.8 %collective-permute-start.2 = (bf16[2,128,1024]{2,1,0:T(8,128)(2,1)S(1)}, bf16[2,128,1024]{2,1,0:T(8,128)(2,1)S(1)}, u32[]{:S(2)}, u32[]{:S(2)}) collective-permute-start(bf16[2,128,1024]{2,1,0:T(8,128)(2,1)S(1)} %bitcast.16), channel_id=1, source_target_pairs={{0,128},{499,114},{4,132},{503,118},{8,136},{507,122},{12,140},{51... | collective-permute-start | bytes 1572872 | tf_op jit(solution)/shard_map/ppermute | solution.py:227
  41.9 26.2 %collective-permute-start = (bf16[2,128,1024]{2,1,0:T(8,128)(2,1)S(1)}, bf16[2,128,1024]{2,1,0:T(8,128)(2,1)S(1)}, u32[]{:S(2)}, u32[]{:S(2)}) collective-permute-start(bf16[2,128,1024]{2,1,0:T(8,128)(2,1)S(1)} %bitcast.17), channel_id=1, source_target_pairs={{0,144},{499,2},{4,148},{503,6},{8,152},{507,10},{12,156},{511,14}... | collective-permute-start | bytes 1572872 | tf_op jit(solution)/shard_map/ppermute | solution.py:227
  51.5 12.1 %copy-start.1 = (bf16[1024,1024]{1,0:T(8,128)(2,1)S(1)}, bf16[1024,1024]{1,0:T(8,128)(2,1)}, u32[]{:S(2)}) copy-start(bf16[1024,1024]{1,0:T(8,128)(2,1)} %x_ref.7) | copy-start | bytes 6291460
  52.8 19.5 %collective-permute-start.6 = (bf16[8,16,1024]{2,1,0:T(8,128)(2,1)}, bf16[8,16,1024]{2,1,0:T(8,128)(2,1)S(1)}, u32[]{:S(2)}, u32[]{:S(2)}) collective-permute-start(bf16[8,16,1024]{2,1,0:T(8,128)(2,1)} %get-tuple-element.9), channel_id=1, source_target_pairs={{0,128},{499,114},{4,132},{503,118},{8,136},{507,122},{12,140},{51... | collective-permute-start | bytes 786440 | tf_op jit(solution)/shard_map/ppermute | solution.py:227
  56.1 23.0 %collective-permute-start.7 = (bf16[8,16,1024]{2,1,0:T(8,128)(2,1)}, bf16[8,16,1024]{2,1,0:T(8,128)(2,1)S(1)}, u32[]{:S(2)}, u32[]{:S(2)}) collective-permute-start(bf16[8,16,1024]{2,1,0:T(8,128)(2,1)} %get-tuple-element.10), channel_id=1, source_target_pairs={{0,16},{499,387},{4,20},{503,391},{8,24},{507,395},{12,28},{511,39... | collective-permute-start | bytes 786440 | tf_op jit(solution)/shard_map/ppermute | solution.py:227
  58.1 21.0 %collective-permute-start.8 = (bf16[8,16,1024]{2,1,0:T(8,128)(2,1)}, bf16[8,16,1024]{2,1,0:T(8,128)(2,1)S(1)}, u32[]{:S(2)}, u32[]{:S(2)}) collective-permute-start(bf16[8,16,1024]{2,1,0:T(8,128)(2,1)} %get-tuple-element.11), channel_id=1, source_target_pairs={{0,144},{499,2},{4,148},{503,6},{8,152},{507,10},{12,156},{511,14}... | collective-permute-start | bytes 786440 | tf_op jit(solution)/shard_map/ppermute | solution.py:227
  64.7 14.4 %collective-permute-start.5 = (bf16[128,1024]{1,0:T(8,128)(2,1)S(1)}, bf16[128,1024]{1,0:T(8,128)(2,1)S(1)}, u32[]{:S(2)}, u32[]{:S(2)}) collective-permute-start(bf16[128,1024]{1,0:T(8,128)(2,1)S(1)} %shard_map.54), channel_id=1, source_target_pairs={{0,16},{499,387},{4,20},{503,391},{8,24},{507,395},{12,28},{511,39... | collective-permute-start | bytes 786440 | tf_op jit(solution)/shard_map/ppermute | solution.py:227
  68.1 11.0 %collective-permute-start.3 = (bf16[128,1024]{1,0:T(8,128)(2,1)S(1)}, bf16[128,1024]{1,0:T(8,128)(2,1)S(1)}, u32[]{:S(2)}, u32[]{:S(2)}) collective-permute-start(bf16[128,1024]{1,0:T(8,128)(2,1)S(1)} %shard_map.53), channel_id=1, source_target_pairs={{0,128},{499,114},{4,132},{503,118},{8,136},{507,122},{12,140},{51... | collective-permute-start | bytes 786440 | tf_op jit(solution)/shard_map/ppermute | solution.py:227
  72.3 10.6 %copy-start.2 = (bf16[8,16,1024]{2,1,0:T(8,128)(2,1)S(1)}, bf16[8,16,1024]{2,1,0:T(8,128)(2,1)}, u32[]{:S(2)}) copy-start(bf16[8,16,1024]{2,1,0:T(8,128)(2,1)} %get-tuple-element.8.refs_4_) | copy-start | bytes 786436
  72.3 10.6 %collective-permute-start.1 = (bf16[128,1024]{1,0:T(8,128)(2,1)S(1)}, bf16[128,1024]{1,0:T(8,128)(2,1)S(1)}, u32[]{:S(2)}, u32[]{:S(2)}) collective-permute-start(bf16[128,1024]{1,0:T(8,128)(2,1)S(1)} %shard_map.52), channel_id=1, source_target_pairs={{0,144},{499,2},{4,148},{503,6},{8,152},{507,10},{12,156},{511,14}... | collective-permute-start | bytes 786440 | tf_op jit(solution)/shard_map/ppermute | solution.py:227
  79.1 23.9 %copy-start.3 = (f32[1024,16]{0,1:T(8,128)S(1)}, f32[1024,16]{0,1:T(8,128)}, u32[]{:S(2)}) copy-start(f32[1024,16]{0,1:T(8,128)} %param.5) | copy-start | bytes 196612

commit v11 on v10

--- a/solution.py
+++ b/solution.py
@@ -148,11 +148,31 @@
     return call(pick_kernel, [shape] * 4, [vmem()], [hbm()] * 4, rows, scratch_shapes=scratch)
 
 
+def gram_part(rows, x):
+    whitened = lax.dot_general(rows, x, ROWS_ROWS, preferred_element_type=f32)
+    return jnp.dot(whitened.astype(bf16), x, preferred_element_type=f32).astype(bf16)
+
+
+def own_rows_kernel(rows_ref, x_ref, out_ref):
+    out_ref[...] = rows_ref[position()[5]]
+
+
+def own_rows(rows, x):
+    shape = jax.ShapeDtypeStruct(rows.shape[1:], bf16)
+    return call(own_rows_kernel, shape, [vmem()] * 2, vmem(), rows, x)
+
+
+def own_moment_kernel(rows_ref, x_ref, out_ref):
+    out_ref[...] = gram_part(rows_ref[...], x_ref[...])
+
+
+def own_moment(rows, x):
+    shape = jax.ShapeDtypeStruct(rows.shape, bf16)
+    return call(own_moment_kernel, shape, [vmem()] * 2, vmem(), rows, x)
+
+
 def moment_kernel(rows_ref, x_ref, out_ref):
-    x = x_ref[...]
-    rows = rows_ref[position()[5]]
-    whitened = lax.dot_general(rows, x, ROWS_ROWS, preferred_element_type=f32)
-    out_ref[...] = jnp.dot(whitened.astype(bf16), x, preferred_element_type=f32).astype(bf16)
+    out_ref[...] = gram_part(rows_ref[position()[5]], x_ref[...])
 
 
 def moment_of(rows, x):
@@ -179,7 +199,7 @@
 
 def finish_kernel(tokens, *refs):
     sums_ref, own_ref, blocks = refs[0], refs[1], refs[2:6]
-    new_ref, direction_ref = refs[6:]
+    new_ref, direction_ref, rows = refs[6:]
     _, _, _, yh, zh, h = position()
     at = h * 128 + (2 * yh + zh) * 16
     own = own_ref[...]
@@ -190,17 +210,15 @@
     high = inner_rows.astype(bf16)
     low = (inner_rows - high.astype(f32)).astype(bf16)
     left = jnp.concatenate([high, low, total[16:].astype(bf16)], axis=0)
-    result = jnp.zeros((32, own.shape[1]), f32)
     for k, block in enumerate(blocks):
-        part = block[...]
-        product = lax.dot_general(left, part, ROWS_ROWS, preferred_element_type=f32)
-        curve = product[:16] + product[16:32]
-        if k == 0:
-            column = lax.broadcasted_iota(jnp.int32, curve.shape, 1)
-            row = lax.broadcasted_iota(jnp.int32, curve.shape, 0)
-            curve = curve - (column == row + at).astype(f32)
-        right = jnp.concatenate([curve.astype(bf16), product[32:].astype(bf16)], axis=0)
-        result = result + jnp.dot(right, part, preferred_element_type=f32)
+        rows[pl.ds(k * 256, 256)] = block[...]
+    product = lax.dot_general(left, rows[...], ROWS_ROWS, preferred_element_type=f32)
+    curve = product[:16] + product[16:32]
+    column = lax.broadcasted_iota(jnp.int32, curve.shape, 1)
+    row = lax.broadcasted_iota(jnp.int32, curve.shape, 0)
+    curve = curve - (column == row + at).astype(f32)
+    right = jnp.concatenate([curve.astype(bf16), product[32:].astype(bf16)], axis=0)
+    result = jnp.dot(right, rows[...], preferred_element_type=f32)
     new_ref[...] = own - 0.5 * step_size * result[:16]
     direction_ref[...] = result[16:]
 
@@ -214,6 +232,7 @@
         sums,
         own,
         *[block.reshape(256, own.shape[1]) for block in blocks],
+        scratch_shapes=[pltpu.VMEM((4 * 256, own.shape[1]), bf16)],
     )
 
 
@@ -240,7 +259,8 @@
     near = {0: mine}
     for d in ORDER:
         near[d] = turn(mine, INNER[d])
-    moments = [moment_of(mine, activations)]
+    own_block = own_rows(mine, activations)
+    moments = [own_moment(own_block, activations)]
     for d in ORDER:
         moment = moment_of(near[d], activations)
         moments.append(turn(moment, INNER[d]))

time: 106 us -> 105 us (level)
    pallas_call x8 -> x9, Pallas kernels: 10.2 us -> 9.7 us  [call(): pl.pallas_call(kernel, out_shape=out_shape, in_specs=in_specs, out_specs=...]
  transfers between devices with their start and end apart: 9 -> 9, of which waited for: 1 -> 1; matrix products, arithmetic and copies ran while one was open for 4% -> 4% of each run, Pallas kernels for 5% -> 6%
where the time goes in v11:
time: 105 us
  blocking collectives  53.9 us (51%)
  starting transfers between devices  32.5 us (31%)
  Pallas kernels  9.7 us (9%)
  matrix products  3.98 us (4%)
  waiting for transfers between devices  3.71 us (4%)
    all_to_all x2, blocking collectives, exchange(): lax.all_to_all(blocks, PLANES, split_axis=0, concat_axis=0, tiled=True, a...  53.9 us
    ppermute x9, starting transfers between devices, turn(): return lax.ppermute(block, PLANES, pairs)  32.5 us
    pallas_call x9, Pallas kernels, call(): pl.pallas_call(kernel, out_shape=out_shape, in_specs=in_specs, out_specs=...  9.7 us
    dot_general x1, matrix products, on_device(): lax.dot_general(cotangent, activations, TOKENS_FIRST, preferred_element_t...  3.98 us
    ppermute x9, waiting for transfers between devices, turn(): return lax.ppermute(block, PLANES, pairs)  3.71 us
  transfers between devices with their start and end apart: 9, of which 1 were waited for; matrix products, arithmetic and copies ran while one was open for 4% of the time, Pallas kernels for 6%

profile of v11, /device:TPU:1, one launch (start us, length us, event | category | flops | bytes accessed | tf_op | source)
XLA Modules:
  0.0 104.7 jit_solution(8133979034568078911)
XLA Ops:
  0.6 0.0 copy-start
  0.6 1.9 %shard_map.50 = bf16[16,16,1024]{2,1,0:T(8,128)(2,1)} custom-call(f32[16,1024]{1,0:T(8,128)} %bitcast.28), custom_call_target="tpu_custom_call" | custom-call | tf_op jit(solution)/shard_map/pallas_call | solution.py:98
  2.6 34.1 %all_to_all.10 = bf16[16,16,1024]{2,1,0:T(8,128)(2,1)S(1)} all-to-all(bf16[16,16,1024]{2,1,0:T(8,128)(2,1)} %shard_map.50), channel_id=1, replica_groups={{0,256,32,288,64,320,96,352,1,257,33,289,65,321,97,353},{128,384,160,41..., dimensions={0} | all-to-all | bytes 1048576 | tf_op jit(solution)/shard_map/all_to_all | solution.py:70
  36.7 2.3 %collective-permute-start.4 = (bf16[2,128,1024]{2,1,0:T(8,128)(2,1)S(1)}, bf16[2,128,1024]{2,1,0:T(8,128)(2,1)S(1)}, u32[]{:S(2)}, u32[]{:S(2)}) collective-permute-start(bf16[2,128,1024]{2,1,0:T(8,128)(2,1)S(1)} %bitcast.15), channel_id=1, source_target_pairs={{0,16},{499,387},{4,20},{503,391},{8,24},{507,395},{12,28},{511,39... | collective-permute-start | bytes 1572872 | tf_op jit(solution)/shard_map/ppermute | solution.py:246
  38.9 3.0 %collective-permute-start.2 = (bf16[2,128,1024]{2,1,0:T(8,128)(2,1)S(1)}, bf16[2,128,1024]{2,1,0:T(8,128)(2,1)S(1)}, u32[]{:S(2)}, u32[]{:S(2)}) collective-permute-start(bf16[2,128,1024]{2,1,0:T(8,128)(2,1)S(1)} %bitcast.16), channel_id=1, source_target_pairs={{0,128},{499,114},{4,132},{503,118},{8,136},{507,122},{12,140},{51... | collective-permute-start | bytes 1572872 | tf_op jit(solution)/shard_map/ppermute | solution.py:246
  41.9 5.5 %collective-permute-start = (bf16[2,128,1024]{2,1,0:T(8,128)(2,1)S(1)}, bf16[2,128,1024]{2,1,0:T(8,128)(2,1)S(1)}, u32[]{:S(2)}, u32[]{:S(2)}) collective-permute-start(bf16[2,128,1024]{2,1,0:T(8,128)(2,1)S(1)} %bitcast.17), channel_id=1, source_target_pairs={{0,144},{499,2},{4,148},{503,6},{8,152},{507,10},{12,156},{511,14}... | collective-permute-start | bytes 1572872 | tf_op jit(solution)/shard_map/ppermute | solution.py:246
  47.5 4.0 %convolution_convert_fusion = bf16[1024,1024]{1,0:T(8,128)(2,1)S(1)} fusion(bf16[1024,1024]{1,0:T(8,128)(2,1)S(1)} %copy-done, bf16[1024,1024]{1,0:T(8,128)(2,1)} %x_ref.9), kind=kOutput, calls=%fused_computation | convolution fusion | flops 2148532224 | bytes 6291456 | tf_op jit(solution)/shard_map/dot_general | solution.py:251
  51.5 0.0 copy-start.1
  51.5 1.3 %shard_map.56 = (bf16[8,16,1024]{2,1,0:T(8,128)(2,1)}, bf16[8,16,1024]{2,1,0:T(8,128)(2,1)}, bf16[8,16,1024]{2,1,0:T(8,128)(2,1)}, bf16[8,16,1024]{2,1,0:T(8,128)(2,1)}) custom-call(bf16[64,16,1024]{2,1,0:T(8,128)(2,1)S(1)} %bitcast.20), custom_call_target="tpu_custom_call" | custom-call | tf_op jit(solution)/shard_map/pallas_call | solution.py:98
  52.8 3.3 %collective-permute-start.6 = (bf16[8,16,1024]{2,1,0:T(8,128)(2,1)}, bf16[8,16,1024]{2,1,0:T(8,128)(2,1)S(1)}, u32[]{:S(2)}, u32[]{:S(2)}) collective-permute-start(bf16[8,16,1024]{2,1,0:T(8,128)(2,1)} %get-tuple-element.9), channel_id=1, source_target_pairs={{0,128},{499,114},{4,132},{503,118},{8,136},{507,122},{12,140},{51... | collective-permute-start | bytes 786440 | tf_op jit(solution)/shard_map/ppermute | solution.py:246
  56.1 1.9 %collective-permute-start.7 = (bf16[8,16,1024]{2,1,0:T(8,128)(2,1)}, bf16[8,16,1024]{2,1,0:T(8,128)(2,1)S(1)}, u32[]{:S(2)}, u32[]{:S(2)}) collective-permute-start(bf16[8,16,1024]{2,1,0:T(8,128)(2,1)} %get-tuple-element.10), channel_id=1, source_target_pairs={{0,16},{499,387},{4,20},{503,391},{8,24},{507,395},{12,28},{511,39... | collective-permute-start | bytes 786440 | tf_op jit(solution)/shard_map/ppermute | solution.py:246
  58.1 0.0 collective-permute-done.4.rows_ref
  58.1 5.5 %collective-permute-start.8 = (bf16[8,16,1024]{2,1,0:T(8,128)(2,1)}, bf16[8,16,1024]{2,1,0:T(8,128)(2,1)S(1)}, u32[]{:S(2)}, u32[]{:S(2)}) collective-permute-start(bf16[8,16,1024]{2,1,0:T(8,128)(2,1)} %get-tuple-element.11), channel_id=1, source_target_pairs={{0,144},{499,2},{4,148},{503,6},{8,152},{507,10},{12,156},{511,14}... | collective-permute-start | bytes 786440 | tf_op jit(solution)/shard_map/ppermute | solution.py:246
  63.6 1.1 %shard_map.55 = bf16[128,1024]{1,0:T(8,128)(2,1)S(1)} custom-call(bf16[2,128,1024]{2,1,0:T(8,128)(2,1)S(1)} %collective-permute-done.4.rows_ref, bf16[1024,1024]{1,0:T(8,128)(2,1)S(1)} %copy-done.1), custom_call_target="tpu_custom_call" | custom-call | tf_op jit(solution)/shard_map/pallas_call | solution.py:98
  64.7 0.0 collective-permute-done.2.rows_ref
  64.7 2.3 %collective-permute-start.5 = (bf16[128,1024]{1,0:T(8,128)(2,1)S(1)}, bf16[128,1024]{1,0:T(8,128)(2,1)S(1)}, u32[]{:S(2)}, u32[]{:S(2)}) collective-permute-start(bf16[128,1024]{1,0:T(8,128)(2,1)S(1)} %shard_map.55), channel_id=1, source_target_pairs={{0,16},{499,387},{4,20},{503,391},{8,24},{507,395},{12,28},{511,39... | collective-permute-start | bytes 786440 | tf_op jit(solution)/shard_map/ppermute | solution.py:246
  67.0 1.1 %shard_map.54 = bf16[128,1024]{1,0:T(8,128)(2,1)S(1)} custom-call(bf16[2,128,1024]{2,1,0:T(8,128)(2,1)S(1)} %collective-permute-done.2.rows_ref, bf16[1024,1024]{1,0:T(8,128)(2,1)S(1)} %copy-done.1), custom_call_target="tpu_custom_call" | custom-call | tf_op jit(solution)/shard_map/pallas_call | solution.py:98
  68.1 0.0 collective-permute-done.rows_ref
  68.1 3.0 %collective-permute-start.3 = (bf16[128,1024]{1,0:T(8,128)(2,1)S(1)}, bf16[128,1024]{1,0:T(8,128)(2,1)S(1)}, u32[]{:S(2)}, u32[]{:S(2)}) collective-permute-start(bf16[128,1024]{1,0:T(8,128)(2,1)S(1)} %shard_map.54), channel_id=1, source_target_pairs={{0,128},{499,114},{4,132},{503,118},{8,136},{507,122},{12,140},{51... | collective-permute-start | bytes 786440 | tf_op jit(solution)/shard_map/ppermute | solution.py:246
  71.2 1.1 %shard_map.53 = bf16[128,1024]{1,0:T(8,128)(2,1)S(1)} custom-call(bf16[2,128,1024]{2,1,0:T(8,128)(2,1)S(1)} %collective-permute-done.rows_ref, bf16[1024,1024]{1,0:T(8,128)(2,1)S(1)} %copy-done.1), custom_call_target="tpu_custom_call" | custom-call | tf_op jit(solution)/shard_map/pallas_call | solution.py:98
  72.3 0.0 collective-permute-done.6.refs_5_
  72.3 5.7 %collective-permute-start.1 = (bf16[128,1024]{1,0:T(8,128)(2,1)S(1)}, bf16[128,1024]{1,0:T(8,128)(2,1)S(1)}, u32[]{:S(2)}, u32[]{:S(2)}) collective-permute-start(bf16[128,1024]{1,0:T(8,128)(2,1)S(1)} %shard_map.53), channel_id=1, source_target_pairs={{0,144},{499,2},{4,148},{503,6},{8,152},{507,10},{12,156},{511,14}... | collective-permute-start | bytes 786440 | tf_op jit(solution)/shard_map/ppermute | solution.py:246
  78.0 1.1 %shard_map.52 = bf16[128,1024]{1,0:T(8,128)(2,1)S(1)} custom-call(bf16[128,1024]{1,0:T(8,128)(2,1)S(1)} %shard_map.51.rows_ref, bf16[1024,1024]{1,0:T(8,128)(2,1)S(1)} %copy-done.1), custom_call_target="tpu_custom_call" | custom-call | tf_op jit(solution)/shard_map/pallas_call | solution.py:98
  79.1 0.0 copy-start.3
  79.1 0.0 collective-permute-done.7.refs_6_
  79.2 0.0 collective-permute-done.8.refs_7_
  79.2 0.0 collective-permute-done.5
  79.2 0.0 collective-permute-done.3
  79.2 3.7 %collective-permute-done.1 = bf16[128,1024]{1,0:T(8,128)(2,1)S(1)} collective-permute-done((bf16[128,1024]{1,0:T(8,128)(2,1)S(1)}, bf16[128,1024]{1,0:T(8,128)(2,1)S(1)}, u32[]{:S(2)}, u32[]{:S(2)}) %collective-permute-start.1) | collective-permute-done | bytes 262176 | tf_op jit(solution)/shard_map/ppermute | solution.py:246
  82.9 0.3 shard_map.57
  83.1 19.8 %all_to_all.11.refs_0_ = bf16[8,32,1024]{2,1,0:T(8,128)(2,1)S(1)} all-to-all(bf16[8,32,1024]{2,1,0:T(8,128)(2,1)S(1)} %shard_map.57), channel_id=1, replica_groups={{0,256,32,288,64,320,96,352},{128,384,160,416,192,448,224,480},{16,272,..., dimensions={0} | all-to-all | bytes 1048576 | tf_op jit(solution)/shard_map/all_to_all | solution.py:70
  102.9 1.7 %shard_map.58 = (f32[16,1024]{1,0:T(8,128)}, f32[16,1024]{1,0:T(8,128)}) custom-call(bf16[8,32,1024]{2,1,0:T(8,128)(2,1)S(1)} %all_to_all.11.refs_0_, f32[16,1024]{1,0:T(8,128)S(1)} %bitcast.29, bf16[256,1024]{1,0:T(8,128)(2,1)S(1)} %bitcast.19, bf16[256,1024]{1,0:T(8,128)(2,1)S(1)} %bitcast.22, bf16[256,1024]{1,0:T(8,128)(2,1)S(1)} %bitcast.21, ...), custom_call_target="tpu_custom_call" | custom-call | tf_op jit(solution)/shard_map/pallas_call | solution.py:98
  (6 shorter events, 0.0 us)
Async XLA Ops:
  0.6 46.8 %copy-start = (bf16[1024,1024]{1,0:T(8,128)(2,1)S(1)}, bf16[1024,1024]{1,0:T(8,128)(2,1)}, u32[]{:S(2)}) copy-start(bf16[1024,1024]{1,0:T(8,128)(2,1)} %param.4) | copy-start | bytes 6291460
  36.7 21.4 %collective-permute-start.4 = (bf16[2,128,1024]{2,1,0:T(8,128)(2,1)S(1)}, bf16[2,128,1024]{2,1,0:T(8,128)(2,1)S(1)}, u32[]{:S(2)}, u32[]{:S(2)}) collective-permute-start(bf16[2,128,1024]{2,1,0:T(8,128)(2,1)S(1)} %bitcast.15), channel_id=1, source_target_pairs={{0,16},{499,387},{4,20},{503,391},{8,24},{507,395},{12,28},{511,39... | collective-permute-start | bytes 1572872 | tf_op jit(solution)/shard_map/ppermute | solution.py:246
  38.9 25.8 %collective-permute-start.2 = (bf16[2,128,1024]{2,1,0:T(8,128)(2,1)S(1)}, bf16[2,128,1024]{2,1,0:T(8,128)(2,1)S(1)}, u32[]{:S(2)}, u32[]{:S(2)}) collective-permute-start(bf16[2,128,1024]{2,1,0:T(8,128)(2,1)S(1)} %bitcast.16), channel_id=1, source_target_pairs={{0,128},{499,114},{4,132},{503,118},{8,136},{507,122},{12,140},{51... | collective-permute-start | bytes 1572872 | tf_op jit(solution)/shard_map/ppermute | solution.py:246
  41.9 26.2 %collective-permute-start = (bf16[2,128,1024]{2,1,0:T(8,128)(2,1)S(1)}, bf16[2,128,1024]{2,1,0:T(8,128)(2,1)S(1)}, u32[]{:S(2)}, u32[]{:S(2)}) collective-permute-start(bf16[2,128,1024]{2,1,0:T(8,128)(2,1)S(1)} %bitcast.17), channel_id=1, source_target_pairs={{0,144},{499,2},{4,148},{503,6},{8,152},{507,10},{12,156},{511,14}... | collective-permute-start | bytes 1572872 | tf_op jit(solution)/shard_map/ppermute | solution.py:246
  51.5 12.1 %copy-start.1 = (bf16[1024,1024]{1,0:T(8,128)(2,1)S(1)}, bf16[1024,1024]{1,0:T(8,128)(2,1)}, u32[]{:S(2)}) copy-start(bf16[1024,1024]{1,0:T(8,128)(2,1)} %x_ref.9) | copy-start | bytes 6291460
  52.8 19.5 %collective-permute-start.6 = (bf16[8,16,1024]{2,1,0:T(8,128)(2,1)}, bf16[8,16,1024]{2,1,0:T(8,128)(2,1)S(1)}, u32[]{:S(2)}, u32[]{:S(2)}) collective-permute-start(bf16[8,16,1024]{2,1,0:T(8,128)(2,1)} %get-tuple-element.9), channel_id=1, source_target_pairs={{0,128},{499,114},{4,132},{503,118},{8,136},{507,122},{12,140},{51... | collective-permute-start | bytes 786440 | tf_op jit(solution)/shard_map/ppermute | solution.py:246
  56.1 23.0 %collective-permute-start.7 = (bf16[8,16,1024]{2,1,0:T(8,128)(2,1)}, bf16[8,16,1024]{2,1,0:T(8,128)(2,1)S(1)}, u32[]{:S(2)}, u32[]{:S(2)}) collective-permute-start(bf16[8,16,1024]{2,1,0:T(8,128)(2,1)} %get-tuple-element.10), channel_id=1, source_target_pairs={{0,16},{499,387},{4,20},{503,391},{8,24},{507,395},{12,28},{511,39... | collective-permute-start | bytes 786440 | tf_op jit(solution)/shard_map/ppermute | solution.py:246
  58.1 21.1 %collective-permute-start.8 = (bf16[8,16,1024]{2,1,0:T(8,128)(2,1)}, bf16[8,16,1024]{2,1,0:T(8,128)(2,1)S(1)}, u32[]{:S(2)}, u32[]{:S(2)}) collective-permute-start(bf16[8,16,1024]{2,1,0:T(8,128)(2,1)} %get-tuple-element.11), channel_id=1, source_target_pairs={{0,144},{499,2},{4,148},{503,6},{8,152},{507,10},{12,156},{511,14}... | collective-permute-start | bytes 786440 | tf_op jit(solution)/shard_map/ppermute | solution.py:246
  64.7 14.4 %collective-permute-start.5 = (bf16[128,1024]{1,0:T(8,128)(2,1)S(1)}, bf16[128,1024]{1,0:T(8,128)(2,1)S(1)}, u32[]{:S(2)}, u32[]{:S(2)}) collective-permute-start(bf16[128,1024]{1,0:T(8,128)(2,1)S(1)} %shard_map.55), channel_id=1, source_target_pairs={{0,16},{499,387},{4,20},{503,391},{8,24},{507,395},{12,28},{511,39... | collective-permute-start | bytes 786440 | tf_op jit(solution)/shard_map/ppermute | solution.py:246
  68.1 11.0 %collective-permute-start.3 = (bf16[128,1024]{1,0:T(8,128)(2,1)S(1)}, bf16[128,1024]{1,0:T(8,128)(2,1)S(1)}, u32[]{:S(2)}, u32[]{:S(2)}) collective-permute-start(bf16[128,1024]{1,0:T(8,128)(2,1)S(1)} %shard_map.54), channel_id=1, source_target_pairs={{0,128},{499,114},{4,132},{503,118},{8,136},{507,122},{12,140},{51... | collective-permute-start | bytes 786440 | tf_op jit(solution)/shard_map/ppermute | solution.py:246
  72.3 10.6 %copy-start.2 = (bf16[8,16,1024]{2,1,0:T(8,128)(2,1)S(1)}, bf16[8,16,1024]{2,1,0:T(8,128)(2,1)}, u32[]{:S(2)}) copy-start(bf16[8,16,1024]{2,1,0:T(8,128)(2,1)} %get-tuple-element.8.refs_4_) | copy-start | bytes 786436
  72.3 10.6 %collective-permute-start.1 = (bf16[128,1024]{1,0:T(8,128)(2,1)S(1)}, bf16[128,1024]{1,0:T(8,128)(2,1)S(1)}, u32[]{:S(2)}, u32[]{:S(2)}) collective-permute-start(bf16[128,1024]{1,0:T(8,128)(2,1)S(1)} %shard_map.53), channel_id=1, source_target_pairs={{0,144},{499,2},{4,148},{503,6},{8,152},{507,10},{12,156},{511,14}... | collective-permute-start | bytes 786440 | tf_op jit(solution)/shard_map/ppermute | solution.py:246
  79.1 23.8 %copy-start.3 = (f32[1024,16]{0,1:T(8,128)S(1)}, f32[1024,16]{0,1:T(8,128)}, u32[]{:S(2)}) copy-start(f32[1024,16]{0,1:T(8,128)} %param.5) | copy-start | bytes 196612
